TPU v7x, 128 devices: a whole 4x4x4 slice. The times are simulated.
128 devices in a mesh: board: 8 (over z, x_hi), cent: 16 (over y, x_lo, core).
Axes of the slice: x: 4 (x_hi: 2, x_lo: 2; x = x_hi * 2 + x_lo), y: 4, z: 4, core: 2. Of those that a mesh axis runs over, the one named last changes fastest.
Arguments:
- turn_hist: bfloat16 [50, 3080192], P(None, ('board', 'cent')), may hold values from 0.0009994507 to 1
- turn_assign: int32 [3080192], P(('board', 'cent')), may hold values from 0 to 199
- child_rows: int32 [47, 65536], P(None, ('board', 'cent')), may hold values from 0 to 187, as said below
- turn_centers: float32 [50, 200], replicated, may hold values from 0.001 to 1
- flop_centers: float32 [200, 2000], P(None, 'cent'), may hold values from 0.01 to 1
- flop_assign: int32 [65536], P(('board', 'cent')), may hold values from 0 to 1999
Outputs:
- nearest: float32 [65536], P(('board', 'cent'))
- turn_sums: float32 [50, 200], replicated
- flop_sums: float32 [2000, 200], P('cent')
Inputs may be any that keep to these rules, and one draw needn't show every extreme that they name: `child_rows`: on each device's 512 flop hands, the entries whose n = i * 512 + g share one value of n // 188 form a permutation of 0 to 187.
All inputs are finite; a program needn't handle non-finite values.
Results may differ from a plain program's by a relative error of at most 0.0003.
Values may be sent and summed in bfloat16 or wider, within the bound.
No kernel may reach another device: no remote copies, remote signals or barrier semaphores. Data moves between devices by JAX's collectives and lax.ppermute only.
A program may use at most 128 MiB of HBM per device.

v0:
```python
import functools

import jax
import jax.numpy as jnp
from jax import lax
from jax.experimental import pallas as pl
from jax.experimental.pallas import tpu as pltpu
from jax.sharding import PartitionSpec as P

sharpness = 4.0
highest = lax.Precision.HIGHEST
f32, bf16, i32 = jnp.float32, jnp.bfloat16, jnp.int32
LANES = 128
BLOCK = 188
BINS = 50
KIDS = 47
TURN_CENT = 200
HANDS = 512
PANEL = 125
DEVICES = 128
SOURCES_PER_STEP = 32
PACK_ROWS = 80


def fold_table(bins):
    upper = lax.iota(i32, bins)[:, None]
    lower = lax.iota(i32, bins)[None, :]
    table = 0.5 * (lower <= upper).astype(f32)
    table = table + 0.25 * (lower <= upper - 1).astype(f32)
    table = table + 0.25 * ((lower <= upper + 1) & (lower >= 1)).astype(f32)
    return table


def pack_kernel(hist_ref, out_ref):
    lane = lax.broadcasted_iota(i32, (16, LANES), 1)
    for d in range(SOURCES_PER_STEP):
        t0, o = divmod(BLOCK * d, LANES)
        three = o + BLOCK > 2 * LANES

        def parts(lo, hi):
            tiles = [hist_ref[lo:hi, (t0 + t) * LANES:(t0 + t + 1) * LANES].astype(f32)
                     for t in range(3 if three else 2)]
            upper = lane[:hi - lo] >= o
            a = jnp.where(upper, tiles[0], tiles[1]) if o else tiles[0]
            b = jnp.where(upper, tiles[1], tiles[2]) if three else tiles[1]
            return a, b

        a0, b0 = parts(0, 16)
        a1, b1 = parts(16, 32)
        a2, b2 = parts(32, 48)
        a3, b3 = parts(48, 50)
        first = ((lane - o) & 127) < 64
        out_ref[d, 0:16, :] = a0.astype(bf16)
        out_ref[d, 16:32, :] = a1.astype(bf16)
        out_ref[d, 32:48, :] = a2.astype(bf16)
        out_ref[d, 48:64, :] = jnp.where(first, b0, pltpu.roll(b1, 64, 1)).astype(bf16)
        tail = jnp.concatenate(
            [pltpu.roll(b3, 64, 1), a3, pltpu.roll(a3, 64, 1), jnp.zeros((10, LANES), f32)], axis=0)
        out_ref[d, 64:80, :] = jnp.where(first, b2, tail).astype(bf16)


def pack(turn_hist):
    width = SOURCES_PER_STEP * BLOCK
    return pl.pallas_call(
        pack_kernel,
        grid=(DEVICES // SOURCES_PER_STEP,),
        in_specs=[pl.BlockSpec((BINS, width), lambda i: (0, i))],
        out_specs=pl.BlockSpec((SOURCES_PER_STEP, PACK_ROWS, LANES), lambda i: (i, 0, 0)),
        out_shape=jax.ShapeDtypeStruct((DEVICES, PACK_ROWS, LANES), bf16),
        name="pack",
    )(turn_hist)


def turn_kernel(hist_ref, label_ref, out_ref):
    @pl.when(pl.program_id(0) == 0)
    def _():
        out_ref[...] = jnp.zeros_like(out_ref)

    values = hist_ref[...].astype(f32)
    normal = values / jnp.sum(values, axis=0, keepdims=True)
    hi = normal.astype(bf16)
    rest = normal - hi.astype(f32)
    mid = rest.astype(bf16)
    low = (rest - mid.astype(f32)).astype(bf16)
    ids = lax.broadcasted_iota(i32, (TURN_CENT, values.shape[1]), 0)
    onehot = (label_ref[...] == ids).astype(f32).astype(bf16)
    total = out_ref[...]
    for part in (hi, mid, low):
        total = total + lax.dot_general(part, onehot, (((1,), (1,)), ((), ())), preferred_element_type=f32)
    out_ref[...] = total


def turn_partial(turn_hist, labels):
    width = SOURCES_PER_STEP * BLOCK // 2 if (SOURCES_PER_STEP * BLOCK // 2) % LANES == 0 else SOURCES_PER_STEP * BLOCK
    steps = turn_hist.shape[1] // width
    return pl.pallas_call(
        turn_kernel,
        grid=(steps,),
        in_specs=[pl.BlockSpec((BINS, width), lambda i: (0, i)), pl.BlockSpec((1, width), lambda i: (0, i))],
        out_specs=pl.BlockSpec((BINS, TURN_CENT), lambda i: (0, 0)),
        out_shape=jax.ShapeDtypeStruct((BINS, TURN_CENT), f32),
        name="turn_sums",
    )(turn_hist, labels)


TILE = 256
TILES = KIDS * HANDS // TILE


def split3(x):
    hi = x.astype(bf16)
    rest = x - hi.astype(f32)
    mid = rest.astype(bf16)
    low = (rest - mid.astype(f32)).astype(bf16)
    return hi, mid, low


def member_kernel(scalar_ref, recv_ref, place_ref, table_ref, assign_ref, hist_ref, keep_ref, send_ref, cols_ref):
    o = scalar_ref[0]
    core = scalar_ref[1]
    lane = lax.broadcasted_iota(i32, (16, LANES), 1)
    row = lax.broadcasted_iota(i32, (16, LANES), 0)
    first = ((lane - o) & 127) < 64
    from_c1 = (~first) & (row >= 2) & (row < 4)
    from_r1 = first & (row >= 4) & (row < 6)
    b3_rows = row < 2
    wide_lane = lax.broadcasted_iota(i32, (64, TILE), 1)
    one_lane = lax.broadcasted_iota(i32, (1, TILE), 1)
    sub = lax.broadcasted_iota(i32, (TILE, TILE), 0)

    def place(s, carry):
        start = s * BLOCK
        t0 = start // TILE
        a = start - t0 * TILE
        c0 = recv_ref[s, 48:64, :].astype(f32)
        c1 = recv_ref[s, 64:80, :].astype(f32)
        r0 = pltpu.roll(c0, 64, 1)
        r1 = pltpu.roll(c1, 64, 1)
        a3 = jnp.where(from_c1, c1, jnp.where(from_r1, r1, 0.0))
        b3 = jnp.where(b3_rows, r1, 0.0)
        left = jnp.concatenate([recv_ref[s, 0:48, :], a3.astype(bf16)], axis=0)
        right = jnp.concatenate(
            [recv_ref[s, 48:64, :], r0.astype(bf16), recv_ref[s, 64:80, :], b3.astype(bf16)], axis=0)
        payload = jnp.concatenate([left, right], axis=1)
        q = jnp.where(one_lane >= a, place_ref[pl.ds(t0, 1), :], place_ref[pl.ds(t0 + 1, 1), :])
        onehot = (sub == q).astype(f32).astype(bf16)
        cols = jnp.dot(payload, onehot, preferred_element_type=f32)
        cols_ref[t0] = jnp.where(wide_lane >= a, cols, cols_ref[t0])
        cols_ref[t0 + 1] = cols
        return carry

    cols_ref[0] = jnp.zeros((64, TILE), f32)
    lax.fori_loop(0, DEVICES, place, 0, unroll=2)

    hist_ref[...] = jnp.zeros_like(hist_ref)

    def kid(i, carry):
        h = jnp.concatenate([cols_ref[2 * i].astype(bf16), cols_ref[2 * i + 1].astype(bf16)], axis=1)
        z = jnp.dot(table_ref[...], jnp.concatenate([h, h, h], axis=0), preferred_element_type=f32)
        cdf = z[200:256]
        total = z[256:264]
        sq = jnp.sum(cdf * cdf, axis=0, keepdims=True)
        extra = total[0:1] + sharpness * sq / total[0:1]
        y = z[0:200] + extra
        w = 1.0 / (y * y)
        hist_ref[...] += w * (1.0 / jnp.sum(w, axis=0, keepdims=True))
        return carry

    lax.fori_loop(0, KIDS, kid, 0)

    hi, mid, low = split3(hist_ref[...])
    stack = jnp.concatenate([hi, mid, low], axis=0)
    ids = lax.broadcasted_iota(i32, (LANES, HANDS), 0)
    valid = ids < PANEL
    for i in range(8):
        halves = []
        for side in (core, 1 - core):
            base = PANEL * (2 * i + side)
            halves.append((valid & (assign_ref[...] - base == ids)).astype(f32).astype(bf16))
        onehot = jnp.concatenate(halves, axis=0)
        sums = lax.dot_general(stack, onehot, (((1,), (1,)), ((), ())), preferred_element_type=f32)
        both = sums[0:200] + sums[200:400] + sums[400:600]
        keep_ref[i] = both[:, :LANES]
        send_ref[i] = both[:, LANES:]


def member(scalars, recv, place, table, assign):
    vmem = pl.BlockSpec(memory_space=pltpu.VMEM)
    return pl.pallas_call(
        member_kernel,
        in_specs=[pl.BlockSpec(memory_space=pltpu.SMEM), vmem, vmem, vmem, vmem],
        out_specs=[vmem, vmem, vmem],
        out_shape=[
            jax.ShapeDtypeStruct((TURN_CENT, HANDS), f32),
            jax.ShapeDtypeStruct((8, TURN_CENT, LANES), f32),
            jax.ShapeDtypeStruct((8, TURN_CENT, LANES), f32),
        ],
        scratch_shapes=[pltpu.VMEM((TILES + 1, 64, TILE), f32)],
        compiler_params=pltpu.CompilerParams(vmem_limit_bytes=48 * 1024 * 1024),
        name="member",
    )(scalars, recv, place, table, assign)


def center_table(turn_centers):
    table = fold_table(BINS)
    values = turn_centers.astype(f32)
    normal = values / jnp.sum(values, axis=0, keepdims=True)
    center_cdf = jnp.dot(table, normal, precision=highest, preferred_element_type=f32)
    center_sq = jnp.sum(center_cdf * center_cdf, axis=0)
    folded = lax.dot_general(
        center_cdf, table, (((0,), (0,)), ((), ())), precision=highest, preferred_element_type=f32)
    folded = sharpness * center_sq[:, None] - 2.0 * sharpness * folded

    def spread(x):
        return jnp.concatenate(
            [x[:, :48], x[:, 48:], x[:, 48:], x[:, 48:], jnp.zeros((x.shape[0], 10), f32)], axis=1)

    hi = lax.reduce_precision(folded, 8, 7)
    mid = lax.reduce_precision(folded - hi, 8, 7)
    low = lax.reduce_precision(folded - hi - mid, 8, 7)
    top = jnp.concatenate([spread(hi), spread(mid), spread(low)], axis=1)
    rows = jnp.concatenate([table, jnp.zeros((6, BINS), f32), jnp.ones((8, BINS), f32)], axis=0)
    bottom = jnp.concatenate([spread(rows), jnp.zeros((64, 128), f32)], axis=1)
    return jnp.concatenate([top, bottom], axis=0).astype(bf16)


CHIPS = [[2 * i + c for i in range(8)] for c in range(2)]


def swap(x, axis, mask):
    size = 8 if axis == "board" else 16
    return lax.ppermute(x, axis, [(i, i ^ mask) for i in range(size)])


def add_over_board(x):
    for mask in (1, 2, 6):
        x = x + swap(x, "board", mask)
    return x


def add_over_all(x):
    for mask in (1, 2, 4, 12):
        x = x + swap(x, "cent", mask)
    return add_over_board(x)


def nearest_of(pieces, flop_hist):
    best = None
    for piece in pieces:
        cross = lax.dot_general(
            piece, flop_hist, (((1,), (0,)), ((), ())), precision=highest, preferred_element_type=f32)
        part = jnp.min(jnp.sum(jnp.square(piece), axis=1)[:, :, None] - 2.0 * cross, axis=(0, 1))
        best = part if best is None else jnp.minimum(best, part)
    return best + jnp.sum(jnp.square(flop_hist), axis=0)


def body(turn_hist, turn_assign, child_rows, turn_centers, flop_centers, flop_assign):
    sent = pack(turn_hist)
    arrived = lax.all_to_all(sent, ("board", "cent"), split_axis=0, concat_axis=0, tiled=True)

    device = lax.axis_index("board") * 16 + lax.axis_index("cent")
    offset = (device * BLOCK) % LANES
    scalars = jnp.stack([offset, lax.axis_index("cent") % 2]).astype(i32)

    turn_part = turn_partial(turn_hist, turn_assign[None, :])
    turn_sums = add_over_all(turn_part) * (BINS * TURN_CENT / (turn_hist.shape[1] * DEVICES))

    copies = jnp.broadcast_to(flop_centers[None], (8,) + flop_centers.shape)
    mine = lax.all_to_all(copies, "cent", split_axis=0, concat_axis=0, tiled=True, axis_index_groups=CHIPS)
    other = swap(mine, "cent", 1)

    place = (child_rows & 128) + ((child_rows + offset) & 127)
    place = jnp.concatenate([place.reshape(TILES, TILE), jnp.full((2, TILE), -1, i32)], axis=0)
    table = center_table(turn_centers)

    flop_hist, keep, send = member(scalars, arrived, place, table, flop_assign[None, :])

    half = keep + swap(send, "cent", 1)
    parts = lax.all_to_all(half, "cent", split_axis=0, concat_axis=0, tiled=True, axis_index_groups=CHIPS)
    flop_part = add_over_board(jnp.sum(parts, axis=0))
    flop_sums = flop_part[:, :PANEL].T * (PANEL * 16 / (HANDS * DEVICES))

    nearest = nearest_of((mine, other), flop_hist)
    return nearest, turn_sums, flop_sums


def solution(mesh):
    in_specs = (
        P(None, ("board", "cent")),
        P(("board", "cent")),
        P(None, ("board", "cent")),
        P(),
        P(None, "cent"),
        P(("board", "cent")),
    )
    out_specs = (P(("board", "cent")), P(), P("cent", None))
    return jax.shard_map(body, mesh=mesh, in_specs=in_specs, out_specs=out_specs, check_vma=False)
```

profile of v0, /device:TPU:0, one launch (start us, length us, event | category | flops | bytes accessed | tf_op | source)
XLA Modules:
  0.0 170.0 jit_solution(9414152115381592740)
XLA Ops:
  0.6 4.4 %pack.1 = bf16[128,80,128]{2,1,0:T(8,128)(2,1)} custom-call(bf16[50,24064]{1,0:T(8,128)(2,1)} %hist_ref.3), custom_call_target="tpu_custom_call" | custom-call | tf_op jit(solution)/shard_map/pack/pallas_call | solution.py:64
  5.0 11.2 %all-to-all-start.1 = ((bf16[128,80,128]{2,1,0:T(8,128)(2,1)}), bf16[128,80,128]{2,1,0:T(8,128)(2,1)S(1)}, u32[]{:S(2)}, u32[]{:S(2)}) async-start(bf16[128,80,128]{2,1,0:T(8,128)(2,1)} %pack.1), calls=%async_computation.1 | async-start | bytes 5242880 | tf_op jit(solution)/shard_map/all_to_all | solution.py:259
  17.3 34.9 %all-to-all-done.1.recv_ref = bf16[128,80,128]{2,1,0:T(8,128)(2,1)S(1)} async-done(((bf16[128,80,128]{2,1,0:T(8,128)(2,1)}), bf16[128,80,128]{2,1,0:T(8,128)(2,1)S(1)}, u32[]{:S(2)}, u32[]{:S(2)}) %all-to-all-start.1) | async-done | bytes 2621472 | tf_op jit(solution)/shard_map/all_to_all | solution.py:259
  53.1 4.2 %all-to-all-start = ((f32[8,200,125]{2,1,0:T(8,128)}), f32[8,200,125]{2,1,0:T(8,128)}, u32[]{:S(2)}, u32[]{:S(2)}) async-start(f32[8,200,125]{2,1,0:T(8,128)} %broadcast_in_dim.14), calls=%async_computation | async-start | bytes 1638400 | tf_op jit(solution)/shard_map/all_to_all | solution.py:269
  58.3 34.0 %member.1 = (f32[200,512]{1,0:T(8,128)S(1)}, f32[8,200,128]{2,1,0:T(8,128)S(1)}, f32[8,200,128]{2,1,0:T(8,128)}) custom-call(s32[2]{0:T(128)S(1)} %pad_add_fusion.scalar_ref, bf16[128,80,128]{2,1,0:T(8,128)(2,1)S(1)} %all-to-all-done.1.recv_ref, s32[96,256]{1,0:T(8,128)S(1)} %concatenate.20.place_ref, bf16[264,192]{1,0:T(8,128)(2,1)S(1)} %pad_maximum_fusion.table_ref, ...), custom_call_target="tpu_custom_call" | custom-call | tf_op jit(solution)/shard_map/member/pallas_call | solution.py:189
  93.6 1.6 broadcast_in_dim.37.label_ref
  95.2 12.2 %turn_sums.1 = f32[50,200]{1,0:T(8,128)} custom-call(bf16[50,24064]{1,0:T(8,128)(2,1)} %hist_ref.3, s32[1,24064]{1,0:T(1,128)} %broadcast_in_dim.37.label_ref), custom_call_target="tpu_custom_call" | custom-call | tf_op jit(solution)/shard_map/turn_sums/pallas_call | solution.py:96
  109.6 1.9 %collective-permute-start.2 = (f32[50,200]{1,0:T(8,128)S(1)}, f32[50,200]{1,0:T(8,128)S(1)}, u32[]{:S(2)}, u32[]{:S(2)}) collective-permute-start(f32[50,200]{1,0:T(8,128)S(1)} %add.99), channel_id=1, source_target_pairs={{0,2},{1,3},{2,0},{3,1},{4,6},{5,7},{6,4},{7,5},{8,10},{9,11},{10,... | collective-permute-start | bytes 120008 | tf_op jit(solution)/shard_map/ppermute | solution.py:232
  111.5 2.3 %collective-permute-done.2 = f32[50,200]{1,0:T(8,128)S(1)} collective-permute-done((f32[50,200]{1,0:T(8,128)S(1)}, f32[50,200]{1,0:T(8,128)S(1)}, u32[]{:S(2)}, u32[]{:S(2)}) %collective-permute-start.2) | collective-permute-done | bytes 40032 | tf_op jit(solution)/shard_map/ppermute | solution.py:232
  113.8 2.0 %collective-permute-start.3 = (f32[50,200]{1,0:T(8,128)S(1)}, f32[50,200]{1,0:T(8,128)S(1)}, u32[]{:S(2)}, u32[]{:S(2)}) collective-permute-start(f32[50,200]{1,0:T(8,128)S(1)} %add.100), channel_id=1, source_target_pairs={{0,4},{1,5},{2,6},{3,7},{4,0},{5,1},{6,2},{7,3},{8,12},{9,13},{10,... | collective-permute-start | bytes 120008 | tf_op jit(solution)/shard_map/ppermute | solution.py:232
  115.8 2.3 %collective-permute-done.3 = f32[50,200]{1,0:T(8,128)S(1)} collective-permute-done((f32[50,200]{1,0:T(8,128)S(1)}, f32[50,200]{1,0:T(8,128)S(1)}, u32[]{:S(2)}, u32[]{:S(2)}) %collective-permute-start.3) | collective-permute-done | bytes 40032 | tf_op jit(solution)/shard_map/ppermute | solution.py:232
  118.1 3.2 %collective-permute-start.4 = (f32[50,200]{1,0:T(8,128)S(1)}, f32[50,200]{1,0:T(8,128)S(1)}, u32[]{:S(2)}, u32[]{:S(2)}) collective-permute-start(f32[50,200]{1,0:T(8,128)S(1)} %add.101), channel_id=1, source_target_pairs={{0,12},{1,13},{2,14},{3,15},{4,8},{5,9},{6,10},{7,11},{8,4},{9,5},... | collective-permute-start | bytes 120008 | tf_op jit(solution)/shard_map/ppermute | solution.py:232
  121.3 2.3 %collective-permute-done.4 = f32[50,200]{1,0:T(8,128)S(1)} collective-permute-done((f32[50,200]{1,0:T(8,128)S(1)}, f32[50,200]{1,0:T(8,128)S(1)}, u32[]{:S(2)}, u32[]{:S(2)}) %collective-permute-start.4) | collective-permute-done | bytes 40032 | tf_op jit(solution)/shard_map/ppermute | solution.py:232
  124.2 5.1 %collective-permute-done.5 = f32[50,200]{1,0:T(8,128)S(1)} collective-permute-done((f32[50,200]{1,0:T(8,128)S(1)}, f32[50,200]{1,0:T(8,128)S(1)}, u32[]{:S(2)}, u32[]{:S(2)}) %collective-permute-start.5) | collective-permute-done | bytes 40032 | tf_op jit(solution)/shard_map/ppermute | solution.py:232
  129.4 4.2 %collective-permute-done.6 = f32[50,200]{1,0:T(8,128)S(1)} collective-permute-done((f32[50,200]{1,0:T(8,128)S(1)}, f32[50,200]{1,0:T(8,128)S(1)}, u32[]{:S(2)}, u32[]{:S(2)}) %collective-permute-start.6) | collective-permute-done | bytes 40032 | tf_op jit(solution)/shard_map/ppermute | solution.py:232
  135.3 5.5 %all-to-all-start.2 = ((f32[8,200,128]{2,1,0:T(8,128)}), f32[8,200,128]{2,1,0:T(8,128)S(1)}, u32[]{:S(2)}, u32[]{:S(2)}) async-start(f32[8,200,128]{2,1,0:T(8,128)} %add.106), calls=%async_computation.2 | async-start | bytes 1638400 | tf_op jit(solution)/shard_map/all_to_all | solution.py:279
  142.7 3.2 %subtract_reduce_fusion.1 = f32[512]{0:T(512)S(1)} fusion(f32[8,200,125]{2,1,0:T(8,128)} %all-to-all-done, f32[8,125]{1,0:T(8,128)S(1)} %multiply_reduce_fusion.1, f32[200,512]{1,0:T(8,128)S(1)} %copy-done.1), kind=kOutput, calls=%fused_computation.1 | convolution fusion | flops 1230335488 | bytes 1215648 | tf_op jit(solution)/shard_map/dot_general | solution.py:250
  146.0 6.1 %all-to-all-done.2 = f32[8,200,128]{2,1,0:T(8,128)S(1)} async-done(((f32[8,200,128]{2,1,0:T(8,128)}), f32[8,200,128]{2,1,0:T(8,128)S(1)}, u32[]{:S(2)}, u32[]{:S(2)}) %all-to-all-start.2) | async-done | bytes 819232 | tf_op jit(solution)/shard_map/all_to_all | solution.py:279
  152.2 1.5 collective-permute-start.9
  153.6 2.1 %subtract_reduce_fusion = f32[512]{0:T(512)S(1)} fusion(f32[8,125]{1,0:T(8,128)S(1)} %multiply_reduce_fusion, f32[8,200,125]{2,1,0:T(8,128)S(1)} %collective-permute-done, f32[200,512]{1,0:T(8,128)S(1)} %copy-done.1), kind=kOutput, calls=%fused_computation | convolution fusion | flops 1230335488 | bytes 1215648 | tf_op jit(solution)/shard_map/dot_general | solution.py:250
  155.7 2.9 %collective-permute-done.9 = f32[200,128]{1,0:T(8,128)S(1)} collective-permute-done((f32[200,128]{1,0:T(8,128)S(1)}, f32[200,128]{1,0:T(8,128)S(1)}, u32[]{:S(2)}, u32[]{:S(2)}) %collective-permute-start.9) | collective-permute-done | bytes 102432 | tf_op jit(solution)/shard_map/ppermute | solution.py:232
  158.7 4.6 %collective-permute-done.10 = f32[200,128]{1,0:T(8,128)S(1)} collective-permute-done((f32[200,128]{1,0:T(8,128)S(1)}, f32[200,128]{1,0:T(8,128)S(1)}, u32[]{:S(2)}, u32[]{:S(2)}) %collective-permute-start.10) | collective-permute-done | bytes 102432 | tf_op jit(solution)/shard_map/ppermute | solution.py:232
  163.3 2.8 %collective-permute-start.11 = (f32[200,128]{1,0:T(8,128)S(1)}, f32[200,128]{1,0:T(8,128)S(1)}, u32[]{:S(2)}, u32[]{:S(2)}) collective-permute-start(f32[200,128]{1,0:T(8,128)S(1)} %add.108), channel_id=1, source_target_pairs={{0,96},{16,112},{32,64},{48,80},{64,32},{80,48},{96,0},{112,16},{1... | collective-permute-start | bytes 307208 | tf_op jit(solution)/shard_map/ppermute | solution.py:232
  166.7 2.6 %collective-permute-done.11 = f32[200,128]{1,0:T(8,128)S(1)} collective-permute-done((f32[200,128]{1,0:T(8,128)S(1)}, f32[200,128]{1,0:T(8,128)S(1)}, u32[]{:S(2)}, u32[]{:S(2)}) %collective-permute-start.11) | collective-permute-done | bytes 102432 | tf_op jit(solution)/shard_map/ppermute | solution.py:232
  (68 shorter events, 12.3 us)
Async XLA Ops:
  5.0 11.4 %copy-start.5 = (f32[50,200]{1,0:T(8,128)S(1)}, f32[50,200]{1,0:T(8,128)}, u32[]{:S(2)}) copy-start(f32[50,200]{1,0:T(8,128)} %param.9) | copy-start | bytes 120004
  5.0 11.8 %copy-start.4 = (s32[47,512]{1,0:T(8,128)S(1)}, s32[47,512]{1,0:T(8,128)}, u32[]{:S(2)}) copy-start(s32[47,512]{1,0:T(8,128)} %param.8) | copy-start | bytes 288772
  5.0 47.2 %copy-start.3 = (f32[200,125]{1,0:T(8,128)S(1)}, f32[200,125]{1,0:T(8,128)}, u32[]{:S(2)}) copy-start(f32[200,125]{1,0:T(8,128)} %param.10) | copy-start | bytes 300004
  5.0 47.2 %all-to-all-start.1 = ((bf16[128,80,128]{2,1,0:T(8,128)(2,1)}), bf16[128,80,128]{2,1,0:T(8,128)(2,1)S(1)}, u32[]{:S(2)}, u32[]{:S(2)}) async-start(bf16[128,80,128]{2,1,0:T(8,128)(2,1)} %pack.1), calls=%async_computation.1 | async-start | bytes 5242880 | tf_op jit(solution)/shard_map/all_to_all | solution.py:259
  17.3 41.1 %copy-start.2 = (s32[512]{0:T(512)S(1)}, s32[512]{0:T(512)}, u32[]{:S(2)}) copy-start(s32[512]{0:T(512)} %param.11) | copy-start | bytes 6148
  53.1 39.9 %all-to-all-start = ((f32[8,200,125]{2,1,0:T(8,128)}), f32[8,200,125]{2,1,0:T(8,128)}, u32[]{:S(2)}, u32[]{:S(2)}) async-start(f32[8,200,125]{2,1,0:T(8,128)} %broadcast_in_dim.14), calls=%async_computation | async-start | bytes 1638400 | tf_op jit(solution)/shard_map/all_to_all | solution.py:269
  92.3 0.7 copy-start
  93.1 41.2 %collective-permute-start.8 = (f32[8,200,128]{2,1,0:T(8,128)}, f32[8,200,128]{2,1,0:T(8,128)S(1)}, u32[]{:S(2)}, u32[]{:S(2)}) collective-permute-start(f32[8,200,128]{2,1,0:T(8,128)} %get-tuple-element.8), channel_id=1, source_target_pairs={{0,1},{1,0},{2,3},{3,2},{4,5},{5,4},{6,7},{7,6},{8,9},{9,8},{10,11... | collective-permute-start | bytes 2457608 | tf_op jit(solution)/shard_map/ppermute | solution.py:232
  93.1 49.5 %collective-permute-start = (f32[8,200,125]{2,1,0:T(8,128)}, f32[8,200,125]{2,1,0:T(8,128)S(1)}, u32[]{:S(2)}, u32[]{:S(2)}) collective-permute-start(f32[8,200,125]{2,1,0:T(8,128)} %all-to-all-done), channel_id=1, source_target_pairs={{0,1},{1,0},{2,3},{3,2},{4,5},{5,4},{6,7},{7,6},{8,9},{9,8},{10,11... | collective-permute-start | bytes 2400008 | tf_op jit(solution)/shard_map/ppermute | solution.py:232
  107.3 1.5 collective-permute-start.1
  109.6 4.2 %collective-permute-start.2 = (f32[50,200]{1,0:T(8,128)S(1)}, f32[50,200]{1,0:T(8,128)S(1)}, u32[]{:S(2)}, u32[]{:S(2)}) collective-permute-start(f32[50,200]{1,0:T(8,128)S(1)} %add.99), channel_id=1, source_target_pairs={{0,2},{1,3},{2,0},{3,1},{4,6},{5,7},{6,4},{7,5},{8,10},{9,11},{10,... | collective-permute-start | bytes 120008 | tf_op jit(solution)/shard_map/ppermute | solution.py:232
  113.8 4.3 %collective-permute-start.3 = (f32[50,200]{1,0:T(8,128)S(1)}, f32[50,200]{1,0:T(8,128)S(1)}, u32[]{:S(2)}, u32[]{:S(2)}) collective-permute-start(f32[50,200]{1,0:T(8,128)S(1)} %add.100), channel_id=1, source_target_pairs={{0,4},{1,5},{2,6},{3,7},{4,0},{5,1},{6,2},{7,3},{8,12},{9,13},{10,... | collective-permute-start | bytes 120008 | tf_op jit(solution)/shard_map/ppermute | solution.py:232
  118.1 5.5 %collective-permute-start.4 = (f32[50,200]{1,0:T(8,128)S(1)}, f32[50,200]{1,0:T(8,128)S(1)}, u32[]{:S(2)}, u32[]{:S(2)}) collective-permute-start(f32[50,200]{1,0:T(8,128)S(1)} %add.101), channel_id=1, source_target_pairs={{0,12},{1,13},{2,14},{3,15},{4,8},{5,9},{6,10},{7,11},{8,4},{9,5},... | collective-permute-start | bytes 120008 | tf_op jit(solution)/shard_map/ppermute | solution.py:232
  123.6 5.8 %collective-permute-start.5 = (f32[50,200]{1,0:T(8,128)S(1)}, f32[50,200]{1,0:T(8,128)S(1)}, u32[]{:S(2)}, u32[]{:S(2)}) collective-permute-start(f32[50,200]{1,0:T(8,128)S(1)} %add.102), channel_id=1, source_target_pairs={{0,16},{16,0},{32,48},{48,32},{64,80},{80,64},{96,112},{112,96},{1... | collective-permute-start | bytes 120008 | tf_op jit(solution)/shard_map/ppermute | solution.py:232
  129.3 4.3 %collective-permute-start.6 = (f32[50,200]{1,0:T(8,128)S(1)}, f32[50,200]{1,0:T(8,128)S(1)}, u32[]{:S(2)}, u32[]{:S(2)}) collective-permute-start(f32[50,200]{1,0:T(8,128)S(1)} %add.103), channel_id=1, source_target_pairs={{0,32},{16,48},{32,0},{48,16},{64,96},{80,112},{96,64},{112,80},{1... | collective-permute-start | bytes 120008 | tf_op jit(solution)/shard_map/ppermute | solution.py:232
  133.6 7.1 %collective-permute-start.7 = (f32[50,200]{1,0:T(8,128)S(1)}, f32[50,200]{1,0:T(8,128)S(1)}, u32[]{:S(2)}, u32[]{:S(2)}) collective-permute-start(f32[50,200]{1,0:T(8,128)S(1)} %add.104), channel_id=1, source_target_pairs={{0,96},{16,112},{32,64},{48,80},{64,32},{80,48},{96,0},{112,16},{1... | collective-permute-start | bytes 120008 | tf_op jit(solution)/shard_map/ppermute | solution.py:232
  135.3 7.5 %copy-start.1 = (f32[200,512]{1,0:T(8,128)S(1)}, f32[200,512]{1,0:T(8,128)}, u32[]{:S(2)}) copy-start(f32[200,512]{1,0:T(8,128)} %copy-done) | copy-start | bytes 1228804
  135.3 16.8 %all-to-all-start.2 = ((f32[8,200,128]{2,1,0:T(8,128)}), f32[8,200,128]{2,1,0:T(8,128)S(1)}, u32[]{:S(2)}, u32[]{:S(2)}) async-start(f32[8,200,128]{2,1,0:T(8,128)} %add.106), calls=%async_computation.2 | async-start | bytes 1638400 | tf_op jit(solution)/shard_map/all_to_all | solution.py:279
  152.2 6.4 %collective-permute-start.9 = (f32[200,128]{1,0:T(8,128)S(1)}, f32[200,128]{1,0:T(8,128)S(1)}, u32[]{:S(2)}, u32[]{:S(2)}) collective-permute-start(f32[200,128]{1,0:T(8,128)S(1)} %reduce_sum.59), channel_id=1, source_target_pairs={{0,16},{16,0},{32,48},{48,32},{64,80},{80,64},{96,112},{112,96},{1... | collective-permute-start | bytes 307208 | tf_op jit(solution)/shard_map/ppermute | solution.py:232
  158.6 4.7 %collective-permute-start.10 = (f32[200,128]{1,0:T(8,128)S(1)}, f32[200,128]{1,0:T(8,128)S(1)}, u32[]{:S(2)}, u32[]{:S(2)}) collective-permute-start(f32[200,128]{1,0:T(8,128)S(1)} %add.107), channel_id=1, source_target_pairs={{0,32},{16,48},{32,0},{48,16},{64,96},{80,112},{96,64},{112,80},{1... | collective-permute-start | bytes 307208 | tf_op jit(solution)/shard_map/ppermute | solution.py:232
  163.3 6.0 %collective-permute-start.11 = (f32[200,128]{1,0:T(8,128)S(1)}, f32[200,128]{1,0:T(8,128)S(1)}, u32[]{:S(2)}, u32[]{:S(2)}) collective-permute-start(f32[200,128]{1,0:T(8,128)S(1)} %add.108), channel_id=1, source_target_pairs={{0,96},{16,112},{32,64},{48,80},{64,32},{80,48},{96,0},{112,16},{1... | collective-permute-start | bytes 307208 | tf_op jit(solution)/shard_map/ppermute | solution.py:232
where the time goes:
time: 171 us; the launch traced here: 170 us
  waiting for transfers between devices  68.6 us (40%)
  Pallas kernels  50.5 us (30%)
  starting transfers between devices  34.1 us (20%)
  matrix products  6.04 us (4%)
  other arithmetic  5.56 us (3%)
  local copies, waits for them, and re-layouts  4.21 us (2%)
    all_to_all x1, waiting for transfers between devices, body(): lax.all_to_all(sent, ('board', 'cent'), split_axis=0, concat_axis=0, tile...  34.9 us
    pallas_call x1, Pallas kernels, member(): pl.pallas_call(member_kernel, in_specs=[pl.BlockSpec(memory_space=pltpu.S...  34 us
    ppermute x12, waiting for transfers between devices, swap(): return lax.ppermute(x, axis, [(i, i ^ mask) for i in range(size)])  27.6 us
    ppermute x12, starting transfers between devices, swap(): return lax.ppermute(x, axis, [(i, i ^ mask) for i in range(size)])  13.3 us
    pallas_call x1, Pallas kernels, turn_partial(): pl.pallas_call(turn_kernel, grid=(steps,), in_specs=[pl.BlockSpec((BINS,...  12.2 us
    all_to_all x1, starting transfers between devices, body(): lax.all_to_all(sent, ('board', 'cent'), split_axis=0, concat_axis=0, tile...  11.2 us
    all_to_all x1, waiting for transfers between devices, body(): lax.all_to_all(half, 'cent', split_axis=0, concat_axis=0, tiled=True, axi...  6.12 us
    all_to_all x1, starting transfers between devices, body(): lax.all_to_all(half, 'cent', split_axis=0, concat_axis=0, tiled=True, axi...  5.47 us
  transfers between devices with their start and end apart: 15, of which 11 were waited for; matrix products, arithmetic and copies ran while one was open for 8% of the time, Pallas kernels for 27%

commit v1 on v0

--- a/solution.py
+++ b/solution.py
@@ -1,11 +1,10 @@
-import functools
-
 import jax
 import jax.numpy as jnp
 from jax import lax
 from jax.experimental import pallas as pl
 from jax.experimental.pallas import tpu as pltpu
 from jax.sharding import PartitionSpec as P
+
 
 sharpness = 4.0
 highest = lax.Precision.HIGHEST
@@ -256,23 +255,26 @@
 
 def body(turn_hist, turn_assign, child_rows, turn_centers, flop_centers, flop_assign):
     sent = pack(turn_hist)
-    arrived = lax.all_to_all(sent, ("board", "cent"), split_axis=0, concat_axis=0, tiled=True)
-
     device = lax.axis_index("board") * 16 + lax.axis_index("cent")
     offset = (device * BLOCK) % LANES
     scalars = jnp.stack([offset, lax.axis_index("cent") % 2]).astype(i32)
 
-    turn_part = turn_partial(turn_hist, turn_assign[None, :])
+    labels, sent = lax.optimization_barrier((turn_assign[None, :], sent))
+    arrived = lax.all_to_all(sent, ("board", "cent"), split_axis=0, concat_axis=0, tiled=True)
+    turn_part = turn_partial(turn_hist, labels)
+    flop_centers, turn_part = lax.optimization_barrier((flop_centers, turn_part))
+    group = flop_centers[None]
+    for mask in (2, 4, 12):
+        group = jnp.concatenate([group, swap(group, "cent", mask)], axis=0)
+    mine, other = group, swap(group, "cent", 1)
     turn_sums = add_over_all(turn_part) * (BINS * TURN_CENT / (turn_hist.shape[1] * DEVICES))
-
-    copies = jnp.broadcast_to(flop_centers[None], (8,) + flop_centers.shape)
-    mine = lax.all_to_all(copies, "cent", split_axis=0, concat_axis=0, tiled=True, axis_index_groups=CHIPS)
-    other = swap(mine, "cent", 1)
 
     place = (child_rows & 128) + ((child_rows + offset) & 127)
     place = jnp.concatenate([place.reshape(TILES, TILE), jnp.full((2, TILE), -1, i32)], axis=0)
     table = center_table(turn_centers)
 
+    scalars, turn_sums, mine, other, place, table = lax.optimization_barrier(
+        (scalars, turn_sums, mine, other, place, table))
     flop_hist, keep, send = member(scalars, arrived, place, table, flop_assign[None, :])
 
     half = keep + swap(send, "cent", 1)

time: 171 us -> 159 us (0.930)
  waiting for transfers between devices: 68.6 us -> 49.8 us
  other arithmetic: 5.56 us -> 10.8 us
  starting transfers between devices: 34.1 us -> 36.3 us
  matrix products: 6.04 us -> 7.85 us
    all_to_all x1, waiting for transfers between devices: 34.9 us -> 0.01 us  [body(): lax.all_to_all(sent, ('board', 'cent'), split_axis=0, concat_axis=0, tile...]
    ppermute x12 -> x15, waiting for transfers between devices: 27.6 us -> 41.9 us  [swap(): return lax.ppermute(x, axis, [(i, i ^ mask) for i in range(size)])]
    ppermute x12 -> x15, starting transfers between devices: 13.3 us -> 21.4 us  [swap(): return lax.ppermute(x, axis, [(i, i ^ mask) for i in range(size)])]
    all_to_all x1 -> x0, starting transfers between devices: 4.21 us -> none  [body(): lax.all_to_all(copies, 'cent', split_axis=0, concat_axis=0, tiled=True, a...]
    concatenate x0 -> x3, other arithmetic: none -> 1.81 us  [body(): group = jnp.concatenate([group, swap(group, 'cent', mask)], axis=0)]
    all_to_all x1, waiting for transfers between devices: 6.12 us -> 7.89 us  [body(): lax.all_to_all(half, 'cent', split_axis=0, concat_axis=0, tiled=True, axi...]
    all_to_all x1, starting transfers between devices: 5.47 us -> 3.73 us  [body(): lax.all_to_all(half, 'cent', split_axis=0, concat_axis=0, tiled=True, axi...]
  transfers between devices with their start and end apart: 15 -> 17, of which waited for: 11 -> 13; matrix products, arithmetic and copies ran while one was open for 8% -> 12% of each run, Pallas kernels for 27% -> 8%
where the time goes in v1:
time: 159 us; the launch traced here: 158 us
  waiting for transfers between devices  49.8 us (31%)
  Pallas kernels  49.5 us (31%)
  starting transfers between devices  36.3 us (23%)
  other arithmetic  10.8 us (7%)
  matrix products  7.85 us (5%)
  local copies, waits for them, and re-layouts  3.36 us (2%)
    ppermute x15, waiting for transfers between devices, swap(): return lax.ppermute(x, axis, [(i, i ^ mask) for i in range(size)])  41.9 us
    pallas_call x1, Pallas kernels, member(): pl.pallas_call(member_kernel, in_specs=[pl.BlockSpec(memory_space=pltpu.S...  32.9 us
    ppermute x15, starting transfers between devices, swap(): return lax.ppermute(x, axis, [(i, i ^ mask) for i in range(size)])  21.4 us
    pallas_call x1, Pallas kernels, turn_partial(): pl.pallas_call(turn_kernel, grid=(steps,), in_specs=[pl.BlockSpec((BINS,...  12.2 us
    all_to_all x1, starting transfers between devices, body(): lax.all_to_all(sent, ('board', 'cent'), split_axis=0, concat_axis=0, tile...  11.2 us
    all_to_all x1, waiting for transfers between devices, body(): lax.all_to_all(half, 'cent', split_axis=0, concat_axis=0, tiled=True, axi...  7.89 us
    dot_general x2, matrix products, nearest_of(): lax.dot_general(piece, flop_hist, (((1,), (0,)), ((), ())), precision=hig...  6.51 us
    pallas_call x1, Pallas kernels, pack(): pl.pallas_call(pack_kernel, grid=(DEVICES // SOURCES_PER_STEP,), in_specs...  4.35 us
  transfers between devices with their start and end apart: 17, of which 13 were waited for; matrix products, arithmetic and copies ran while one was open for 12% of the time, Pallas kernels for 8%

profile of v1, /device:TPU:0, one launch (start us, length us, event | category | flops | bytes accessed | tf_op | source)
XLA Modules:
  0.0 158.4 jit_solution(907081823630370715)
XLA Ops:
  0.6 1.6 %broadcast_in_dim.28.label_ref = s32[1,24064]{1,0:T(1,128)} reshape(s32[24064]{0:T(1024)} %param.7) | data formatting | bytes 192512 | tf_op jit(solution)/shard_map/broadcast_in_dim | solution.py:262
  2.2 4.4 %pack.1 = bf16[128,80,128]{2,1,0:T(8,128)(2,1)} custom-call(bf16[50,24064]{1,0:T(8,128)(2,1)} %hist_ref.3), custom_call_target="tpu_custom_call" | custom-call | tf_op jit(solution)/shard_map/pack/pallas_call | solution.py:63
  6.6 11.2 %all-to-all-start = ((bf16[128,80,128]{2,1,0:T(8,128)(2,1)}), bf16[128,80,128]{2,1,0:T(8,128)(2,1)S(1)}, u32[]{:S(2)}, u32[]{:S(2)}) async-start(bf16[128,80,128]{2,1,0:T(8,128)(2,1)} %pack.1), calls=%async_computation | async-start | bytes 5242880 | tf_op jit(solution)/shard_map/all_to_all | solution.py:263
  17.8 12.2 %turn_sums.1 = f32[50,200]{1,0:T(8,128)} custom-call(bf16[50,24064]{1,0:T(8,128)(2,1)} %hist_ref.3, s32[1,24064]{1,0:T(1,128)} %broadcast_in_dim.28.label_ref), custom_call_target="tpu_custom_call" | custom-call | tf_op jit(solution)/shard_map/turn_sums/pallas_call | solution.py:95
  31.4 17.9 %collective-permute-done.7 = f32[1,200,125]{2,1,0:T(8,128)S(1)} collective-permute-done((f32[1,200,125]{2,1,0:T(8,128)S(1)}, f32[1,200,125]{2,1,0:T(8,128)S(1)}, u32[]{:S(2)}, u32[]{:S(2)}) %collective-permute-start.7) | collective-permute-done | bytes 100032 | tf_op jit(solution)/shard_map/ppermute | solution.py:231
  53.3 2.6 %collective-permute-done.8 = f32[2,200,125]{2,1,0:T(8,128)S(1)} collective-permute-done((f32[2,200,125]{2,1,0:T(8,128)S(1)}, f32[2,200,125]{2,1,0:T(8,128)S(1)}, u32[]{:S(2)}, u32[]{:S(2)}) %collective-permute-start.8) | collective-permute-done | bytes 200032 | tf_op jit(solution)/shard_map/ppermute | solution.py:231
  56.7 2.8 %collective-permute-start.9 = (f32[4,200,125]{2,1,0:T(8,128)}, f32[4,200,125]{2,1,0:T(8,128)S(1)}, u32[]{:S(2)}, u32[]{:S(2)}) collective-permute-start(f32[4,200,125]{2,1,0:T(8,128)} %pad_maximum_fusion.1), channel_id=1, source_target_pairs={{0,12},{1,13},{2,14},{3,15},{4,8},{5,9},{6,10},{7,11},{8,4},{9,5},... | collective-permute-start | bytes 1200008 | tf_op jit(solution)/shard_map/ppermute | solution.py:231
  62.1 3.1 %collective-permute-done.2 = f32[50,200]{1,0:T(8,128)S(1)} collective-permute-done((f32[50,200]{1,0:T(8,128)S(1)}, f32[50,200]{1,0:T(8,128)S(1)}, u32[]{:S(2)}, u32[]{:S(2)}) %collective-permute-start.2) | collective-permute-done | bytes 40032 | tf_op jit(solution)/shard_map/ppermute | solution.py:231
  65.8 3.0 %collective-permute-done.9 = f32[4,200,125]{2,1,0:T(8,128)S(1)} collective-permute-done((f32[4,200,125]{2,1,0:T(8,128)}, f32[4,200,125]{2,1,0:T(8,128)S(1)}, u32[]{:S(2)}, u32[]{:S(2)}) %collective-permute-start.9) | collective-permute-done | bytes 400032 | tf_op jit(solution)/shard_map/ppermute | solution.py:231
  70.7 2.8 %collective-permute-start.4 = (f32[50,200]{1,0:T(8,128)S(1)}, f32[50,200]{1,0:T(8,128)S(1)}, u32[]{:S(2)}, u32[]{:S(2)}) collective-permute-start(f32[50,200]{1,0:T(8,128)S(1)} %add.95), channel_id=1, source_target_pairs={{0,16},{16,0},{32,48},{48,32},{64,80},{80,64},{96,112},{112,96},{1... | collective-permute-start | bytes 120008 | tf_op jit(solution)/shard_map/ppermute | solution.py:231
  76.5 1.8 %collective-permute-start.5 = (f32[50,200]{1,0:T(8,128)S(1)}, f32[50,200]{1,0:T(8,128)S(1)}, u32[]{:S(2)}, u32[]{:S(2)}) collective-permute-start(f32[50,200]{1,0:T(8,128)S(1)} %add.96), channel_id=1, source_target_pairs={{0,32},{16,48},{32,0},{48,16},{64,96},{80,112},{96,64},{112,80},{1... | collective-permute-start | bytes 120008 | tf_op jit(solution)/shard_map/ppermute | solution.py:231
  78.3 2.4 %collective-permute-done.5 = f32[50,200]{1,0:T(8,128)S(1)} collective-permute-done((f32[50,200]{1,0:T(8,128)S(1)}, f32[50,200]{1,0:T(8,128)S(1)}, u32[]{:S(2)}, u32[]{:S(2)}) %collective-permute-start.5) | collective-permute-done | bytes 40032 | tf_op jit(solution)/shard_map/ppermute | solution.py:231
  80.7 3.6 %collective-permute-start.6 = (f32[50,200]{1,0:T(8,128)S(1)}, f32[50,200]{1,0:T(8,128)S(1)}, u32[]{:S(2)}, u32[]{:S(2)}) collective-permute-start(f32[50,200]{1,0:T(8,128)S(1)} %add.97), channel_id=1, source_target_pairs={{0,96},{16,112},{32,64},{48,80},{64,32},{80,48},{96,0},{112,16},{1... | collective-permute-start | bytes 120008 | tf_op jit(solution)/shard_map/ppermute | solution.py:231
  84.4 2.0 %collective-permute-done.6 = f32[50,200]{1,0:T(8,128)S(1)} collective-permute-done((f32[50,200]{1,0:T(8,128)S(1)}, f32[50,200]{1,0:T(8,128)S(1)}, u32[]{:S(2)}, u32[]{:S(2)}) %collective-permute-start.6) | collective-permute-done | bytes 40032 | tf_op jit(solution)/shard_map/ppermute | solution.py:231
  87.1 32.9 %member.1 = (f32[200,512]{1,0:T(8,128)S(1)}, f32[8,200,128]{2,1,0:T(8,128)S(1)}, f32[8,200,128]{2,1,0:T(8,128)S(1)}) custom-call(s32[2]{0:T(128)S(1)} %pad_add_fusion.scalar_ref, bf16[128,80,128]{2,1,0:T(8,128)(2,1)S(1)} %all-to-all-done.recv_ref, s32[96,256]{1,0:T(8,128)S(1)} %concatenate.34.place_ref, bf16[264,192]{1,0:T(8,128)(2,1)S(1)} %pad_maximum_fusion.3.table_ref, ...), custom_call_target="tpu_custom_call" | custom-call | tf_op jit(solution)/shard_map/member/pallas_call | solution.py:188
  120.1 2.3 %collective-permute-done.11 = f32[8,200,128]{2,1,0:T(8,128)S(1)} collective-permute-done((f32[8,200,128]{2,1,0:T(8,128)S(1)}, f32[8,200,128]{2,1,0:T(8,128)S(1)}, u32[]{:S(2)}, u32[]{:S(2)}) %collective-permute-start.11) | collective-permute-done | bytes 819232 | tf_op jit(solution)/shard_map/ppermute | solution.py:231
  123.4 3.7 %all-to-all-start.1 = ((f32[8,200,128]{2,1,0:T(8,128)}), f32[8,200,128]{2,1,0:T(8,128)S(1)}, u32[]{:S(2)}, u32[]{:S(2)}) async-start(f32[8,200,128]{2,1,0:T(8,128)} %add.106), calls=%async_computation.1 | async-start | bytes 1638400 | tf_op jit(solution)/shard_map/all_to_all | solution.py:281
  129.6 3.3 %subtract_reduce_fusion.1 = f32[512]{0:T(512)S(1)} fusion(f32[8,200,125]{2,1,0:T(8,128)} %pad_maximum_fusion, f32[8,125]{1,0:T(8,128)S(1)} %multiply_reduce_fusion.1, f32[200,512]{1,0:T(8,128)S(1)} %get-tuple-element.24), kind=kOutput, calls=%fused_computation.1 | convolution fusion | flops 1230335488 | bytes 1215648 | tf_op jit(solution)/shard_map/dot_general | solution.py:249
  132.9 7.9 %all-to-all-done.1 = f32[8,200,128]{2,1,0:T(8,128)S(1)} async-done(((f32[8,200,128]{2,1,0:T(8,128)}), f32[8,200,128]{2,1,0:T(8,128)S(1)}, u32[]{:S(2)}, u32[]{:S(2)}) %all-to-all-start.1) | async-done | bytes 819232 | tf_op jit(solution)/shard_map/all_to_all | solution.py:281
  140.8 2.8 %collective-permute-start.12 = (f32[200,128]{1,0:T(8,128)S(1)}, f32[200,128]{1,0:T(8,128)S(1)}, u32[]{:S(2)}, u32[]{:S(2)}) collective-permute-start(f32[200,128]{1,0:T(8,128)S(1)} %reduce_sum.59), channel_id=1, source_target_pairs={{0,16},{16,0},{32,48},{48,32},{64,80},{80,64},{96,112},{112,96},{1... | collective-permute-start | bytes 307208 | tf_op jit(solution)/shard_map/ppermute | solution.py:231
  143.6 3.3 %subtract_reduce_fusion = f32[512]{0:T(512)S(1)} fusion(f32[8,200,125]{2,1,0:T(8,128)} %collective-permute-done.10, f32[8,125]{1,0:T(8,128)S(1)} %multiply_reduce_fusion, f32[200,512]{1,0:T(8,128)S(1)} %get-tuple-element.24), kind=kOutput, calls=%fused_computation | convolution fusion | flops 1230335488 | bytes 1215648 | tf_op jit(solution)/shard_map/dot_general | solution.py:249
  147.5 4.3 %collective-permute-done.13 = f32[200,128]{1,0:T(8,128)S(1)} collective-permute-done((f32[200,128]{1,0:T(8,128)S(1)}, f32[200,128]{1,0:T(8,128)S(1)}, u32[]{:S(2)}, u32[]{:S(2)}) %collective-permute-start.13) | collective-permute-done | bytes 102432 | tf_op jit(solution)/shard_map/ppermute | solution.py:231
  151.8 3.3 %collective-permute-start.14 = (f32[200,128]{1,0:T(8,128)S(1)}, f32[200,128]{1,0:T(8,128)S(1)}, u32[]{:S(2)}, u32[]{:S(2)}) collective-permute-start(f32[200,128]{1,0:T(8,128)S(1)} %add.108), channel_id=1, source_target_pairs={{0,96},{16,112},{32,64},{48,80},{64,32},{80,48},{96,0},{112,16},{1... | collective-permute-start | bytes 307208 | tf_op jit(solution)/shard_map/ppermute | solution.py:231
  155.7 2.1 %collective-permute-done.14 = f32[200,128]{1,0:T(8,128)S(1)} collective-permute-done((f32[200,128]{1,0:T(8,128)S(1)}, f32[200,128]{1,0:T(8,128)S(1)}, u32[]{:S(2)}, u32[]{:S(2)}) %collective-permute-start.14) | collective-permute-done | bytes 102432 | tf_op jit(solution)/shard_map/ppermute | solution.py:231
  (74 shorter events, 20.4 us)
Async XLA Ops:
  6.6 80.5 %all-to-all-start = ((bf16[128,80,128]{2,1,0:T(8,128)(2,1)}), bf16[128,80,128]{2,1,0:T(8,128)(2,1)S(1)}, u32[]{:S(2)}, u32[]{:S(2)}) async-start(bf16[128,80,128]{2,1,0:T(8,128)(2,1)} %pack.1), calls=%async_computation | async-start | bytes 5242880 | tf_op jit(solution)/shard_map/all_to_all | solution.py:263
  17.8 12.2 %copy-start.1 = (f32[200,125]{1,0:T(8,128)S(1)}, f32[200,125]{1,0:T(8,128)}, u32[]{:S(2)}) copy-start(f32[200,125]{1,0:T(8,128)} %param.10) | copy-start | bytes 300004
  17.8 13.3 %copy-start.5 = (f32[50,200]{1,0:T(8,128)S(1)}, f32[50,200]{1,0:T(8,128)}, u32[]{:S(2)}) copy-start(f32[50,200]{1,0:T(8,128)} %param.9) | copy-start | bytes 120004
  30.0 21.9 %collective-permute-start = (f32[50,200]{1,0:T(8,128)}, f32[50,200]{1,0:T(8,128)S(1)}, u32[]{:S(2)}, u32[]{:S(2)}) collective-permute-start(f32[50,200]{1,0:T(8,128)} %turn_sums.1), channel_id=1, source_target_pairs={{0,1},{1,0},{2,3},{3,2},{4,5},{5,4},{6,7},{7,6},{8,9},{9,8},{10,11... | collective-permute-start | bytes 120008 | tf_op jit(solution)/shard_map/ppermute | solution.py:231
  30.0 19.3 %collective-permute-start.7 = (f32[1,200,125]{2,1,0:T(8,128)S(1)}, f32[1,200,125]{2,1,0:T(8,128)S(1)}, u32[]{:S(2)}, u32[]{:S(2)}) collective-permute-start(f32[1,200,125]{2,1,0:T(8,128)S(1)} %bitcast.15), channel_id=1, source_target_pairs={{0,2},{1,3},{2,0},{3,1},{4,6},{5,7},{6,4},{7,5},{8,10},{9,11},{10,... | collective-permute-start | bytes 300008 | tf_op jit(solution)/shard_map/ppermute | solution.py:231
  49.3 6.6 %collective-permute-start.8 = (f32[2,200,125]{2,1,0:T(8,128)S(1)}, f32[2,200,125]{2,1,0:T(8,128)S(1)}, u32[]{:S(2)}, u32[]{:S(2)}) collective-permute-start(f32[2,200,125]{2,1,0:T(8,128)S(1)} %pad_maximum_fusion.2), channel_id=1, source_target_pairs={{0,4},{1,5},{2,6},{3,7},{4,0},{5,1},{6,2},{7,3},{8,12},{9,13},{10,... | collective-permute-start | bytes 600008 | tf_op jit(solution)/shard_map/ppermute | solution.py:231
  52.8 7.4 %collective-permute-start.1 = (f32[50,200]{1,0:T(8,128)S(1)}, f32[50,200]{1,0:T(8,128)}, u32[]{:S(2)}, u32[]{:S(2)}) collective-permute-start(f32[50,200]{1,0:T(8,128)S(1)} %add.92), channel_id=1, source_target_pairs={{0,2},{1,3},{2,0},{3,1},{4,6},{5,7},{6,4},{7,5},{8,10},{9,11},{10,... | collective-permute-start | bytes 120008 | tf_op jit(solution)/shard_map/ppermute | solution.py:231
  56.7 12.1 %collective-permute-start.9 = (f32[4,200,125]{2,1,0:T(8,128)}, f32[4,200,125]{2,1,0:T(8,128)S(1)}, u32[]{:S(2)}, u32[]{:S(2)}) collective-permute-start(f32[4,200,125]{2,1,0:T(8,128)} %pad_maximum_fusion.1), channel_id=1, source_target_pairs={{0,12},{1,13},{2,14},{3,15},{4,8},{5,9},{6,10},{7,11},{8,4},{9,5},... | collective-permute-start | bytes 1200008 | tf_op jit(solution)/shard_map/ppermute | solution.py:231
  60.2 13.5 %copy-start.4 = (bf16[200,50]{1,0:T(8,128)(2,1)S(1)}, bf16[200,50]{1,0:T(8,128)(2,1)}, u32[]{:S(2)}) copy-start(bf16[200,50]{1,0:T(8,128)(2,1)} %get-tuple-element.29) | copy-start | bytes 60004
  60.2 13.6 %copy-start.3 = (bf16[200,50]{1,0:T(8,128)(2,1)S(1)}, bf16[200,50]{1,0:T(8,128)(2,1)}, u32[]{:S(2)}) copy-start(bf16[200,50]{1,0:T(8,128)(2,1)} %get-tuple-element.30) | copy-start | bytes 60004
  60.2 13.7 %copy-start.2 = (bf16[200,50]{1,0:T(8,128)(2,1)S(1)}, bf16[200,50]{1,0:T(8,128)(2,1)}, u32[]{:S(2)}) copy-start(bf16[200,50]{1,0:T(8,128)(2,1)} %get-tuple-element.31) | copy-start | bytes 60004
  61.0 4.2 %collective-permute-start.2 = (f32[50,200]{1,0:T(8,128)S(1)}, f32[50,200]{1,0:T(8,128)S(1)}, u32[]{:S(2)}, u32[]{:S(2)}) collective-permute-start(f32[50,200]{1,0:T(8,128)S(1)} %add.93), channel_id=1, source_target_pairs={{0,4},{1,5},{2,6},{3,7},{4,0},{5,1},{6,2},{7,3},{8,12},{9,13},{10,... | collective-permute-start | bytes 120008 | tf_op jit(solution)/shard_map/ppermute | solution.py:231
  65.2 21.9 %copy-start = (s32[512]{0:T(512)S(1)}, s32[512]{0:T(512)}, u32[]{:S(2)}) copy-start(s32[512]{0:T(512)} %param.11) | copy-start | bytes 6148
  65.2 5.5 %collective-permute-start.3 = (f32[50,200]{1,0:T(8,128)S(1)}, f32[50,200]{1,0:T(8,128)S(1)}, u32[]{:S(2)}, u32[]{:S(2)}) collective-permute-start(f32[50,200]{1,0:T(8,128)S(1)} %add.94), channel_id=1, source_target_pairs={{0,12},{1,13},{2,14},{3,15},{4,8},{5,9},{6,10},{7,11},{8,4},{9,5},... | collective-permute-start | bytes 120008 | tf_op jit(solution)/shard_map/ppermute | solution.py:231
  69.8 17.3 %collective-permute-start.10 = (f32[8,200,125]{2,1,0:T(8,128)}, f32[8,200,125]{2,1,0:T(8,128)}, u32[]{:S(2)}, u32[]{:S(2)}) collective-permute-start(f32[8,200,125]{2,1,0:T(8,128)} %pad_maximum_fusion), channel_id=1, source_target_pairs={{0,1},{1,0},{2,3},{3,2},{4,5},{5,4},{6,7},{7,6},{8,9},{9,8},{10,11... | collective-permute-start | bytes 2400008 | tf_op jit(solution)/shard_map/ppermute | solution.py:231
  70.7 5.8 %collective-permute-start.4 = (f32[50,200]{1,0:T(8,128)S(1)}, f32[50,200]{1,0:T(8,128)S(1)}, u32[]{:S(2)}, u32[]{:S(2)}) collective-permute-start(f32[50,200]{1,0:T(8,128)S(1)} %add.95), channel_id=1, source_target_pairs={{0,16},{16,0},{32,48},{48,32},{64,80},{80,64},{96,112},{112,96},{1... | collective-permute-start | bytes 120008 | tf_op jit(solution)/shard_map/ppermute | solution.py:231
  76.5 4.3 %collective-permute-start.5 = (f32[50,200]{1,0:T(8,128)S(1)}, f32[50,200]{1,0:T(8,128)S(1)}, u32[]{:S(2)}, u32[]{:S(2)}) collective-permute-start(f32[50,200]{1,0:T(8,128)S(1)} %add.96), channel_id=1, source_target_pairs={{0,32},{16,48},{32,0},{48,16},{64,96},{80,112},{96,64},{112,80},{1... | collective-permute-start | bytes 120008 | tf_op jit(solution)/shard_map/ppermute | solution.py:231
  80.7 5.7 %collective-permute-start.6 = (f32[50,200]{1,0:T(8,128)S(1)}, f32[50,200]{1,0:T(8,128)S(1)}, u32[]{:S(2)}, u32[]{:S(2)}) collective-permute-start(f32[50,200]{1,0:T(8,128)S(1)} %add.97), channel_id=1, source_target_pairs={{0,96},{16,112},{32,64},{48,80},{64,32},{80,48},{96,0},{112,16},{1... | collective-permute-start | bytes 120008 | tf_op jit(solution)/shard_map/ppermute | solution.py:231
  120.0 2.4 %collective-permute-start.11 = (f32[8,200,128]{2,1,0:T(8,128)S(1)}, f32[8,200,128]{2,1,0:T(8,128)S(1)}, u32[]{:S(2)}, u32[]{:S(2)}) collective-permute-start(f32[8,200,128]{2,1,0:T(8,128)S(1)} %get-tuple-element.28), channel_id=1, source_target_pairs={{0,1},{1,0},{2,3},{3,2},{4,5},{5,4},{6,7},{7,6},{8,9},{9,8},{10,11... | collective-permute-start | bytes 2457608 | tf_op jit(solution)/shard_map/ppermute | solution.py:231
  123.4 17.4 %all-to-all-start.1 = ((f32[8,200,128]{2,1,0:T(8,128)}), f32[8,200,128]{2,1,0:T(8,128)S(1)}, u32[]{:S(2)}, u32[]{:S(2)}) async-start(f32[8,200,128]{2,1,0:T(8,128)} %add.106), calls=%async_computation.1 | async-start | bytes 1638400 | tf_op jit(solution)/shard_map/all_to_all | solution.py:281
  140.8 6.2 %collective-permute-start.12 = (f32[200,128]{1,0:T(8,128)S(1)}, f32[200,128]{1,0:T(8,128)S(1)}, u32[]{:S(2)}, u32[]{:S(2)}) collective-permute-start(f32[200,128]{1,0:T(8,128)S(1)} %reduce_sum.59), channel_id=1, source_target_pairs={{0,16},{16,0},{32,48},{48,32},{64,80},{80,64},{96,112},{112,96},{1... | collective-permute-start | bytes 307208 | tf_op jit(solution)/shard_map/ppermute | solution.py:231
  147.1 4.7 %collective-permute-start.13 = (f32[200,128]{1,0:T(8,128)S(1)}, f32[200,128]{1,0:T(8,128)S(1)}, u32[]{:S(2)}, u32[]{:S(2)}) collective-permute-start(f32[200,128]{1,0:T(8,128)S(1)} %add.107), channel_id=1, source_target_pairs={{0,32},{16,48},{32,0},{48,16},{64,96},{80,112},{96,64},{112,80},{1... | collective-permute-start | bytes 307208 | tf_op jit(solution)/shard_map/ppermute | solution.py:231
  151.8 6.0 %collective-permute-start.14 = (f32[200,128]{1,0:T(8,128)S(1)}, f32[200,128]{1,0:T(8,128)S(1)}, u32[]{:S(2)}, u32[]{:S(2)}) collective-permute-start(f32[200,128]{1,0:T(8,128)S(1)} %add.108), channel_id=1, source_target_pairs={{0,96},{16,112},{32,64},{48,80},{64,32},{80,48},{96,0},{112,16},{1... | collective-permute-start | bytes 307208 | tf_op jit(solution)/shard_map/ppermute | solution.py:231

commit v2 on v0

--- a/solution.py
+++ b/solution.py
@@ -1,11 +1,10 @@
-import functools
-
 import jax
 import jax.numpy as jnp
 from jax import lax
 from jax.experimental import pallas as pl
 from jax.experimental.pallas import tpu as pltpu
 from jax.sharding import PartitionSpec as P
+
 
 sharpness = 4.0
 highest = lax.Precision.HIGHEST
@@ -20,6 +19,8 @@
 DEVICES = 128
 SOURCES_PER_STEP = 32
 PACK_ROWS = 80
+TURN_SPLIT = 56
+TURN_ROWS = 112
 
 
 def fold_table(bins):
@@ -84,10 +85,12 @@
     low = (rest - mid.astype(f32)).astype(bf16)
     ids = lax.broadcasted_iota(i32, (TURN_CENT, values.shape[1]), 0)
     onehot = (label_ref[...] == ids).astype(f32).astype(bf16)
-    total = out_ref[...]
+    total = None
     for part in (hi, mid, low):
-        total = total + lax.dot_general(part, onehot, (((1,), (1,)), ((), ())), preferred_element_type=f32)
-    out_ref[...] = total
+        more = lax.dot_general(part, onehot, (((1,), (1,)), ((), ())), preferred_element_type=f32)
+        total = more if total is None else total + more
+    out_ref[0:BINS, :] += total[:, :LANES]
+    out_ref[TURN_SPLIT:TURN_SPLIT + BINS, 0:TURN_CENT - LANES] += total[:, LANES:]
 
 
 def turn_partial(turn_hist, labels):
@@ -97,8 +100,8 @@
         turn_kernel,
         grid=(steps,),
         in_specs=[pl.BlockSpec((BINS, width), lambda i: (0, i)), pl.BlockSpec((1, width), lambda i: (0, i))],
-        out_specs=pl.BlockSpec((BINS, TURN_CENT), lambda i: (0, 0)),
-        out_shape=jax.ShapeDtypeStruct((BINS, TURN_CENT), f32),
+        out_specs=pl.BlockSpec((TURN_ROWS, LANES), lambda i: (0, 0)),
+        out_shape=jax.ShapeDtypeStruct((TURN_ROWS, LANES), f32),
         name="turn_sums",
     )(turn_hist, labels)
 
@@ -115,9 +118,8 @@
     return hi, mid, low
 
 
-def member_kernel(scalar_ref, recv_ref, place_ref, table_ref, assign_ref, hist_ref, keep_ref, send_ref, cols_ref):
+def place_kernel(scalar_ref, recv_ref, place_ref, cols_ref):
     o = scalar_ref[0]
-    core = scalar_ref[1]
     lane = lax.broadcasted_iota(i32, (16, LANES), 1)
     row = lax.broadcasted_iota(i32, (16, LANES), 0)
     first = ((lane - o) & 127) < 64
@@ -152,6 +154,9 @@
     cols_ref[0] = jnp.zeros((64, TILE), f32)
     lax.fori_loop(0, DEVICES, place, 0, unroll=2)
 
+
+def member_kernel(scalar_ref, cols_ref, table_ref, assign_ref, hist_ref, keep_ref, send_ref):
+    core = scalar_ref[1]
     hist_ref[...] = jnp.zeros_like(hist_ref)
 
     def kid(i, carry):
@@ -184,21 +189,32 @@
         send_ref[i] = both[:, LANES:]
 
 
-def member(scalars, recv, place, table, assign):
-    vmem = pl.BlockSpec(memory_space=pltpu.VMEM)
+VMEM = pl.BlockSpec(memory_space=pltpu.VMEM)
+SMEM = pl.BlockSpec(memory_space=pltpu.SMEM)
+
+
+def place_columns(scalars, recv, place):
+    return pl.pallas_call(
+        place_kernel,
+        in_specs=[SMEM, VMEM, VMEM],
+        out_specs=VMEM,
+        out_shape=jax.ShapeDtypeStruct((TILES + 1, 64, TILE), f32),
+        name="place",
+    )(scalars, recv, place)
+
+
+def member(scalars, cols, table, assign):
     return pl.pallas_call(
         member_kernel,
-        in_specs=[pl.BlockSpec(memory_space=pltpu.SMEM), vmem, vmem, vmem, vmem],
-        out_specs=[vmem, vmem, vmem],
+        in_specs=[SMEM, VMEM, VMEM, VMEM],
+        out_specs=[VMEM, VMEM, VMEM],
         out_shape=[
             jax.ShapeDtypeStruct((TURN_CENT, HANDS), f32),
             jax.ShapeDtypeStruct((8, TURN_CENT, LANES), f32),
             jax.ShapeDtypeStruct((8, TURN_CENT, LANES), f32),
         ],
-        scratch_shapes=[pltpu.VMEM((TILES + 1, 64, TILE), f32)],
-        compiler_params=pltpu.CompilerParams(vmem_limit_bytes=48 * 1024 * 1024),
         name="member",
-    )(scalars, recv, place, table, assign)
+    )(scalars, cols, table, assign)
 
 
 def center_table(turn_centers):
@@ -232,18 +248,6 @@
     return lax.ppermute(x, axis, [(i, i ^ mask) for i in range(size)])
 
 
-def add_over_board(x):
-    for mask in (1, 2, 6):
-        x = x + swap(x, "board", mask)
-    return x
-
-
-def add_over_all(x):
-    for mask in (1, 2, 4, 12):
-        x = x + swap(x, "cent", mask)
-    return add_over_board(x)
-
-
 def nearest_of(pieces, flop_hist):
     best = None
     for piece in pieces:
@@ -256,6 +260,7 @@
 
 def body(turn_hist, turn_assign, child_rows, turn_centers, flop_centers, flop_assign):
     sent = pack(turn_hist)
+    turn_assign, sent = lax.optimization_barrier((turn_assign, sent))
     arrived = lax.all_to_all(sent, ("board", "cent"), split_axis=0, concat_axis=0, tiled=True)
 
     device = lax.axis_index("board") * 16 + lax.axis_index("cent")
@@ -263,24 +268,37 @@
     scalars = jnp.stack([offset, lax.axis_index("cent") % 2]).astype(i32)
 
     turn_part = turn_partial(turn_hist, turn_assign[None, :])
-    turn_sums = add_over_all(turn_part) * (BINS * TURN_CENT / (turn_hist.shape[1] * DEVICES))
-
-    copies = jnp.broadcast_to(flop_centers[None], (8,) + flop_centers.shape)
-    mine = lax.all_to_all(copies, "cent", split_axis=0, concat_axis=0, tiled=True, axis_index_groups=CHIPS)
-    other = swap(mine, "cent", 1)
+    own = jnp.concatenate([jnp.pad(flop_centers, ((0, 0), (0, LANES - PANEL))), turn_part], axis=0)
+    pieces = [own]
+    for mask in range(2, 16, 2):
+        pieces.append(swap(own, "cent", mask))
 
     place = (child_rows & 128) + ((child_rows + offset) & 127)
     place = jnp.concatenate([place.reshape(TILES, TILE), jnp.full((2, TILE), -1, i32)], axis=0)
     table = center_table(turn_centers)
-
-    flop_hist, keep, send = member(scalars, arrived, place, table, flop_assign[None, :])
+    place, table, scalars = lax.optimization_barrier((place, table, scalars))
+
+    cols = place_columns(scalars, arrived, place)
+
+    mine = jnp.stack([piece[:TURN_CENT] for piece in pieces])
+    turn_part = sum((piece[TURN_CENT:] for piece in pieces[1:]), turn_part)
+    other = swap(mine, "cent", 1)
+    turn_part = turn_part + swap(turn_part, "cent", 1)
+
+    flop_hist, keep, send = member(scalars, cols, table, flop_assign[None, :])
 
     half = keep + swap(send, "cent", 1)
     parts = lax.all_to_all(half, "cent", split_axis=0, concat_axis=0, tiled=True, axis_index_groups=CHIPS)
-    flop_part = add_over_board(jnp.sum(parts, axis=0))
-    flop_sums = flop_part[:, :PANEL].T * (PANEL * 16 / (HANDS * DEVICES))
-
-    nearest = nearest_of((mine, other), flop_hist)
+    total = jnp.concatenate([jnp.sum(parts, axis=0), turn_part], axis=0)
+    for mask in (1, 2, 6):
+        total = total + swap(total, "board", mask)
+    flop_sums = total[:TURN_CENT, :PANEL].T * (PANEL * 16 / (HANDS * DEVICES))
+    turn_low = total[TURN_CENT:TURN_CENT + BINS]
+    turn_high = total[TURN_CENT + TURN_SPLIT:TURN_CENT + TURN_SPLIT + BINS, :TURN_CENT - LANES]
+    turn_sums = jnp.concatenate([turn_low, turn_high], axis=1)
+    turn_sums = turn_sums * (BINS * TURN_CENT / (turn_hist.shape[1] * DEVICES))
+
+    nearest = nearest_of((mine[:, :, :PANEL], other[:, :, :PANEL]), flop_hist)
     return nearest, turn_sums, flop_sums
 
 

time: 171 us -> 162 us (0.947)
  waiting for transfers between devices: 68.6 us -> 50.1 us
  Pallas kernels: 50.5 us -> 57.5 us
  local copies, waits for them, and re-layouts: 4.21 us -> 10.2 us
  starting transfers between devices: 34.1 us -> 29.1 us
  other arithmetic: 5.56 us -> 8.47 us
    ppermute x12 -> x13, waiting for transfers between devices: 27.6 us -> 13 us  [swap(): return lax.ppermute(x, axis, [(i, i ^ mask) for i in range(size)])]
    all_to_all x1, waiting for transfers between devices: 34.9 us -> 25.9 us  [body(): lax.all_to_all(sent, ('board', 'cent'), split_axis=0, concat_axis=0, tile...]
    pallas_call x1 -> x2, Pallas kernels: 34 us -> 40.9 us  [the longest x1 23.2 us: member(): pl.pallas_call(member_kernel, in_specs=[SMEM, VMEM, VMEM, VMEM], out_spec...]
    unnamed x12 -> x21, local copies, waits for them, and re-layouts: 0.77 us -> 7.01 us
    all_to_all x1, waiting for transfers between devices: 6.12 us -> 11.2 us  [body(): lax.all_to_all(half, 'cent', split_axis=0, concat_axis=0, tiled=True, axi...]
    all_to_all x1 -> x0, starting transfers between devices: 4.21 us -> none  [body(): lax.all_to_all(copies, 'cent', split_axis=0, concat_axis=0, tiled=True, a...]
    all_to_all x1, starting transfers between devices: 5.47 us -> 3.55 us  [body(): lax.all_to_all(half, 'cent', split_axis=0, concat_axis=0, tiled=True, axi...]
    ppermute x12 -> x13, starting transfers between devices: 13.3 us -> 14.8 us  [swap(): return lax.ppermute(x, axis, [(i, i ^ mask) for i in range(size)])]
  transfers between devices with their start and end apart: 15 -> 15, of which waited for: 11 -> 6; matrix products, arithmetic and copies ran while one was open for 8% -> 11% of each run, Pallas kernels for 27% -> 25%
where the time goes in v2:
time: 162 us; the launch traced here: 161 us
  Pallas kernels  57.5 us (35%)
  waiting for transfers between devices  50.1 us (31%)
  starting transfers between devices  29.1 us (18%)
  local copies, waits for them, and re-layouts  10.2 us (6%)
  other arithmetic  8.47 us (5%)
  matrix products  4.96 us (3%)
    all_to_all x1, waiting for transfers between devices, body(): lax.all_to_all(sent, ('board', 'cent'), split_axis=0, concat_axis=0, tile...  25.9 us
    pallas_call x1, Pallas kernels, member(): pl.pallas_call(member_kernel, in_specs=[SMEM, VMEM, VMEM, VMEM], out_spec...  23.2 us
    pallas_call x1, Pallas kernels, place_columns(): pl.pallas_call(place_kernel, in_specs=[SMEM, VMEM, VMEM], out_specs=VMEM,...  17.6 us
    ppermute x13, starting transfers between devices, swap(): return lax.ppermute(x, axis, [(i, i ^ mask) for i in range(size)])  14.8 us
    ppermute x13, waiting for transfers between devices, swap(): return lax.ppermute(x, axis, [(i, i ^ mask) for i in range(size)])  13 us
    pallas_call x1, Pallas kernels, turn_partial(): pl.pallas_call(turn_kernel, grid=(steps,), in_specs=[pl.BlockSpec((BINS,...  12.2 us
    all_to_all x1, waiting for transfers between devices, body(): lax.all_to_all(half, 'cent', split_axis=0, concat_axis=0, tiled=True, axi...  11.2 us
    all_to_all x1, starting transfers between devices, body(): lax.all_to_all(sent, ('board', 'cent'), split_axis=0, concat_axis=0, tile...  10.8 us
  transfers between devices with their start and end apart: 15, of which 6 were waited for; matrix products, arithmetic and copies ran while one was open for 11% of the time, Pallas kernels for 25%

profile of v2, /device:TPU:0, one launch (start us, length us, event | category | flops | bytes accessed | tf_op | source)
XLA Modules:
  0.0 161.1 jit_solution(6092062809012692473)
XLA Ops:
  0.6 4.4 %pack.1 = bf16[128,80,128]{2,1,0:T(8,128)(2,1)} custom-call(bf16[50,24064]{1,0:T(8,128)(2,1)} %hist_ref.3), custom_call_target="tpu_custom_call" | custom-call | tf_op jit(solution)/shard_map/pack/pallas_call | solution.py:65
  5.7 12.2 %turn_sums.1 = f32[112,128]{1,0:T(8,128)} custom-call(bf16[50,24064]{1,0:T(8,128)(2,1)} %hist_ref.3, s32[1,24064]{1,0:T(1,128)} %broadcast_in_dim.12.label_ref), custom_call_target="tpu_custom_call" | custom-call | tf_op jit(solution)/shard_map/turn_sums/pallas_call | solution.py:99
  18.0 1.5 pad_maximum_fusion
  19.5 1.6 collective-permute-start
  21.1 1.6 collective-permute-start.1
  23.0 3.3 %collective-permute-start.3 = (f32[312,128]{1,0:T(8,128)}, f32[312,128]{1,0:T(8,128)}, u32[]{:S(2)}, u32[]{:S(2)}) collective-permute-start(f32[312,128]{1,0:T(8,128)} %pad_maximum_fusion), channel_id=1, source_target_pairs={{0,8},{1,9},{2,10},{3,11},{4,12},{5,13},{6,14},{7,15},{8,0},{9,1},... | collective-permute-start | bytes 479240 | tf_op jit(solution)/shard_map/ppermute | solution.py:248
  26.3 1.3 collective-permute-start.4
  27.6 10.8 %all-to-all-start = ((bf16[128,80,128]{2,1,0:T(8,128)(2,1)}), bf16[128,80,128]{2,1,0:T(8,128)(2,1)S(1)}, u32[]{:S(2)}, u32[]{:S(2)}) async-start(bf16[128,80,128]{2,1,0:T(8,128)(2,1)} %pack.1), calls=%async_computation | async-start | bytes 5242880 | tf_op jit(solution)/shard_map/all_to_all | solution.py:264
  42.2 2.3 %collective-permute-start.5 = (f32[312,128]{1,0:T(8,128)}, f32[312,128]{1,0:T(8,128)}, u32[]{:S(2)}, u32[]{:S(2)}) collective-permute-start(f32[312,128]{1,0:T(8,128)} %pad_maximum_fusion), channel_id=1, source_target_pairs={{0,12},{1,13},{2,14},{3,15},{4,8},{5,9},{6,10},{7,11},{8,4},{9,5},... | collective-permute-start | bytes 479240 | tf_op jit(solution)/shard_map/ppermute | solution.py:248
  45.5 1.5 collective-permute-start.6
  49.7 25.9 %all-to-all-done.recv_ref = bf16[128,80,128]{2,1,0:T(8,128)(2,1)S(1)} async-done(((bf16[128,80,128]{2,1,0:T(8,128)(2,1)}), bf16[128,80,128]{2,1,0:T(8,128)(2,1)S(1)}, u32[]{:S(2)}, u32[]{:S(2)}) %all-to-all-start) | async-done | bytes 2621472 | tf_op jit(solution)/shard_map/all_to_all | solution.py:264
  75.6 1.6 copy-done
  77.2 17.6 %place.1.cols_ref = f32[95,64,256]{2,1,0:T(8,128)} custom-call(s32[2]{0:T(128)} %pad_add_fusion.scalar_ref, bf16[128,80,128]{2,1,0:T(8,128)(2,1)} %copy-done, s32[96,256]{1,0:T(8,128)} %concatenate.30.place_ref), custom_call_target="tpu_custom_call" | custom-call | tf_op jit(solution)/shard_map/place/pallas_call | solution.py:197
  94.8 23.2 %member.1 = (f32[200,512]{1,0:T(8,128)}, f32[8,200,128]{2,1,0:T(8,128)}, f32[8,200,128]{2,1,0:T(8,128)}) custom-call(s32[2]{0:T(128)} %pad_add_fusion.scalar_ref, f32[95,64,256]{2,1,0:T(8,128)} %place.1.cols_ref, bf16[264,192]{1,0:T(8,128)(2,1)} %pad_maximum_fusion.2.table_ref, s32[1,512]{1,0:T(1,128)} %bitcast.41), custom_call_target="tpu_custom_call" | custom-call | tf_op jit(solution)/shard_map/member/pallas_call | solution.py:207
  121.3 2.2 %add.104 = f32[8,200,128]{2,1,0:T(8,128)} add(f32[8,200,128]{2,1,0:T(8,128)} %get-tuple-element.17, f32[8,200,128]{2,1,0:T(8,128)S(1)} %collective-permute-done.8) | non-fusion elementwise | flops 204800 | bytes 2457600 | tf_op jit(solution)/shard_map/add | solution.py:290
  123.5 3.5 %all-to-all-start.1 = ((f32[8,200,128]{2,1,0:T(8,128)}), f32[8,200,128]{2,1,0:T(8,128)S(1)}, u32[]{:S(2)}, u32[]{:S(2)}) async-start(f32[8,200,128]{2,1,0:T(8,128)} %add.104), calls=%async_computation.1 | async-start | bytes 1638400 | tf_op jit(solution)/shard_map/all_to_all | solution.py:291
  128.3 1.1 collective-permute-done.9
  129.6 11.2 %all-to-all-done.1 = f32[8,200,128]{2,1,0:T(8,128)S(1)} async-done(((f32[8,200,128]{2,1,0:T(8,128)}), f32[8,200,128]{2,1,0:T(8,128)S(1)}, u32[]{:S(2)}, u32[]{:S(2)}) %all-to-all-start.1) | async-done | bytes 819232 | tf_op jit(solution)/shard_map/all_to_all | solution.py:291
  140.8 1.3 collective-permute-start.10
  142.1 2.1 %subtract_reduce_fusion.1 = f32[512]{0:T(512)S(1)} fusion(f32[8,125]{1,0:T(8,128)S(1)} %multiply_reduce_fusion.1, f32[8,200,128]{2,1,0:T(8,128)S(1)} %fusion.9, f32[200,512]{1,0:T(8,128)S(1)} %copy-done.2), kind=kOutput, calls=%fused_computation.1 | convolution fusion | flops 1230335488 | bytes 1234848 | tf_op jit(solution)/shard_map/dot_general | solution.py:254
  144.2 3.5 %collective-permute-done.10 = f32[312,128]{1,0:T(8,128)S(1)} collective-permute-done((f32[312,128]{1,0:T(8,128)S(1)}, f32[312,128]{1,0:T(8,128)S(1)}, u32[]{:S(2)}, u32[]{:S(2)}) %collective-permute-start.10) | collective-permute-done | bytes 159776 | tf_op jit(solution)/shard_map/ppermute | solution.py:248
  148.0 2.2 %subtract_reduce_fusion = f32[512]{0:T(512)S(1)} fusion(f32[8,125]{1,0:T(8,128)S(1)} %multiply_reduce_fusion, f32[8,200,128]{2,1,0:T(8,128)S(1)} %collective-permute-done.7, f32[200,512]{1,0:T(8,128)S(1)} %copy-done.2), kind=kOutput, calls=%fused_computation | convolution fusion | flops 1230335488 | bytes 1234848 | tf_op jit(solution)/shard_map/dot_general | solution.py:254
  150.2 3.1 %collective-permute-done.11 = f32[312,128]{1,0:T(8,128)S(1)} collective-permute-done((f32[312,128]{1,0:T(8,128)S(1)}, f32[312,128]{1,0:T(8,128)S(1)}, u32[]{:S(2)}, u32[]{:S(2)}) %collective-permute-start.11) | collective-permute-done | bytes 159776 | tf_op jit(solution)/shard_map/ppermute | solution.py:248
  154.5 5.3 %collective-permute-done.12 = f32[312,128]{1,0:T(8,128)S(1)} collective-permute-done((f32[312,128]{1,0:T(8,128)S(1)}, f32[312,128]{1,0:T(8,128)S(1)}, u32[]{:S(2)}, u32[]{:S(2)}) %collective-permute-start.12) | collective-permute-done | bytes 159776 | tf_op jit(solution)/shard_map/ppermute | solution.py:248
  (80 shorter events, 16.0 us)
Async XLA Ops:
  0.6 4.4 %copy-start.4 = (s32[24064]{0:T(1024)S(1)}, s32[24064]{0:T(1024)}, u32[]{:S(2)}) copy-start(s32[24064]{0:T(1024)} %param.7) | copy-start | bytes 288772
  5.0 13.0 %copy-start.3 = (f32[200,125]{1,0:T(8,128)S(1)}, f32[200,125]{1,0:T(8,128)}, u32[]{:S(2)}) copy-start(f32[200,125]{1,0:T(8,128)} %param.10) | copy-start | bytes 300004
  19.5 18.9 %copy-start.6 = (f32[50,200]{1,0:T(8,128)S(1)}, f32[50,200]{1,0:T(8,128)}, u32[]{:S(2)}) copy-start(f32[50,200]{1,0:T(8,128)} %param.9) | copy-start | bytes 120004
  19.5 22.7 %collective-permute-start = (f32[312,128]{1,0:T(8,128)}, f32[312,128]{1,0:T(8,128)}, u32[]{:S(2)}, u32[]{:S(2)}) collective-permute-start(f32[312,128]{1,0:T(8,128)} %pad_maximum_fusion), channel_id=1, source_target_pairs={{0,2},{1,3},{2,0},{3,1},{4,6},{5,7},{6,4},{7,5},{8,10},{9,11},{10,... | collective-permute-start | bytes 479240 | tf_op jit(solution)/shard_map/ppermute | solution.py:248
  21.1 24.3 %collective-permute-start.1 = (f32[312,128]{1,0:T(8,128)}, f32[312,128]{1,0:T(8,128)}, u32[]{:S(2)}, u32[]{:S(2)}) collective-permute-start(f32[312,128]{1,0:T(8,128)} %pad_maximum_fusion), channel_id=1, source_target_pairs={{0,4},{1,5},{2,6},{3,7},{4,0},{5,1},{6,2},{7,3},{8,12},{9,13},{10,... | collective-permute-start | bytes 479240 | tf_op jit(solution)/shard_map/ppermute | solution.py:248
  22.7 25.2 %collective-permute-start.2 = (f32[312,128]{1,0:T(8,128)}, f32[312,128]{1,0:T(8,128)}, u32[]{:S(2)}, u32[]{:S(2)}) collective-permute-start(f32[312,128]{1,0:T(8,128)} %pad_maximum_fusion), channel_id=1, source_target_pairs={{0,6},{1,7},{2,4},{3,5},{4,2},{5,3},{6,0},{7,1},{8,14},{9,15},{10,... | collective-permute-start | bytes 479240 | tf_op jit(solution)/shard_map/ppermute | solution.py:248
  23.0 25.8 %collective-permute-start.3 = (f32[312,128]{1,0:T(8,128)}, f32[312,128]{1,0:T(8,128)}, u32[]{:S(2)}, u32[]{:S(2)}) collective-permute-start(f32[312,128]{1,0:T(8,128)} %pad_maximum_fusion), channel_id=1, source_target_pairs={{0,8},{1,9},{2,10},{3,11},{4,12},{5,13},{6,14},{7,15},{8,0},{9,1},... | collective-permute-start | bytes 479240 | tf_op jit(solution)/shard_map/ppermute | solution.py:248
  26.3 91.7 %collective-permute-start.4 = (f32[312,128]{1,0:T(8,128)}, f32[312,128]{1,0:T(8,128)}, u32[]{:S(2)}, u32[]{:S(2)}) collective-permute-start(f32[312,128]{1,0:T(8,128)} %pad_maximum_fusion), channel_id=1, source_target_pairs={{0,10},{1,11},{2,8},{3,9},{4,14},{5,15},{6,12},{7,13},{8,2},{9,3},... | collective-permute-start | bytes 479240 | tf_op jit(solution)/shard_map/ppermute | solution.py:248
  27.6 48.0 %all-to-all-start = ((bf16[128,80,128]{2,1,0:T(8,128)(2,1)}), bf16[128,80,128]{2,1,0:T(8,128)(2,1)S(1)}, u32[]{:S(2)}, u32[]{:S(2)}) async-start(bf16[128,80,128]{2,1,0:T(8,128)(2,1)} %pack.1), calls=%async_computation | async-start | bytes 5242880 | tf_op jit(solution)/shard_map/all_to_all | solution.py:264
  38.3 2.6 %copy-start.5 = (s32[47,512]{1,0:T(8,128)S(1)}, s32[47,512]{1,0:T(8,128)}, u32[]{:S(2)}) copy-start(s32[47,512]{1,0:T(8,128)} %param.8) | copy-start | bytes 288772
  42.2 76.7 %collective-permute-start.5 = (f32[312,128]{1,0:T(8,128)}, f32[312,128]{1,0:T(8,128)}, u32[]{:S(2)}, u32[]{:S(2)}) collective-permute-start(f32[312,128]{1,0:T(8,128)} %pad_maximum_fusion), channel_id=1, source_target_pairs={{0,12},{1,13},{2,14},{3,15},{4,8},{5,9},{6,10},{7,11},{8,4},{9,5},... | collective-permute-start | bytes 479240 | tf_op jit(solution)/shard_map/ppermute | solution.py:248
  45.5 74.4 %collective-permute-start.6 = (f32[312,128]{1,0:T(8,128)}, f32[312,128]{1,0:T(8,128)}, u32[]{:S(2)}, u32[]{:S(2)}) collective-permute-start(f32[312,128]{1,0:T(8,128)} %pad_maximum_fusion), channel_id=1, source_target_pairs={{0,14},{1,15},{2,12},{3,13},{4,10},{5,11},{6,8},{7,9},{8,6},{9,7},... | collective-permute-start | bytes 479240 | tf_op jit(solution)/shard_map/ppermute | solution.py:248
  75.6 1.6 copy-start
  118.0 3.3 %collective-permute-start.8 = (f32[8,200,128]{2,1,0:T(8,128)}, f32[8,200,128]{2,1,0:T(8,128)S(1)}, u32[]{:S(2)}, u32[]{:S(2)}) collective-permute-start(f32[8,200,128]{2,1,0:T(8,128)} %get-tuple-element.18), channel_id=1, source_target_pairs={{0,1},{1,0},{2,3},{3,2},{4,5},{5,4},{6,7},{7,6},{8,9},{9,8},{10,11... | collective-permute-start | bytes 2457608 | tf_op jit(solution)/shard_map/ppermute | solution.py:248
  120.7 6.3 %copy-start.1 = (f32[112,128]{1,0:T(8,128)S(1)}, f32[112,128]{1,0:T(8,128)}, u32[]{:S(2)}) copy-start(f32[112,128]{1,0:T(8,128)} %turn_sums.1) | copy-start | bytes 172036
  120.8 8.7 %collective-permute-start.7 = (f32[8,200,128]{2,1,0:T(8,128)S(1)}, f32[8,200,128]{2,1,0:T(8,128)S(1)}, u32[]{:S(2)}, u32[]{:S(2)}) collective-permute-start(f32[8,200,128]{2,1,0:T(8,128)S(1)} %fusion.9), channel_id=1, source_target_pairs={{0,1},{1,0},{2,3},{3,2},{4,5},{5,4},{6,7},{7,6},{8,9},{9,8},{10,11... | collective-permute-start | bytes 2457608 | tf_op jit(solution)/shard_map/ppermute | solution.py:248
  123.5 17.2 %all-to-all-start.1 = ((f32[8,200,128]{2,1,0:T(8,128)}), f32[8,200,128]{2,1,0:T(8,128)S(1)}, u32[]{:S(2)}, u32[]{:S(2)}) async-start(f32[8,200,128]{2,1,0:T(8,128)} %add.104), calls=%async_computation.1 | async-start | bytes 1638400 | tf_op jit(solution)/shard_map/all_to_all | solution.py:291
  127.1 15.0 %copy-start.2 = (f32[200,512]{1,0:T(8,128)S(1)}, f32[200,512]{1,0:T(8,128)}, u32[]{:S(2)}) copy-start(f32[200,512]{1,0:T(8,128)} %get-tuple-element.16) | copy-start | bytes 1228804
  128.1 1.3 collective-permute-start.9
  140.8 6.9 %collective-permute-start.10 = (f32[312,128]{1,0:T(8,128)S(1)}, f32[312,128]{1,0:T(8,128)S(1)}, u32[]{:S(2)}, u32[]{:S(2)}) collective-permute-start(f32[312,128]{1,0:T(8,128)S(1)} %pad_maximum_fusion.1), channel_id=1, source_target_pairs={{0,16},{16,0},{32,48},{48,32},{64,80},{80,64},{96,112},{112,96},{1... | collective-permute-start | bytes 479240 | tf_op jit(solution)/shard_map/ppermute | solution.py:248
  147.7 5.5 %collective-permute-start.11 = (f32[312,128]{1,0:T(8,128)S(1)}, f32[312,128]{1,0:T(8,128)S(1)}, u32[]{:S(2)}, u32[]{:S(2)}) collective-permute-start(f32[312,128]{1,0:T(8,128)S(1)} %fusion.28), channel_id=1, source_target_pairs={{0,32},{16,48},{32,0},{48,16},{64,96},{80,112},{96,64},{112,80},{1... | collective-permute-start | bytes 479240 | tf_op jit(solution)/shard_map/ppermute | solution.py:248
  153.2 6.6 %collective-permute-start.12 = (f32[312,128]{1,0:T(8,128)S(1)}, f32[312,128]{1,0:T(8,128)S(1)}, u32[]{:S(2)}, u32[]{:S(2)}) collective-permute-start(f32[312,128]{1,0:T(8,128)S(1)} %add.114), channel_id=1, source_target_pairs={{0,96},{16,112},{32,64},{48,80},{64,32},{80,48},{96,0},{112,16},{1... | collective-permute-start | bytes 479240 | tf_op jit(solution)/shard_map/ppermute | solution.py:248

commit v3 on v2

--- a/solution.py
+++ b/solution.py
@@ -110,71 +110,89 @@
 TILES = KIDS * HANDS // TILE
 
 
-def split3(x):
-    hi = x.astype(bf16)
-    rest = x - hi.astype(f32)
-    mid = rest.astype(bf16)
-    low = (rest - mid.astype(f32)).astype(bf16)
-    return hi, mid, low
-
-
-def place_kernel(scalar_ref, recv_ref, place_ref, cols_ref):
-    o = scalar_ref[0]
-    lane = lax.broadcasted_iota(i32, (16, LANES), 1)
-    row = lax.broadcasted_iota(i32, (16, LANES), 0)
-    first = ((lane - o) & 127) < 64
-    from_c1 = (~first) & (row >= 2) & (row < 4)
-    from_r1 = first & (row >= 4) & (row < 6)
-    b3_rows = row < 2
-    wide_lane = lax.broadcasted_iota(i32, (64, TILE), 1)
-    one_lane = lax.broadcasted_iota(i32, (1, TILE), 1)
-    sub = lax.broadcasted_iota(i32, (TILE, TILE), 0)
+def place_columns(o, recv_ref, place_ref, cols_ref):
+    row = lax.broadcasted_iota(i32, (8, LANES), 0)
+    lane = lax.broadcasted_iota(i32, (8, LANES), 1)
+    tail_hi, tail_mid, tail_low = row < 2, (row >= 2) & (row < 4), (row >= 4) & (row < 6)
+    zero = jnp.zeros((8, LANES), f32)
+
+    def gather(x, index):
+        return jnp.take_along_axis(x, index, axis=1)
 
     def place(s, carry):
         start = s * BLOCK
         t0 = start // TILE
         a = start - t0 * TILE
-        c0 = recv_ref[s, 48:64, :].astype(f32)
-        c1 = recv_ref[s, 64:80, :].astype(f32)
-        r0 = pltpu.roll(c0, 64, 1)
-        r1 = pltpu.roll(c1, 64, 1)
-        a3 = jnp.where(from_c1, c1, jnp.where(from_r1, r1, 0.0))
-        b3 = jnp.where(b3_rows, r1, 0.0)
-        left = jnp.concatenate([recv_ref[s, 0:48, :], a3.astype(bf16)], axis=0)
-        right = jnp.concatenate(
-            [recv_ref[s, 48:64, :], r0.astype(bf16), recv_ref[s, 64:80, :], b3.astype(bf16)], axis=0)
-        payload = jnp.concatenate([left, right], axis=1)
-        q = jnp.where(one_lane >= a, place_ref[pl.ds(t0, 1), :], place_ref[pl.ds(t0 + 1, 1), :])
-        onehot = (sub == q).astype(f32).astype(bf16)
-        cols = jnp.dot(payload, onehot, preferred_element_type=f32)
-        cols_ref[t0] = jnp.where(wide_lane >= a, cols, cols_ref[t0])
-        cols_ref[t0 + 1] = cols
+        tiles = []
+        for t in range(PACK_ROWS // 16):
+            both = recv_ref[s, 16 * t:16 * t + 16, :].astype(f32)
+            tiles += [both[0:8], both[8:16]]
+        now, later = place_ref[pl.ds(t0, 1), :], place_ref[pl.ds(t0 + 1, 1), :]
+        following = []
+        for half in range(2):
+            side = slice(half * LANES, (half + 1) * LANES)
+            mask = lane + half * LANES >= a
+            spill = lane + (half * LANES + TILE) < a + BLOCK
+            r = jnp.where(mask, now[:, side], later[:, side])
+            p = (r + o) & 127
+            p2 = p ^ 64
+            far = r >= LANES
+            first = ((p - o) & 127) < 64
+            out = []
+            for g in range(6):
+                source, index = tiles[(6, 7, 6, 7, 8, 9)[g]], p2 if g in (2, 3) else p
+                out.append(jnp.where(far, gather(source, index), gather(tiles[g], p)))
+            near, turned = gather(tiles[8], p), gather(tiles[8], p2)
+            out.append(jnp.where(far & tail_hi | ~far & first & tail_low, turned,
+                                 jnp.where(~far & ~first & tail_mid, near, zero)))
+            merged = [jnp.where(mask, out[g], carry[7 * half + g]) for g in range(7)]
+            for g in range(4):
+                pair = jnp.concatenate([merged[2 * g], merged[2 * g + 1] if g < 3 else zero], axis=0)
+                cols_ref[t0, 16 * g:16 * g + 16, side] = pair.astype(bf16)
+            following += [jnp.where(spill, out[g], merged[g]) for g in range(7)]
+        return tuple(following)
+
+    lax.fori_loop(0, DEVICES, place, (zero,) * 14, unroll=4)
+
+
+def member_kernel(scalar_ref, recv_ref, place_ref, table_ref, assign_ref,
+                  hist_ref, keep_ref, send_ref, cols_ref, even_ref, odd_ref):
+    core = scalar_ref[1]
+    place_columns(scalar_ref[0], recv_ref, place_ref, cols_ref)
+
+    def products(i, out_ref):
+        h = jnp.concatenate([cols_ref[2 * i], cols_ref[2 * i + 1]], axis=1)
+        out_ref[...] = jnp.dot(
+            table_ref[...], jnp.concatenate([h, h, h], axis=0), preferred_element_type=f32)
+
+    def add_kid(z_ref):
+        for c in range(HANDS // LANES):
+            at = slice(c * LANES, (c + 1) * LANES)
+            cdf = z_ref[200:256, at]
+            total = z_ref[256:264, at]
+            sq = jnp.sum(cdf * cdf, axis=0, keepdims=True)
+            extra = total + sharpness * sq / total
+            y = z_ref[0:200, at].reshape(25, 8, LANES) + extra[None]
+            w = 1.0 / (y * y)
+            scale = 1.0 / jnp.sum(jnp.sum(w, axis=0), axis=0, keepdims=True)
+            hist_ref[:, at] += (w * scale[None]).reshape(200, LANES)
+
+    hist_ref[...] = jnp.zeros_like(hist_ref)
+    products(0, even_ref)
+
+    def two_kids(j, carry):
+        products(2 * j + 1, odd_ref)
+        add_kid(even_ref)
+        products(2 * j + 2, even_ref)
+        add_kid(odd_ref)
         return carry
 
-    cols_ref[0] = jnp.zeros((64, TILE), f32)
-    lax.fori_loop(0, DEVICES, place, 0, unroll=2)
-
-
-def member_kernel(scalar_ref, cols_ref, table_ref, assign_ref, hist_ref, keep_ref, send_ref):
-    core = scalar_ref[1]
-    hist_ref[...] = jnp.zeros_like(hist_ref)
-
-    def kid(i, carry):
-        h = jnp.concatenate([cols_ref[2 * i].astype(bf16), cols_ref[2 * i + 1].astype(bf16)], axis=1)
-        z = jnp.dot(table_ref[...], jnp.concatenate([h, h, h], axis=0), preferred_element_type=f32)
-        cdf = z[200:256]
-        total = z[256:264]
-        sq = jnp.sum(cdf * cdf, axis=0, keepdims=True)
-        extra = total[0:1] + sharpness * sq / total[0:1]
-        y = z[0:200] + extra
-        w = 1.0 / (y * y)
-        hist_ref[...] += w * (1.0 / jnp.sum(w, axis=0, keepdims=True))
-        return carry
-
-    lax.fori_loop(0, KIDS, kid, 0)
-
-    hi, mid, low = split3(hist_ref[...])
-    stack = jnp.concatenate([hi, mid, low], axis=0)
+    lax.fori_loop(0, KIDS // 2, two_kids, 0)
+    add_kid(even_ref)
+
+    hi = hist_ref[...].astype(bf16)
+    rest = (hist_ref[...] - hi.astype(f32)).astype(bf16)
+    stack = jnp.concatenate([hi, rest], axis=0)
     ids = lax.broadcasted_iota(i32, (LANES, HANDS), 0)
     valid = ids < PANEL
     for i in range(8):
@@ -184,7 +202,7 @@
             halves.append((valid & (assign_ref[...] - base == ids)).astype(f32).astype(bf16))
         onehot = jnp.concatenate(halves, axis=0)
         sums = lax.dot_general(stack, onehot, (((1,), (1,)), ((), ())), preferred_element_type=f32)
-        both = sums[0:200] + sums[200:400] + sums[400:600]
+        both = sums[0:200] + sums[200:400]
         keep_ref[i] = both[:, :LANES]
         send_ref[i] = both[:, LANES:]
 
@@ -193,28 +211,52 @@
 SMEM = pl.BlockSpec(memory_space=pltpu.SMEM)
 
 
-def place_columns(scalars, recv, place):
-    return pl.pallas_call(
-        place_kernel,
-        in_specs=[SMEM, VMEM, VMEM],
-        out_specs=VMEM,
-        out_shape=jax.ShapeDtypeStruct((TILES + 1, 64, TILE), f32),
-        name="place",
-    )(scalars, recv, place)
-
-
-def member(scalars, cols, table, assign):
+def member(scalars, recv, place, table, assign):
     return pl.pallas_call(
         member_kernel,
-        in_specs=[SMEM, VMEM, VMEM, VMEM],
+        in_specs=[SMEM, VMEM, VMEM, VMEM, VMEM],
         out_specs=[VMEM, VMEM, VMEM],
         out_shape=[
             jax.ShapeDtypeStruct((TURN_CENT, HANDS), f32),
             jax.ShapeDtypeStruct((8, TURN_CENT, LANES), f32),
             jax.ShapeDtypeStruct((8, TURN_CENT, LANES), f32),
         ],
+        scratch_shapes=[
+            pltpu.VMEM((TILES, 64, TILE), bf16),
+            pltpu.VMEM((264, HANDS), f32),
+            pltpu.VMEM((264, HANDS), f32),
+        ],
         name="member",
-    )(scalars, cols, table, assign)
+    )(scalars, recv, place, table, assign)
+
+
+def nearest_kernel(mine_ref, partner_ref, *refs):
+    pieces, out_ref = refs[:-1], refs[-1]
+    one = jnp.where(lax.broadcasted_iota(i32, (8, 2 * HANDS), 0) == 0, 1.0, 0.0)
+    hands = jnp.concatenate([jnp.concatenate([mine_ref[...], partner_ref[...]], axis=1), one], axis=0)
+    lane = lax.broadcasted_iota(i32, (8, LANES), 1)
+    best = None
+    for ref in pieces:
+        c = ref[0:TURN_CENT, :]
+        sq = jnp.broadcast_to(jnp.sum(c * c, axis=0, keepdims=True), (8, LANES))
+        sides = jnp.concatenate([-2.0 * c, jnp.where(lane < PANEL, sq, 1e30)], axis=0)
+        dist = lax.dot_general(
+            sides, hands, (((0,), (0,)), ((), ())), precision=highest, preferred_element_type=f32)
+        part = jnp.min(dist, axis=0, keepdims=True)
+        best = part if best is None else jnp.minimum(best, part)
+    out_ref[...] = best
+
+
+def nearest_of(pieces, flop_hist, partner):
+    best = pl.pallas_call(
+        nearest_kernel,
+        in_specs=[VMEM] * (2 + len(pieces)),
+        out_specs=VMEM,
+        out_shape=jax.ShapeDtypeStruct((1, 2 * HANDS), f32),
+        name="nearest",
+    )(flop_hist, partner, *pieces)
+    best = jnp.minimum(best[:, :HANDS], swap(best[:, HANDS:], "cent", 1))
+    return best[0] + jnp.sum(jnp.square(flop_hist), axis=0)
 
 
 def center_table(turn_centers):
@@ -248,16 +290,6 @@
     return lax.ppermute(x, axis, [(i, i ^ mask) for i in range(size)])
 
 
-def nearest_of(pieces, flop_hist):
-    best = None
-    for piece in pieces:
-        cross = lax.dot_general(
-            piece, flop_hist, (((1,), (0,)), ((), ())), precision=highest, preferred_element_type=f32)
-        part = jnp.min(jnp.sum(jnp.square(piece), axis=1)[:, :, None] - 2.0 * cross, axis=(0, 1))
-        best = part if best is None else jnp.minimum(best, part)
-    return best + jnp.sum(jnp.square(flop_hist), axis=0)
-
-
 def body(turn_hist, turn_assign, child_rows, turn_centers, flop_centers, flop_assign):
     sent = pack(turn_hist)
     turn_assign, sent = lax.optimization_barrier((turn_assign, sent))
@@ -273,20 +305,15 @@
     for mask in range(2, 16, 2):
         pieces.append(swap(own, "cent", mask))
 
-    place = (child_rows & 128) + ((child_rows + offset) & 127)
-    place = jnp.concatenate([place.reshape(TILES, TILE), jnp.full((2, TILE), -1, i32)], axis=0)
+    place = jnp.concatenate([child_rows.reshape(TILES, TILE), jnp.zeros((2, TILE), i32)], axis=0)
     table = center_table(turn_centers)
     place, table, scalars = lax.optimization_barrier((place, table, scalars))
 
-    cols = place_columns(scalars, arrived, place)
-
-    mine = jnp.stack([piece[:TURN_CENT] for piece in pieces])
+    flop_hist, keep, send = member(scalars, arrived, place, table, flop_assign[None, :])
+
+    partner = swap(flop_hist, "cent", 1)
     turn_part = sum((piece[TURN_CENT:] for piece in pieces[1:]), turn_part)
-    other = swap(mine, "cent", 1)
     turn_part = turn_part + swap(turn_part, "cent", 1)
-
-    flop_hist, keep, send = member(scalars, cols, table, flop_assign[None, :])
-
     half = keep + swap(send, "cent", 1)
     parts = lax.all_to_all(half, "cent", split_axis=0, concat_axis=0, tiled=True, axis_index_groups=CHIPS)
     total = jnp.concatenate([jnp.sum(parts, axis=0), turn_part], axis=0)
@@ -298,7 +325,7 @@
     turn_sums = jnp.concatenate([turn_low, turn_high], axis=1)
     turn_sums = turn_sums * (BINS * TURN_CENT / (turn_hist.shape[1] * DEVICES))
 
-    nearest = nearest_of((mine[:, :, :PANEL], other[:, :, :PANEL]), flop_hist)
+    nearest = nearest_of(pieces, flop_hist, partner)
     return nearest, turn_sums, flop_sums
 
 

time: 162 us -> 154 us (0.951)
  waiting for transfers between devices: 50.1 us -> 68.7 us
  Pallas kernels: 57.5 us -> 44.5 us
  local copies, waits for them, and re-layouts: 10.2 us -> 5.26 us
  matrix products: 4.96 us -> 0.68 us
  other arithmetic: 8.47 us -> 5.33 us
  starting transfers between devices: 29.1 us -> 27.2 us
    ppermute x13 -> x14, waiting for transfers between devices: 13 us -> 36.5 us  [swap(): return lax.ppermute(x, axis, [(i, i ^ mask) for i in range(size)])]
    pallas_call x2, Pallas kernels: 40.9 us -> 27.9 us  [the longest x1 22.2 us: member(): pl.pallas_call(member_kernel, in_specs=[SMEM, VMEM, VMEM, VMEM, VMEM], ou...]
    all_to_all x1, waiting for transfers between devices: 11.2 us -> 0.01 us  [body(): lax.all_to_all(half, 'cent', split_axis=0, concat_axis=0, tiled=True, axi...]
    all_to_all x1, waiting for transfers between devices: 25.9 us -> 32.1 us  [body(): lax.all_to_all(sent, ('board', 'cent'), split_axis=0, concat_axis=0, tile...]
    unnamed x21 -> x36, local copies, waits for them, and re-layouts: 7.01 us -> 2.35 us
    dot_general x2 -> x0, matrix products: 4.27 us -> none  [nearest_of(): lax.dot_general(piece, flop_hist, (((1,), (0,)), ((), ())), precision=hig...]
    ppermute x13 -> x14, starting transfers between devices: 14.8 us -> 12.5 us  [swap(): return lax.ppermute(x, axis, [(i, i ^ mask) for i in range(size)])]
  transfers between devices with their start and end apart: 15 -> 16, of which waited for: 6 -> 9; matrix products, arithmetic and copies ran while one was open for 11% -> 4% of each run, Pallas kernels for 25% -> 12%
where the time goes in v3:
time: 154 us; the launch traced here: 153 us
  waiting for transfers between devices  68.7 us (45%)
  Pallas kernels  44.5 us (29%)
  starting transfers between devices  27.2 us (18%)
  other arithmetic  5.33 us (3%)
  local copies, waits for them, and re-layouts  5.26 us (3%)
    ppermute x14, waiting for transfers between devices, swap(): return lax.ppermute(x, axis, [(i, i ^ mask) for i in range(size)])  36.5 us
    all_to_all x1, waiting for transfers between devices, body(): lax.all_to_all(sent, ('board', 'cent'), split_axis=0, concat_axis=0, tile...  32.1 us
    pallas_call x1, Pallas kernels, member(): pl.pallas_call(member_kernel, in_specs=[SMEM, VMEM, VMEM, VMEM, VMEM], ou...  22.2 us
    ppermute x14, starting transfers between devices, swap(): return lax.ppermute(x, axis, [(i, i ^ mask) for i in range(size)])  12.5 us
    pallas_call x1, Pallas kernels, turn_partial(): pl.pallas_call(turn_kernel, grid=(steps,), in_specs=[pl.BlockSpec((BINS,...  12.2 us
    all_to_all x1, starting transfers between devices, body(): lax.all_to_all(sent, ('board', 'cent'), split_axis=0, concat_axis=0, tile...  11.2 us
    pallas_call x1, Pallas kernels, nearest_of(): pl.pallas_call(nearest_kernel, in_specs=[VMEM] * (2 + len(pieces)), out_s...  5.67 us
    pallas_call x1, Pallas kernels, pack(): pl.pallas_call(pack_kernel, grid=(DEVICES // SOURCES_PER_STEP,), in_specs...  4.36 us
  transfers between devices with their start and end apart: 16, of which 9 were waited for; matrix products, arithmetic and copies ran while one was open for 4% of the time, Pallas kernels for 12%

profile of v3, /device:TPU:0, one launch (start us, length us, event | category | flops | bytes accessed | tf_op | source)
XLA Modules:
  0.0 152.6 jit_solution(2903912042828298863)
XLA Ops:
  0.6 4.4 %pack.1 = bf16[128,80,128]{2,1,0:T(8,128)(2,1)} custom-call(bf16[50,24064]{1,0:T(8,128)(2,1)} %hist_ref.3), custom_call_target="tpu_custom_call" | custom-call | tf_op jit(solution)/shard_map/pack/pallas_call | solution.py:65
  5.0 11.2 %all-to-all-start = ((bf16[128,80,128]{2,1,0:T(8,128)(2,1)}), bf16[128,80,128]{2,1,0:T(8,128)(2,1)S(1)}, u32[]{:S(2)}, u32[]{:S(2)}) async-start(bf16[128,80,128]{2,1,0:T(8,128)(2,1)} %pack.1), calls=%async_computation | async-start | bytes 5242880 | tf_op jit(solution)/shard_map/all_to_all | solution.py:296
  20.0 32.1 %all-to-all-done.recv_ref = bf16[128,80,128]{2,1,0:T(8,128)(2,1)S(1)} async-done(((bf16[128,80,128]{2,1,0:T(8,128)(2,1)}), bf16[128,80,128]{2,1,0:T(8,128)(2,1)S(1)}, u32[]{:S(2)}, u32[]{:S(2)}) %all-to-all-start) | async-done | bytes 2621472 | tf_op jit(solution)/shard_map/all_to_all | solution.py:296
  52.2 1.5 copy-done
  53.7 22.2 %member.1 = (f32[200,512]{1,0:T(8,128)}, f32[8,200,128]{2,1,0:T(8,128)}, f32[8,200,128]{2,1,0:T(8,128)}) custom-call(s32[2]{0:T(128)} %pad_add_fusion.scalar_ref, bf16[128,80,128]{2,1,0:T(8,128)(2,1)} %copy-done, s32[96,256]{1,0:T(8,128)} %concatenate.29.place_ref, bf16[264,192]{1,0:T(8,128)(2,1)} %pad_maximum_fusion.1.table_ref, s32[1,512]{1,0:T(1,128)} %bitcast.8), custom_call_target="tpu_custom_call" | custom-call | tf_op jit(solution)/shard_map/member/pallas_call | solution.py:215
  75.9 0.7 broadcast_in_dim.28.label_ref
  76.6 12.2 %turn_sums.1 = f32[112,128]{1,0:T(8,128)} custom-call(bf16[50,24064]{1,0:T(8,128)(2,1)} %hist_ref.3, s32[1,24064]{1,0:T(1,128)} %broadcast_in_dim.28.label_ref), custom_call_target="tpu_custom_call" | custom-call | tf_op jit(solution)/shard_map/turn_sums/pallas_call | solution.py:99
  88.9 1.0 add.92
  89.9 3.5 %all-to-all-start.1 = ((f32[8,200,128]{2,1,0:T(8,128)}), f32[8,200,128]{2,1,0:T(8,128)S(1)}, u32[]{:S(2)}, u32[]{:S(2)}) async-start(f32[8,200,128]{2,1,0:T(8,128)} %add.92), calls=%async_computation.1 | async-start | bytes 1638400 | tf_op jit(solution)/shard_map/all_to_all | solution.py:318
  93.5 4.1 %collective-permute-start.7 = (f32[312,128]{1,0:T(8,128)S(1)}, f32[312,128]{1,0:T(8,128)S(1)}, u32[]{:S(2)}, u32[]{:S(2)}) collective-permute-start(f32[312,128]{1,0:T(8,128)S(1)} %select_maximum_fusion.refs_0_), channel_id=1, source_target_pairs={{0,14},{1,15},{2,12},{3,13},{4,10},{5,11},{6,8},{7,9},{8,6},{9,7},... | collective-permute-start | bytes 479240 | tf_op jit(solution)/shard_map/ppermute | solution.py:290
  98.2 1.8 %collective-permute-start.5 = (f32[312,128]{1,0:T(8,128)S(1)}, f32[312,128]{1,0:T(8,128)S(1)}, u32[]{:S(2)}, u32[]{:S(2)}) collective-permute-start(f32[312,128]{1,0:T(8,128)S(1)} %select_maximum_fusion.refs_0_), channel_id=1, source_target_pairs={{0,10},{1,11},{2,8},{3,9},{4,14},{5,15},{6,12},{7,13},{8,2},{9,3},... | collective-permute-start | bytes 479240 | tf_op jit(solution)/shard_map/ppermute | solution.py:290
  99.9 1.3 collective-permute-start.4
  101.3 1.6 %collective-permute-start.3 = (f32[312,128]{1,0:T(8,128)S(1)}, f32[312,128]{1,0:T(8,128)S(1)}, u32[]{:S(2)}, u32[]{:S(2)}) collective-permute-start(f32[312,128]{1,0:T(8,128)S(1)} %select_maximum_fusion.refs_0_), channel_id=1, source_target_pairs={{0,6},{1,7},{2,4},{3,5},{4,2},{5,3},{6,0},{7,1},{8,14},{9,15},{10,... | collective-permute-start | bytes 479240 | tf_op jit(solution)/shard_map/ppermute | solution.py:290
  102.9 11.5 %collective-permute-done.7.refs_7_ = f32[312,128]{1,0:T(8,128)S(1)} collective-permute-done((f32[312,128]{1,0:T(8,128)S(1)}, f32[312,128]{1,0:T(8,128)S(1)}, u32[]{:S(2)}, u32[]{:S(2)}) %collective-permute-start.7) | collective-permute-done | bytes 159776 | tf_op jit(solution)/shard_map/ppermute | solution.py:290
  114.5 6.1 %collective-permute-done.6.refs_6_ = f32[312,128]{1,0:T(8,128)S(1)} collective-permute-done((f32[312,128]{1,0:T(8,128)S(1)}, f32[312,128]{1,0:T(8,128)S(1)}, u32[]{:S(2)}, u32[]{:S(2)}) %collective-permute-start.6) | collective-permute-done | bytes 159776 | tf_op jit(solution)/shard_map/ppermute | solution.py:290
  121.4 1.2 collective-permute-done.2.refs_2_
  122.6 4.1 %collective-permute-done.1.refs_1_ = f32[312,128]{1,0:T(8,128)S(1)} collective-permute-done((f32[312,128]{1,0:T(8,128)S(1)}, f32[312,128]{1,0:T(8,128)S(1)}, u32[]{:S(2)}, u32[]{:S(2)}) %collective-permute-start.1) | collective-permute-done | bytes 159776 | tf_op jit(solution)/shard_map/ppermute | solution.py:290
  126.8 1.2 collective-permute-done.10
  128.1 1.0 collective-permute-start.11
  129.1 6.8 %collective-permute-done.11 = f32[312,128]{1,0:T(8,128)S(1)} collective-permute-done((f32[312,128]{1,0:T(8,128)S(1)}, f32[312,128]{1,0:T(8,128)S(1)}, u32[]{:S(2)}, u32[]{:S(2)}) %collective-permute-start.11) | collective-permute-done | bytes 159776 | tf_op jit(solution)/shard_map/ppermute | solution.py:290
  136.3 0.8 copy-done.6
  137.1 5.7 %nearest.1 = f32[1,1024]{1,0:T(1,128)} custom-call(f32[200,512]{1,0:T(8,128)} %get-tuple-element.15.mine_ref, f32[200,512]{1,0:T(8,128)} %copy-done.6, f32[312,128]{1,0:T(8,128)} %copy-done.4, f32[312,128]{1,0:T(8,128)} %copy-done.13, f32[312,128]{1,0:T(8,128)} %copy-done.12, f32[312,128]{1,0:T(8,128)} %copy-done.11, f32[312,128]{1,0:T(8,128)} %copy-done.10, ...), custom_call_target="tpu_custom_call" | custom-call | tf_op jit(solution)/shard_map/nearest/pallas_call | solution.py:251
  143.5 0.9 collective-permute-start.13
  145.8 5.5 %collective-permute-done.13 = f32[312,128]{1,0:T(8,128)S(1)} collective-permute-done((f32[312,128]{1,0:T(8,128)S(1)}, f32[312,128]{1,0:T(8,128)S(1)}, u32[]{:S(2)}, u32[]{:S(2)}) %collective-permute-start.13) | collective-permute-done | bytes 159776 | tf_op jit(solution)/shard_map/ppermute | solution.py:290
  (92 shorter events, 9.1 us)
Async XLA Ops:
  5.0 47.2 %all-to-all-start = ((bf16[128,80,128]{2,1,0:T(8,128)(2,1)}), bf16[128,80,128]{2,1,0:T(8,128)(2,1)S(1)}, u32[]{:S(2)}, u32[]{:S(2)}) async-start(bf16[128,80,128]{2,1,0:T(8,128)(2,1)} %pack.1), calls=%async_computation | async-start | bytes 5242880 | tf_op jit(solution)/shard_map/all_to_all | solution.py:296
  17.3 58.5 %copy-start.16 = (s32[24064]{0:T(1024)S(1)}, s32[24064]{0:T(1024)}, u32[]{:S(2)}) copy-start(s32[24064]{0:T(1024)} %param.7) | copy-start | bytes 288772
  75.9 13.0 %collective-permute-start.9 = (f32[8,200,128]{2,1,0:T(8,128)}, f32[8,200,128]{2,1,0:T(8,128)S(1)}, u32[]{:S(2)}, u32[]{:S(2)}) collective-permute-start(f32[8,200,128]{2,1,0:T(8,128)} %get-tuple-element.18), channel_id=1, source_target_pairs={{0,1},{1,0},{2,3},{3,2},{4,5},{5,4},{6,7},{7,6},{8,9},{9,8},{10,11... | collective-permute-start | bytes 2457608 | tf_op jit(solution)/shard_map/ppermute | solution.py:290
  88.9 40.3 %copy-start.1 = (f32[200,512]{1,0:T(8,128)S(1)}, f32[200,512]{1,0:T(8,128)}, u32[]{:S(2)}) copy-start(f32[200,512]{1,0:T(8,128)} %get-tuple-element.15.mine_ref) | copy-start | bytes 1228804
  89.9 38.2 %all-to-all-start.1 = ((f32[8,200,128]{2,1,0:T(8,128)}), f32[8,200,128]{2,1,0:T(8,128)S(1)}, u32[]{:S(2)}, u32[]{:S(2)}) async-start(f32[8,200,128]{2,1,0:T(8,128)} %add.92), calls=%async_computation.1 | async-start | bytes 1638400 | tf_op jit(solution)/shard_map/all_to_all | solution.py:318
  93.5 49.9 %copy-start.2 = (f32[200,512]{1,0:T(8,128)S(1)}, f32[200,512]{1,0:T(8,128)}, u32[]{:S(2)}) copy-start(f32[200,512]{1,0:T(8,128)} %get-tuple-element.15.mine_ref) | copy-start | bytes 1228804
  93.5 42.7 %copy-start.4 = (f32[312,128]{1,0:T(8,128)}, f32[312,128]{1,0:T(8,128)S(1)}, u32[]{:S(2)}) copy-start(f32[312,128]{1,0:T(8,128)S(1)} %select_maximum_fusion.refs_0_) | copy-start | bytes 479236
  93.5 20.8 %collective-permute-start.7 = (f32[312,128]{1,0:T(8,128)S(1)}, f32[312,128]{1,0:T(8,128)S(1)}, u32[]{:S(2)}, u32[]{:S(2)}) collective-permute-start(f32[312,128]{1,0:T(8,128)S(1)} %select_maximum_fusion.refs_0_), channel_id=1, source_target_pairs={{0,14},{1,15},{2,12},{3,13},{4,10},{5,11},{6,8},{7,9},{8,6},{9,7},... | collective-permute-start | bytes 479240 | tf_op jit(solution)/shard_map/ppermute | solution.py:290
  97.6 23.0 %collective-permute-start.6 = (f32[312,128]{1,0:T(8,128)S(1)}, f32[312,128]{1,0:T(8,128)S(1)}, u32[]{:S(2)}, u32[]{:S(2)}) collective-permute-start(f32[312,128]{1,0:T(8,128)S(1)} %select_maximum_fusion.refs_0_), channel_id=1, source_target_pairs={{0,12},{1,13},{2,14},{3,15},{4,8},{5,9},{6,10},{7,11},{8,4},{9,5},... | collective-permute-start | bytes 479240 | tf_op jit(solution)/shard_map/ppermute | solution.py:290
  98.2 23.2 %collective-permute-start.5 = (f32[312,128]{1,0:T(8,128)S(1)}, f32[312,128]{1,0:T(8,128)S(1)}, u32[]{:S(2)}, u32[]{:S(2)}) collective-permute-start(f32[312,128]{1,0:T(8,128)S(1)} %select_maximum_fusion.refs_0_), channel_id=1, source_target_pairs={{0,10},{1,11},{2,8},{3,9},{4,14},{5,15},{6,12},{7,13},{8,2},{9,3},... | collective-permute-start | bytes 479240 | tf_op jit(solution)/shard_map/ppermute | solution.py:290
  99.9 21.4 %collective-permute-start.4 = (f32[312,128]{1,0:T(8,128)S(1)}, f32[312,128]{1,0:T(8,128)S(1)}, u32[]{:S(2)}, u32[]{:S(2)}) collective-permute-start(f32[312,128]{1,0:T(8,128)S(1)} %select_maximum_fusion.refs_0_), channel_id=1, source_target_pairs={{0,8},{1,9},{2,10},{3,11},{4,12},{5,13},{6,14},{7,15},{8,0},{9,1},... | collective-permute-start | bytes 479240 | tf_op jit(solution)/shard_map/ppermute | solution.py:290
  101.3 20.1 %collective-permute-start.3 = (f32[312,128]{1,0:T(8,128)S(1)}, f32[312,128]{1,0:T(8,128)S(1)}, u32[]{:S(2)}, u32[]{:S(2)}) collective-permute-start(f32[312,128]{1,0:T(8,128)S(1)} %select_maximum_fusion.refs_0_), channel_id=1, source_target_pairs={{0,6},{1,7},{2,4},{3,5},{4,2},{5,3},{6,0},{7,1},{8,14},{9,15},{10,... | collective-permute-start | bytes 479240 | tf_op jit(solution)/shard_map/ppermute | solution.py:290
  114.3 21.9 %copy-start.7 = (f32[312,128]{1,0:T(8,128)}, f32[312,128]{1,0:T(8,128)S(1)}, u32[]{:S(2)}) copy-start(f32[312,128]{1,0:T(8,128)S(1)} %collective-permute-done.7.refs_7_) | copy-start | bytes 479236
  114.3 8.2 %collective-permute-start.2 = (f32[312,128]{1,0:T(8,128)S(1)}, f32[312,128]{1,0:T(8,128)S(1)}, u32[]{:S(2)}, u32[]{:S(2)}) collective-permute-start(f32[312,128]{1,0:T(8,128)S(1)} %select_maximum_fusion.refs_0_), channel_id=1, source_target_pairs={{0,4},{1,5},{2,6},{3,7},{4,0},{5,1},{6,2},{7,3},{8,12},{9,13},{10,... | collective-permute-start | bytes 479240 | tf_op jit(solution)/shard_map/ppermute | solution.py:290
  120.6 15.6 %copy-start.8 = (f32[312,128]{1,0:T(8,128)}, f32[312,128]{1,0:T(8,128)S(1)}, u32[]{:S(2)}) copy-start(f32[312,128]{1,0:T(8,128)S(1)} %collective-permute-done.6.refs_6_) | copy-start | bytes 479236
  120.6 6.0 %collective-permute-start.1 = (f32[312,128]{1,0:T(8,128)S(1)}, f32[312,128]{1,0:T(8,128)S(1)}, u32[]{:S(2)}, u32[]{:S(2)}) collective-permute-start(f32[312,128]{1,0:T(8,128)S(1)} %select_maximum_fusion.refs_0_), channel_id=1, source_target_pairs={{0,2},{1,3},{2,0},{3,1},{4,6},{5,7},{6,4},{7,5},{8,10},{9,11},{10,... | collective-permute-start | bytes 479240 | tf_op jit(solution)/shard_map/ppermute | solution.py:290
  121.3 14.9 %copy-start.9 = (f32[312,128]{1,0:T(8,128)}, f32[312,128]{1,0:T(8,128)S(1)}, u32[]{:S(2)}) copy-start(f32[312,128]{1,0:T(8,128)S(1)} %collective-permute-done.5.refs_5_) | copy-start | bytes 479236
  121.3 14.9 %copy-start.10 = (f32[312,128]{1,0:T(8,128)}, f32[312,128]{1,0:T(8,128)S(1)}, u32[]{:S(2)}) copy-start(f32[312,128]{1,0:T(8,128)S(1)} %collective-permute-done.4.refs_4_) | copy-start | bytes 479236
  126.7 1.3 collective-permute-start.10
  128.1 7.8 %collective-permute-start.11 = (f32[312,128]{1,0:T(8,128)S(1)}, f32[312,128]{1,0:T(8,128)S(1)}, u32[]{:S(2)}, u32[]{:S(2)}) collective-permute-start(f32[312,128]{1,0:T(8,128)S(1)} %pad_maximum_fusion), channel_id=1, source_target_pairs={{0,16},{16,0},{32,48},{48,32},{64,80},{80,64},{96,112},{112,96},{1... | collective-permute-start | bytes 479240 | tf_op jit(solution)/shard_map/ppermute | solution.py:290
  129.1 7.1 %collective-permute-start = (f32[200,512]{1,0:T(8,128)S(1)}, f32[200,512]{1,0:T(8,128)S(1)}, u32[]{:S(2)}, u32[]{:S(2)}) collective-permute-start(f32[200,512]{1,0:T(8,128)S(1)} %copy-done.1), channel_id=1, source_target_pairs={{0,1},{1,0},{2,3},{3,2},{4,5},{5,4},{6,7},{7,6},{8,9},{9,8},{10,11... | collective-permute-start | bytes 1228808 | tf_op jit(solution)/shard_map/ppermute | solution.py:290
  135.9 7.5 %collective-permute-start.12 = (f32[312,128]{1,0:T(8,128)S(1)}, f32[312,128]{1,0:T(8,128)S(1)}, u32[]{:S(2)}, u32[]{:S(2)}) collective-permute-start(f32[312,128]{1,0:T(8,128)S(1)} %fusion.14), channel_id=1, source_target_pairs={{0,32},{16,48},{32,0},{48,16},{64,96},{80,112},{96,64},{112,80},{1... | collective-permute-start | bytes 479240 | tf_op jit(solution)/shard_map/ppermute | solution.py:290
  143.4 1.2 collective-permute-start.8
  143.5 7.8 %collective-permute-start.13 = (f32[312,128]{1,0:T(8,128)S(1)}, f32[312,128]{1,0:T(8,128)S(1)}, u32[]{:S(2)}, u32[]{:S(2)}) collective-permute-start(f32[312,128]{1,0:T(8,128)S(1)} %add.102), channel_id=1, source_target_pairs={{0,96},{16,112},{32,64},{48,80},{64,32},{80,48},{96,0},{112,16},{1... | collective-permute-start | bytes 479240 | tf_op jit(solution)/shard_map/ppermute | solution.py:290
  (10 other events, 85.7 us)

commit v4 on v3

--- a/solution.py
+++ b/solution.py
@@ -108,6 +108,8 @@
 
 TILE = 256
 TILES = KIDS * HANDS // TILE
+EARLY = 16
+AHEAD = 6
 
 
 def place_columns(o, recv_ref, place_ref, cols_ref):
@@ -152,13 +154,20 @@
             following += [jnp.where(spill, out[g], merged[g]) for g in range(7)]
         return tuple(following)
 
-    lax.fori_loop(0, DEVICES, place, (zero,) * 14, unroll=4)
-
-
-def member_kernel(scalar_ref, recv_ref, place_ref, table_ref, assign_ref,
-                  hist_ref, keep_ref, send_ref, cols_ref, even_ref, odd_ref):
+    return place, (zero,) * 14
+
+
+def member_kernel(scalar_ref, arrived_ref, place_ref, table_ref, assign_ref,
+                  hist_ref, keep_ref, send_ref, cols_ref, even_ref, odd_ref, recv_ref, sems):
     core = scalar_ref[1]
-    place_columns(scalar_ref[0], recv_ref, place_ref, cols_ref)
+
+    def load(at):
+        span = (pl.ds(0, EARLY), pl.ds(EARLY, DEVICES - EARLY))[at]
+        return pltpu.make_async_copy(arrived_ref.at[span], recv_ref.at[span], sems.at[at])
+
+    load(0).start()
+    load(1).start()
+    place, carry = place_columns(scalar_ref[0], recv_ref, place_ref, cols_ref)
 
     def products(i, out_ref):
         h = jnp.concatenate([cols_ref[2 * i], cols_ref[2 * i + 1]], axis=1)
@@ -178,16 +187,29 @@
             hist_ref[:, at] += (w * scale[None]).reshape(200, LANES)
 
     hist_ref[...] = jnp.zeros_like(hist_ref)
+    load(0).wait()
+    carry = lax.fori_loop(0, AHEAD, place, carry, unroll=3)
     products(0, even_ref)
 
     def two_kids(j, carry):
+        def some(at, carry):
+            for k in range(AHEAD // 2):
+                carry = place(jnp.minimum(AHEAD * (j + 1) + at + k, DEVICES - 1), carry)
+            return carry
+
+        @pl.when(j == 1)
+        def _():
+            load(1).wait()
+
         products(2 * j + 1, odd_ref)
+        carry = some(0, carry)
         add_kid(even_ref)
         products(2 * j + 2, even_ref)
+        carry = some(AHEAD // 2, carry)
         add_kid(odd_ref)
         return carry
 
-    lax.fori_loop(0, KIDS // 2, two_kids, 0)
+    lax.fori_loop(0, KIDS // 2, two_kids, carry)
     add_kid(even_ref)
 
     hi = hist_ref[...].astype(bf16)
@@ -214,7 +236,7 @@
 def member(scalars, recv, place, table, assign):
     return pl.pallas_call(
         member_kernel,
-        in_specs=[SMEM, VMEM, VMEM, VMEM, VMEM],
+        in_specs=[SMEM, pl.BlockSpec(memory_space=pl.ANY), VMEM, VMEM, VMEM],
         out_specs=[VMEM, VMEM, VMEM],
         out_shape=[
             jax.ShapeDtypeStruct((TURN_CENT, HANDS), f32),
@@ -225,6 +247,8 @@
             pltpu.VMEM((TILES, 64, TILE), bf16),
             pltpu.VMEM((264, HANDS), f32),
             pltpu.VMEM((264, HANDS), f32),
+            pltpu.VMEM((DEVICES, PACK_ROWS, LANES), bf16),
+            pltpu.SemaphoreType.DMA((2,)),
         ],
         name="member",
     )(scalars, recv, place, table, assign)
@@ -311,10 +335,10 @@
 
     flop_hist, keep, send = member(scalars, arrived, place, table, flop_assign[None, :])
 
-    partner = swap(flop_hist, "cent", 1)
     turn_part = sum((piece[TURN_CENT:] for piece in pieces[1:]), turn_part)
     turn_part = turn_part + swap(turn_part, "cent", 1)
-    half = keep + swap(send, "cent", 1)
+    received, partner = lax.optimization_barrier((swap(send, "cent", 1), swap(flop_hist, "cent", 1)))
+    half = keep + received
     parts = lax.all_to_all(half, "cent", split_axis=0, concat_axis=0, tiled=True, axis_index_groups=CHIPS)
     total = jnp.concatenate([jnp.sum(parts, axis=0), turn_part], axis=0)
     for mask in (1, 2, 6):

time: 154 us -> 148 us (0.961)
  Pallas kernels: 44.5 us -> 40 us
    pallas_call x1, Pallas kernels: 22.2 us -> 17.7 us  [member(): pl.pallas_call(member_kernel, in_specs=[SMEM, pl.BlockSpec(memory_space=p...]
where the time goes in v4:
time: 148 us; the launch traced here: 147 us
  waiting for transfers between devices  69 us (47%)
  Pallas kernels  40 us (27%)
  starting transfers between devices  26.8 us (18%)
  other arithmetic  5.26 us (4%)
  local copies, waits for them, and re-layouts  4.48 us (3%)
    ppermute x14, waiting for transfers between devices, swap(): return lax.ppermute(x, axis, [(i, i ^ mask) for i in range(size)])  36.8 us
    all_to_all x1, waiting for transfers between devices, body(): lax.all_to_all(sent, ('board', 'cent'), split_axis=0, concat_axis=0, tile...  32.2 us
    pallas_call x1, Pallas kernels, member(): pl.pallas_call(member_kernel, in_specs=[SMEM, pl.BlockSpec(memory_space=p...  17.7 us
    pallas_call x1, Pallas kernels, turn_partial(): pl.pallas_call(turn_kernel, grid=(steps,), in_specs=[pl.BlockSpec((BINS,...  12.2 us
    ppermute x14, starting transfers between devices, swap(): return lax.ppermute(x, axis, [(i, i ^ mask) for i in range(size)])  12.1 us
    all_to_all x1, starting transfers between devices, body(): lax.all_to_all(sent, ('board', 'cent'), split_axis=0, concat_axis=0, tile...  11.2 us
    pallas_call x1, Pallas kernels, nearest_of(): pl.pallas_call(nearest_kernel, in_specs=[VMEM] * (2 + len(pieces)), out_s...  5.67 us
    pallas_call x1, Pallas kernels, pack(): pl.pallas_call(pack_kernel, grid=(DEVICES // SOURCES_PER_STEP,), in_specs...  4.37 us
  transfers between devices with their start and end apart: 16, of which 9 were waited for; matrix products, arithmetic and copies ran while one was open for 4% of the time, Pallas kernels for 12%

profile of v4, /device:TPU:0, one launch (start us, length us, event | category | flops | bytes accessed | tf_op | source)
XLA Modules:
  0.0 147.3 jit_solution(12363137349138008729)
XLA Ops:
  0.6 4.4 %pack.1 = bf16[128,80,128]{2,1,0:T(8,128)(2,1)} custom-call(bf16[50,24064]{1,0:T(8,128)(2,1)} %hist_ref.3), custom_call_target="tpu_custom_call" | custom-call | tf_op jit(solution)/shard_map/pack/pallas_call | solution.py:65
  5.0 11.2 %all-to-all-start = ((bf16[128,80,128]{2,1,0:T(8,128)(2,1)}), bf16[128,80,128]{2,1,0:T(8,128)(2,1)S(1)}, u32[]{:S(2)}, u32[]{:S(2)}) async-start(bf16[128,80,128]{2,1,0:T(8,128)(2,1)} %pack.1), calls=%async_computation | async-start | bytes 5242880 | tf_op jit(solution)/shard_map/all_to_all | solution.py:320
  20.0 32.2 %all-to-all-done.arrived_ref = bf16[128,80,128]{2,1,0:T(8,128)(2,1)S(1)} async-done(((bf16[128,80,128]{2,1,0:T(8,128)(2,1)}), bf16[128,80,128]{2,1,0:T(8,128)(2,1)S(1)}, u32[]{:S(2)}, u32[]{:S(2)}) %all-to-all-start) | async-done | bytes 2621472 | tf_op jit(solution)/shard_map/all_to_all | solution.py:320
  52.2 1.5 %copy-done = bf16[128,80,128]{2,1,0:T(8,128)(2,1)} copy-done((bf16[128,80,128]{2,1,0:T(8,128)(2,1)}, bf16[128,80,128]{2,1,0:T(8,128)(2,1)S(1)}, u32[]{:S(2)}) %copy-start) | copy-done | bytes 2621464
  53.7 17.7 %member.1 = (f32[200,512]{1,0:T(8,128)}, f32[8,200,128]{2,1,0:T(8,128)}, f32[8,200,128]{2,1,0:T(8,128)}) custom-call(s32[2]{0:T(128)} %pad_add_fusion.scalar_ref, bf16[128,80,128]{2,1,0:T(8,128)(2,1)} %copy-done, s32[96,256]{1,0:T(8,128)} %concatenate.29.place_ref, bf16[264,192]{1,0:T(8,128)(2,1)} %pad_maximum_fusion.1.table_ref, s32[1,512]{1,0:T(1,128)} %bitcast.8), custom_call_target="tpu_custom_call" | custom-call | tf_op jit(solution)/shard_map/member/pallas_call | solution.py:237
  72.0 0.7 broadcast_in_dim.28.label_ref
  72.7 12.2 %turn_sums.1 = f32[112,128]{1,0:T(8,128)} custom-call(bf16[50,24064]{1,0:T(8,128)(2,1)} %hist_ref.3, s32[1,24064]{1,0:T(1,128)} %broadcast_in_dim.28.label_ref), custom_call_target="tpu_custom_call" | custom-call | tf_op jit(solution)/shard_map/turn_sums/pallas_call | solution.py:99
  85.0 1.0 add.92
  86.0 3.5 %all-to-all-start.1 = ((f32[8,200,128]{2,1,0:T(8,128)}), f32[8,200,128]{2,1,0:T(8,128)S(1)}, u32[]{:S(2)}, u32[]{:S(2)}) async-start(f32[8,200,128]{2,1,0:T(8,128)} %add.92), calls=%async_computation.1 | async-start | bytes 1638400 | tf_op jit(solution)/shard_map/all_to_all | solution.py:342
  89.6 4.1 %collective-permute-start.8 = (f32[312,128]{1,0:T(8,128)S(1)}, f32[312,128]{1,0:T(8,128)S(1)}, u32[]{:S(2)}, u32[]{:S(2)}) collective-permute-start(f32[312,128]{1,0:T(8,128)S(1)} %select_maximum_fusion.refs_0_), channel_id=1, source_target_pairs={{0,14},{1,15},{2,12},{3,13},{4,10},{5,11},{6,8},{7,9},{8,6},{9,7},... | collective-permute-start | bytes 479240 | tf_op jit(solution)/shard_map/ppermute | solution.py:314
  94.3 1.8 %collective-permute-start.6 = (f32[312,128]{1,0:T(8,128)S(1)}, f32[312,128]{1,0:T(8,128)S(1)}, u32[]{:S(2)}, u32[]{:S(2)}) collective-permute-start(f32[312,128]{1,0:T(8,128)S(1)} %select_maximum_fusion.refs_0_), channel_id=1, source_target_pairs={{0,10},{1,11},{2,8},{3,9},{4,14},{5,15},{6,12},{7,13},{8,2},{9,3},... | collective-permute-start | bytes 479240 | tf_op jit(solution)/shard_map/ppermute | solution.py:314
  96.0 1.3 collective-permute-start.5
  97.4 1.6 %collective-permute-start.4 = (f32[312,128]{1,0:T(8,128)S(1)}, f32[312,128]{1,0:T(8,128)S(1)}, u32[]{:S(2)}, u32[]{:S(2)}) collective-permute-start(f32[312,128]{1,0:T(8,128)S(1)} %select_maximum_fusion.refs_0_), channel_id=1, source_target_pairs={{0,6},{1,7},{2,4},{3,5},{4,2},{5,3},{6,0},{7,1},{8,14},{9,15},{10,... | collective-permute-start | bytes 479240 | tf_op jit(solution)/shard_map/ppermute | solution.py:314
  99.0 11.9 %collective-permute-done.8.refs_7_ = f32[312,128]{1,0:T(8,128)S(1)} collective-permute-done((f32[312,128]{1,0:T(8,128)S(1)}, f32[312,128]{1,0:T(8,128)S(1)}, u32[]{:S(2)}, u32[]{:S(2)}) %collective-permute-start.8) | collective-permute-done | bytes 159776 | tf_op jit(solution)/shard_map/ppermute | solution.py:314
  110.8 5.3 %collective-permute-done.7.refs_6_ = f32[312,128]{1,0:T(8,128)S(1)} collective-permute-done((f32[312,128]{1,0:T(8,128)S(1)}, f32[312,128]{1,0:T(8,128)S(1)}, u32[]{:S(2)}, u32[]{:S(2)}) %collective-permute-start.7) | collective-permute-done | bytes 159776 | tf_op jit(solution)/shard_map/ppermute | solution.py:314
  116.4 1.7 %collective-permute-done.3.refs_2_ = f32[312,128]{1,0:T(8,128)S(1)} collective-permute-done((f32[312,128]{1,0:T(8,128)S(1)}, f32[312,128]{1,0:T(8,128)S(1)}, u32[]{:S(2)}, u32[]{:S(2)}) %collective-permute-start.3) | collective-permute-done | bytes 159776 | tf_op jit(solution)/shard_map/ppermute | solution.py:314
  118.1 4.0 %collective-permute-done.2.refs_1_ = f32[312,128]{1,0:T(8,128)S(1)} collective-permute-done((f32[312,128]{1,0:T(8,128)S(1)}, f32[312,128]{1,0:T(8,128)S(1)}, u32[]{:S(2)}, u32[]{:S(2)}) %collective-permute-start.2) | collective-permute-done | bytes 159776 | tf_op jit(solution)/shard_map/ppermute | solution.py:314
  122.3 1.2 collective-permute-done.10
  123.6 0.7 collective-permute-start.11
  124.3 7.1 %collective-permute-done.11 = f32[312,128]{1,0:T(8,128)S(1)} collective-permute-done((f32[312,128]{1,0:T(8,128)S(1)}, f32[312,128]{1,0:T(8,128)S(1)}, u32[]{:S(2)}, u32[]{:S(2)}) %collective-permute-start.11) | collective-permute-done | bytes 159776 | tf_op jit(solution)/shard_map/ppermute | solution.py:314
  131.7 5.7 %nearest.1 = f32[1,1024]{1,0:T(1,128)} custom-call(f32[200,512]{1,0:T(8,128)} %get-tuple-element.17.mine_ref, f32[200,512]{1,0:T(8,128)} %copy-done.5, f32[312,128]{1,0:T(8,128)} %copy-done.3, f32[312,128]{1,0:T(8,128)} %copy-done.12, f32[312,128]{1,0:T(8,128)} %copy-done.11, f32[312,128]{1,0:T(8,128)} %copy-done.10, f32[312,128]{1,0:T(8,128)} %copy-done.9, ...), custom_call_target="tpu_custom_call" | custom-call | tf_op jit(solution)/shard_map/nearest/pallas_call | solution.py:275
  138.2 0.9 collective-permute-start.13
  139.2 0.7 slice_minimum_fusion
  140.5 5.5 %collective-permute-done.13 = f32[312,128]{1,0:T(8,128)S(1)} collective-permute-done((f32[312,128]{1,0:T(8,128)S(1)}, f32[312,128]{1,0:T(8,128)S(1)}, u32[]{:S(2)}, u32[]{:S(2)}) %collective-permute-start.13) | collective-permute-done | bytes 159776 | tf_op jit(solution)/shard_map/ppermute | solution.py:314
  (90 shorter events, 8.3 us)
Async XLA Ops:
  5.0 47.2 %all-to-all-start = ((bf16[128,80,128]{2,1,0:T(8,128)(2,1)}), bf16[128,80,128]{2,1,0:T(8,128)(2,1)S(1)}, u32[]{:S(2)}, u32[]{:S(2)}) async-start(bf16[128,80,128]{2,1,0:T(8,128)(2,1)} %pack.1), calls=%async_computation | async-start | bytes 5242880 | tf_op jit(solution)/shard_map/all_to_all | solution.py:320
  17.3 54.6 %copy-start.15 = (s32[24064]{0:T(1024)S(1)}, s32[24064]{0:T(1024)}, u32[]{:S(2)}) copy-start(s32[24064]{0:T(1024)} %param.7) | copy-start | bytes 288772
  71.4 13.6 %collective-permute-start = (f32[8,200,128]{2,1,0:T(8,128)}, f32[8,200,128]{2,1,0:T(8,128)S(1)}, u32[]{:S(2)}, u32[]{:S(2)}) collective-permute-start(f32[8,200,128]{2,1,0:T(8,128)} %get-tuple-element.18), channel_id=1, source_target_pairs={{0,1},{1,0},{2,3},{3,2},{4,5},{5,4},{6,7},{7,6},{8,9},{9,8},{10,11... | collective-permute-start | bytes 2457608 | tf_op jit(solution)/shard_map/ppermute | solution.py:314
  71.5 13.5 %collective-permute-start.1 = (f32[200,512]{1,0:T(8,128)}, f32[200,512]{1,0:T(8,128)S(1)}, u32[]{:S(2)}, u32[]{:S(2)}) collective-permute-start(f32[200,512]{1,0:T(8,128)} %get-tuple-element.17.mine_ref), channel_id=1, source_target_pairs={{0,1},{1,0},{2,3},{3,2},{4,5},{5,4},{6,7},{7,6},{8,9},{9,8},{10,11... | collective-permute-start | bytes 1228808 | tf_op jit(solution)/shard_map/ppermute | solution.py:314
  84.9 38.6 %copy-start.5 = (f32[200,512]{1,0:T(8,128)}, f32[200,512]{1,0:T(8,128)S(1)}, u32[]{:S(2)}) copy-start(f32[200,512]{1,0:T(8,128)S(1)} %collective-permute-done.1.partner_ref) | copy-start | bytes 1228804
  86.0 37.5 %all-to-all-start.1 = ((f32[8,200,128]{2,1,0:T(8,128)}), f32[8,200,128]{2,1,0:T(8,128)S(1)}, u32[]{:S(2)}, u32[]{:S(2)}) async-start(f32[8,200,128]{2,1,0:T(8,128)} %add.92), calls=%async_computation.1 | async-start | bytes 1638400 | tf_op jit(solution)/shard_map/all_to_all | solution.py:342
  89.6 48.5 %copy-start.1 = (f32[200,512]{1,0:T(8,128)S(1)}, f32[200,512]{1,0:T(8,128)}, u32[]{:S(2)}) copy-start(f32[200,512]{1,0:T(8,128)} %get-tuple-element.17.mine_ref) | copy-start | bytes 1228804
  89.6 42.0 %copy-start.3 = (f32[312,128]{1,0:T(8,128)}, f32[312,128]{1,0:T(8,128)S(1)}, u32[]{:S(2)}) copy-start(f32[312,128]{1,0:T(8,128)S(1)} %select_maximum_fusion.refs_0_) | copy-start | bytes 479236
  89.6 21.2 %collective-permute-start.8 = (f32[312,128]{1,0:T(8,128)S(1)}, f32[312,128]{1,0:T(8,128)S(1)}, u32[]{:S(2)}, u32[]{:S(2)}) collective-permute-start(f32[312,128]{1,0:T(8,128)S(1)} %select_maximum_fusion.refs_0_), channel_id=1, source_target_pairs={{0,14},{1,15},{2,12},{3,13},{4,10},{5,11},{6,8},{7,9},{8,6},{9,7},... | collective-permute-start | bytes 479240 | tf_op jit(solution)/shard_map/ppermute | solution.py:314
  93.7 22.4 %collective-permute-start.7 = (f32[312,128]{1,0:T(8,128)S(1)}, f32[312,128]{1,0:T(8,128)S(1)}, u32[]{:S(2)}, u32[]{:S(2)}) collective-permute-start(f32[312,128]{1,0:T(8,128)S(1)} %select_maximum_fusion.refs_0_), channel_id=1, source_target_pairs={{0,12},{1,13},{2,14},{3,15},{4,8},{5,9},{6,10},{7,11},{8,4},{9,5},... | collective-permute-start | bytes 479240 | tf_op jit(solution)/shard_map/ppermute | solution.py:314
  94.3 22.1 %collective-permute-start.6 = (f32[312,128]{1,0:T(8,128)S(1)}, f32[312,128]{1,0:T(8,128)S(1)}, u32[]{:S(2)}, u32[]{:S(2)}) collective-permute-start(f32[312,128]{1,0:T(8,128)S(1)} %select_maximum_fusion.refs_0_), channel_id=1, source_target_pairs={{0,10},{1,11},{2,8},{3,9},{4,14},{5,15},{6,12},{7,13},{8,2},{9,3},... | collective-permute-start | bytes 479240 | tf_op jit(solution)/shard_map/ppermute | solution.py:314
  96.0 20.3 %collective-permute-start.5 = (f32[312,128]{1,0:T(8,128)S(1)}, f32[312,128]{1,0:T(8,128)S(1)}, u32[]{:S(2)}, u32[]{:S(2)}) collective-permute-start(f32[312,128]{1,0:T(8,128)S(1)} %select_maximum_fusion.refs_0_), channel_id=1, source_target_pairs={{0,8},{1,9},{2,10},{3,11},{4,12},{5,13},{6,14},{7,15},{8,0},{9,1},... | collective-permute-start | bytes 479240 | tf_op jit(solution)/shard_map/ppermute | solution.py:314
  97.4 19.0 %collective-permute-start.4 = (f32[312,128]{1,0:T(8,128)S(1)}, f32[312,128]{1,0:T(8,128)S(1)}, u32[]{:S(2)}, u32[]{:S(2)}) collective-permute-start(f32[312,128]{1,0:T(8,128)S(1)} %select_maximum_fusion.refs_0_), channel_id=1, source_target_pairs={{0,6},{1,7},{2,4},{3,5},{4,2},{5,3},{6,0},{7,1},{8,14},{9,15},{10,... | collective-permute-start | bytes 479240 | tf_op jit(solution)/shard_map/ppermute | solution.py:314
  110.8 20.8 %copy-start.6 = (f32[312,128]{1,0:T(8,128)}, f32[312,128]{1,0:T(8,128)S(1)}, u32[]{:S(2)}) copy-start(f32[312,128]{1,0:T(8,128)S(1)} %collective-permute-done.8.refs_7_) | copy-start | bytes 479236
  110.8 7.3 %collective-permute-start.3 = (f32[312,128]{1,0:T(8,128)S(1)}, f32[312,128]{1,0:T(8,128)S(1)}, u32[]{:S(2)}, u32[]{:S(2)}) collective-permute-start(f32[312,128]{1,0:T(8,128)S(1)} %select_maximum_fusion.refs_0_), channel_id=1, source_target_pairs={{0,4},{1,5},{2,6},{3,7},{4,0},{5,1},{6,2},{7,3},{8,12},{9,13},{10,... | collective-permute-start | bytes 479240 | tf_op jit(solution)/shard_map/ppermute | solution.py:314
  116.2 15.5 %copy-start.7 = (f32[312,128]{1,0:T(8,128)}, f32[312,128]{1,0:T(8,128)S(1)}, u32[]{:S(2)}) copy-start(f32[312,128]{1,0:T(8,128)S(1)} %collective-permute-done.7.refs_6_) | copy-start | bytes 479236
  116.2 6.0 %collective-permute-start.2 = (f32[312,128]{1,0:T(8,128)S(1)}, f32[312,128]{1,0:T(8,128)S(1)}, u32[]{:S(2)}, u32[]{:S(2)}) collective-permute-start(f32[312,128]{1,0:T(8,128)S(1)} %select_maximum_fusion.refs_0_), channel_id=1, source_target_pairs={{0,2},{1,3},{2,0},{3,1},{4,6},{5,7},{6,4},{7,5},{8,10},{9,11},{10,... | collective-permute-start | bytes 479240 | tf_op jit(solution)/shard_map/ppermute | solution.py:314
  116.3 15.3 %copy-start.8 = (f32[312,128]{1,0:T(8,128)}, f32[312,128]{1,0:T(8,128)S(1)}, u32[]{:S(2)}) copy-start(f32[312,128]{1,0:T(8,128)S(1)} %collective-permute-done.6.refs_5_) | copy-start | bytes 479236
  116.3 15.3 %copy-start.9 = (f32[312,128]{1,0:T(8,128)}, f32[312,128]{1,0:T(8,128)S(1)}, u32[]{:S(2)}) copy-start(f32[312,128]{1,0:T(8,128)S(1)} %collective-permute-done.5.refs_4_) | copy-start | bytes 479236
  122.2 1.3 collective-permute-start.10
  123.6 7.8 %collective-permute-start.11 = (f32[312,128]{1,0:T(8,128)S(1)}, f32[312,128]{1,0:T(8,128)S(1)}, u32[]{:S(2)}, u32[]{:S(2)}) collective-permute-start(f32[312,128]{1,0:T(8,128)S(1)} %pad_maximum_fusion), channel_id=1, source_target_pairs={{0,16},{16,0},{32,48},{48,32},{64,80},{80,64},{96,112},{112,96},{1... | collective-permute-start | bytes 479240 | tf_op jit(solution)/shard_map/ppermute | solution.py:314
  131.4 6.8 %collective-permute-start.12 = (f32[312,128]{1,0:T(8,128)S(1)}, f32[312,128]{1,0:T(8,128)S(1)}, u32[]{:S(2)}, u32[]{:S(2)}) collective-permute-start(f32[312,128]{1,0:T(8,128)S(1)} %fusion.14), channel_id=1, source_target_pairs={{0,32},{16,48},{32,0},{48,16},{64,96},{80,112},{96,64},{112,80},{1... | collective-permute-start | bytes 479240 | tf_op jit(solution)/shard_map/ppermute | solution.py:314
  138.1 1.2 collective-permute-start.9
  138.2 7.8 %collective-permute-start.13 = (f32[312,128]{1,0:T(8,128)S(1)}, f32[312,128]{1,0:T(8,128)S(1)}, u32[]{:S(2)}, u32[]{:S(2)}) collective-permute-start(f32[312,128]{1,0:T(8,128)S(1)} %add.102), channel_id=1, source_target_pairs={{0,96},{16,112},{32,64},{48,80},{64,32},{80,48},{96,0},{112,16},{1... | collective-permute-start | bytes 479240 | tf_op jit(solution)/shard_map/ppermute | solution.py:314
  (9 other events, 85.9 us)

commit v5 on v4

--- a/solution.py
+++ b/solution.py
@@ -108,7 +108,6 @@
 
 TILE = 256
 TILES = KIDS * HANDS // TILE
-EARLY = 16
 AHEAD = 6
 
 
@@ -157,16 +156,9 @@
     return place, (zero,) * 14
 
 
-def member_kernel(scalar_ref, arrived_ref, place_ref, table_ref, assign_ref,
-                  hist_ref, keep_ref, send_ref, cols_ref, even_ref, odd_ref, recv_ref, sems):
+def member_kernel(scalar_ref, recv_ref, place_ref, table_ref, assign_ref,
+                  hist_ref, keep_ref, send_ref, cols_ref, even_ref, odd_ref):
     core = scalar_ref[1]
-
-    def load(at):
-        span = (pl.ds(0, EARLY), pl.ds(EARLY, DEVICES - EARLY))[at]
-        return pltpu.make_async_copy(arrived_ref.at[span], recv_ref.at[span], sems.at[at])
-
-    load(0).start()
-    load(1).start()
     place, carry = place_columns(scalar_ref[0], recv_ref, place_ref, cols_ref)
 
     def products(i, out_ref):
@@ -187,7 +179,6 @@
             hist_ref[:, at] += (w * scale[None]).reshape(200, LANES)
 
     hist_ref[...] = jnp.zeros_like(hist_ref)
-    load(0).wait()
     carry = lax.fori_loop(0, AHEAD, place, carry, unroll=3)
     products(0, even_ref)
 
@@ -196,10 +187,6 @@
             for k in range(AHEAD // 2):
                 carry = place(jnp.minimum(AHEAD * (j + 1) + at + k, DEVICES - 1), carry)
             return carry
-
-        @pl.when(j == 1)
-        def _():
-            load(1).wait()
 
         products(2 * j + 1, odd_ref)
         carry = some(0, carry)
@@ -236,7 +223,7 @@
 def member(scalars, recv, place, table, assign):
     return pl.pallas_call(
         member_kernel,
-        in_specs=[SMEM, pl.BlockSpec(memory_space=pl.ANY), VMEM, VMEM, VMEM],
+        in_specs=[SMEM, VMEM, VMEM, VMEM, VMEM],
         out_specs=[VMEM, VMEM, VMEM],
         out_shape=[
             jax.ShapeDtypeStruct((TURN_CENT, HANDS), f32),
@@ -247,9 +234,8 @@
             pltpu.VMEM((TILES, 64, TILE), bf16),
             pltpu.VMEM((264, HANDS), f32),
             pltpu.VMEM((264, HANDS), f32),
-            pltpu.VMEM((DEVICES, PACK_ROWS, LANES), bf16),
-            pltpu.SemaphoreType.DMA((2,)),
         ],
+        compiler_params=pltpu.CompilerParams(vmem_limit_bytes=24 * 1024 * 1024),
         name="member",
     )(scalars, recv, place, table, assign)
 
@@ -277,6 +263,7 @@
         in_specs=[VMEM] * (2 + len(pieces)),
         out_specs=VMEM,
         out_shape=jax.ShapeDtypeStruct((1, 2 * HANDS), f32),
+    compiler_params=pltpu.CompilerParams(vmem_limit_bytes=24 * 1024 * 1024),
         name="nearest",
     )(flop_hist, partner, *pieces)
     best = jnp.minimum(best[:, :HANDS], swap(best[:, HANDS:], "cent", 1))
@@ -337,12 +324,14 @@
 
     turn_part = sum((piece[TURN_CENT:] for piece in pieces[1:]), turn_part)
     turn_part = turn_part + swap(turn_part, "cent", 1)
+    turn_part = turn_part + swap(turn_part, "board", 1)
     received, partner = lax.optimization_barrier((swap(send, "cent", 1), swap(flop_hist, "cent", 1)))
     half = keep + received
     parts = lax.all_to_all(half, "cent", split_axis=0, concat_axis=0, tiled=True, axis_index_groups=CHIPS)
-    total = jnp.concatenate([jnp.sum(parts, axis=0), turn_part], axis=0)
-    for mask in (1, 2, 6):
-        total = total + swap(total, "board", mask)
+    flop_part = jnp.sum(parts, axis=0)
+    flop_part = flop_part + swap(flop_part, "board", 1)
+    total = jnp.concatenate([flop_part, turn_part], axis=0)
+    total = (total + swap(total, "board", 2)) + (swap(total, "board", 4) + swap(total, "board", 6))
     flop_sums = total[:TURN_CENT, :PANEL].T * (PANEL * 16 / (HANDS * DEVICES))
     turn_low = total[TURN_CENT:TURN_CENT + BINS]
     turn_high = total[TURN_CENT + TURN_SPLIT:TURN_CENT + TURN_SPLIT + BINS, :TURN_CENT - LANES]

time: 148 us -> 145 us (0.980)
  Pallas kernels: 40 us -> 36.3 us
  starting transfers between devices: 26.8 us -> 30.4 us
  local copies, waits for them, and re-layouts: 4.48 us -> 2.57 us
  other arithmetic: 5.26 us -> 3.42 us
    ppermute x14 -> x16, starting transfers between devices: 12.1 us -> 15.7 us  [swap(): return lax.ppermute(x, axis, [(i, i ^ mask) for i in range(size)])]
    pallas_call x1, Pallas kernels: 5.67 us -> 3.57 us  [nearest_of(): pl.pallas_call(nearest_kernel, in_specs=[VMEM] * (2 + len(pieces)), out_s...]
    all_to_all x1, waiting for transfers between devices: 32.2 us -> 33.9 us  [body(): lax.all_to_all(sent, ('board', 'cent'), split_axis=0, concat_axis=0, tile...]
    pallas_call x1, Pallas kernels: 17.7 us -> 16.1 us  [member(): pl.pallas_call(member_kernel, in_specs=[SMEM, VMEM, VMEM, VMEM, VMEM], ou...]
    ppermute x14 -> x16, waiting for transfers between devices: 36.8 us -> 36.3 us  [swap(): return lax.ppermute(x, axis, [(i, i ^ mask) for i in range(size)])]
  transfers between devices with their start and end apart: 16 -> 18, of which waited for: 9 -> 11; matrix products, arithmetic and copies ran while one was open for 4% -> 2% of each run, Pallas kernels for 12% -> 11%
where the time goes in v5:
time: 145 us
  waiting for transfers between devices  70.2 us (48%)
  Pallas kernels  36.3 us (25%)
  starting transfers between devices  30.4 us (21%)
  other arithmetic  3.42 us (2%)
  local copies, waits for them, and re-layouts  2.57 us (2%)
    ppermute x16, waiting for transfers between devices, swap(): return lax.ppermute(x, axis, [(i, i ^ mask) for i in range(size)])  36.3 us
    all_to_all x1, waiting for transfers between devices, body(): lax.all_to_all(sent, ('board', 'cent'), split_axis=0, concat_axis=0, tile...  33.9 us
    pallas_call x1, Pallas kernels, member(): pl.pallas_call(member_kernel, in_specs=[SMEM, VMEM, VMEM, VMEM, VMEM], ou...  16.1 us
    ppermute x16, starting transfers between devices, swap(): return lax.ppermute(x, axis, [(i, i ^ mask) for i in range(size)])  15.7 us
    pallas_call x1, Pallas kernels, turn_partial(): pl.pallas_call(turn_kernel, grid=(steps,), in_specs=[pl.BlockSpec((BINS,...  12.2 us
    all_to_all x1, starting transfers between devices, body(): lax.all_to_all(sent, ('board', 'cent'), split_axis=0, concat_axis=0, tile...  11.2 us
    pallas_call x1, Pallas kernels, pack(): pl.pallas_call(pack_kernel, grid=(DEVICES // SOURCES_PER_STEP,), in_specs...  4.37 us
    pallas_call x1, Pallas kernels, nearest_of(): pl.pallas_call(nearest_kernel, in_specs=[VMEM] * (2 + len(pieces)), out_s...  3.57 us
  transfers between devices with their start and end apart: 18, of which 11 were waited for; matrix products, arithmetic and copies ran while one was open for 2% of the time, Pallas kernels for 11%

profile of v5, /device:TPU:0, one launch (start us, length us, event | category | flops | bytes accessed | tf_op | source)
XLA Modules:
  0.0 144.6 jit_solution(3214035771019686103)
XLA Ops:
  0.6 4.4 %pack.1 = bf16[128,80,128]{2,1,0:T(8,128)(2,1)} custom-call(bf16[50,24064]{1,0:T(8,128)(2,1)} %hist_ref.3), custom_call_target="tpu_custom_call" | custom-call | tf_op jit(solution)/shard_map/pack/pallas_call | solution.py:65
  5.0 11.2 %all-to-all-start = ((bf16[128,80,128]{2,1,0:T(8,128)(2,1)}), bf16[128,80,128]{2,1,0:T(8,128)(2,1)S(1)}, u32[]{:S(2)}, u32[]{:S(2)}) async-start(bf16[128,80,128]{2,1,0:T(8,128)(2,1)} %pack.1), calls=%async_computation | async-start | bytes 5242880 | tf_op jit(solution)/shard_map/all_to_all | solution.py:307
  18.3 33.9 %all-to-all-done.recv_ref = bf16[128,80,128]{2,1,0:T(8,128)(2,1)S(1)} async-done(((bf16[128,80,128]{2,1,0:T(8,128)(2,1)}), bf16[128,80,128]{2,1,0:T(8,128)(2,1)S(1)}, u32[]{:S(2)}, u32[]{:S(2)}) %all-to-all-start) | async-done | bytes 2621472 | tf_op jit(solution)/shard_map/all_to_all | solution.py:307
  52.2 16.1 %member.1 = (f32[200,512]{1,0:T(8,128)S(1)}, f32[8,200,128]{2,1,0:T(8,128)S(1)}, f32[8,200,128]{2,1,0:T(8,128)}) custom-call(s32[2]{0:T(128)S(1)} %pad_add_fusion.scalar_ref, bf16[128,80,128]{2,1,0:T(8,128)(2,1)S(1)} %all-to-all-done.recv_ref, s32[96,256]{1,0:T(8,128)S(1)} %concatenate.29.place_ref, bf16[264,192]{1,0:T(8,128)(2,1)S(1)} %pad_maximum_fusion.1.table_ref, ...), custom_call_target="tpu_custom_call" | custom-call | tf_op jit(solution)/shard_map/member/pallas_call | solution.py:224
  68.3 0.9 copy-done
  70.5 12.2 %turn_sums.1 = f32[112,128]{1,0:T(8,128)} custom-call(bf16[50,24064]{1,0:T(8,128)(2,1)} %hist_ref.3, s32[1,24064]{1,0:T(1,128)} %broadcast_in_dim.28.label_ref), custom_call_target="tpu_custom_call" | custom-call | tf_op jit(solution)/shard_map/turn_sums/pallas_call | solution.py:99
  82.8 1.0 add.98
  83.7 3.5 %all-to-all-start.1 = ((f32[8,200,128]{2,1,0:T(8,128)}), f32[8,200,128]{2,1,0:T(8,128)S(1)}, u32[]{:S(2)}, u32[]{:S(2)}) async-start(f32[8,200,128]{2,1,0:T(8,128)} %add.98), calls=%async_computation.1 | async-start | bytes 1638400 | tf_op jit(solution)/shard_map/all_to_all | solution.py:330
  87.3 4.1 %collective-permute-start.8 = (f32[312,128]{1,0:T(8,128)S(1)}, f32[312,128]{1,0:T(8,128)S(1)}, u32[]{:S(2)}, u32[]{:S(2)}) collective-permute-start(f32[312,128]{1,0:T(8,128)S(1)} %select_maximum_fusion.refs_0_), channel_id=1, source_target_pairs={{0,14},{1,15},{2,12},{3,13},{4,10},{5,11},{6,8},{7,9},{8,6},{9,7},... | collective-permute-start | bytes 479240 | tf_op jit(solution)/shard_map/ppermute | solution.py:301
  92.0 1.8 %collective-permute-start.6 = (f32[312,128]{1,0:T(8,128)S(1)}, f32[312,128]{1,0:T(8,128)S(1)}, u32[]{:S(2)}, u32[]{:S(2)}) collective-permute-start(f32[312,128]{1,0:T(8,128)S(1)} %select_maximum_fusion.refs_0_), channel_id=1, source_target_pairs={{0,10},{1,11},{2,8},{3,9},{4,14},{5,15},{6,12},{7,13},{8,2},{9,3},... | collective-permute-start | bytes 479240 | tf_op jit(solution)/shard_map/ppermute | solution.py:301
  93.8 1.3 collective-permute-start.5
  95.1 1.6 %collective-permute-start.4 = (f32[312,128]{1,0:T(8,128)S(1)}, f32[312,128]{1,0:T(8,128)S(1)}, u32[]{:S(2)}, u32[]{:S(2)}) collective-permute-start(f32[312,128]{1,0:T(8,128)S(1)} %select_maximum_fusion.refs_0_), channel_id=1, source_target_pairs={{0,6},{1,7},{2,4},{3,5},{4,2},{5,3},{6,0},{7,1},{8,14},{9,15},{10,... | collective-permute-start | bytes 479240 | tf_op jit(solution)/shard_map/ppermute | solution.py:301
  96.7 11.9 %collective-permute-done.8.refs_7_ = f32[312,128]{1,0:T(8,128)S(1)} collective-permute-done((f32[312,128]{1,0:T(8,128)S(1)}, f32[312,128]{1,0:T(8,128)S(1)}, u32[]{:S(2)}, u32[]{:S(2)}) %collective-permute-start.8) | collective-permute-done | bytes 159776 | tf_op jit(solution)/shard_map/ppermute | solution.py:301
  108.6 5.2 %collective-permute-done.7.refs_6_ = f32[312,128]{1,0:T(8,128)S(1)} collective-permute-done((f32[312,128]{1,0:T(8,128)S(1)}, f32[312,128]{1,0:T(8,128)S(1)}, u32[]{:S(2)}, u32[]{:S(2)}) %collective-permute-start.7) | collective-permute-done | bytes 159776 | tf_op jit(solution)/shard_map/ppermute | solution.py:301
  113.9 1.7 %collective-permute-done.3.refs_2_ = f32[312,128]{1,0:T(8,128)S(1)} collective-permute-done((f32[312,128]{1,0:T(8,128)S(1)}, f32[312,128]{1,0:T(8,128)S(1)}, u32[]{:S(2)}, u32[]{:S(2)}) %collective-permute-start.3) | collective-permute-done | bytes 159776 | tf_op jit(solution)/shard_map/ppermute | solution.py:301
  115.6 4.0 %collective-permute-done.2.refs_1_ = f32[312,128]{1,0:T(8,128)S(1)} collective-permute-done((f32[312,128]{1,0:T(8,128)S(1)}, f32[312,128]{1,0:T(8,128)S(1)}, u32[]{:S(2)}, u32[]{:S(2)}) %collective-permute-start.2) | collective-permute-done | bytes 159776 | tf_op jit(solution)/shard_map/ppermute | solution.py:301
  119.7 1.2 collective-permute-done.11
  121.9 4.8 %collective-permute-done.12 = f32[112,128]{1,0:T(8,128)S(1)} collective-permute-done((f32[112,128]{1,0:T(8,128)S(1)}, f32[112,128]{1,0:T(8,128)S(1)}, u32[]{:S(2)}, u32[]{:S(2)}) %collective-permute-start.12) | collective-permute-done | bytes 57376 | tf_op jit(solution)/shard_map/ppermute | solution.py:301
  126.8 1.1 collective-permute-start.10
  128.0 3.6 %nearest.1 = f32[1,1024]{1,0:T(1,128)S(1)} custom-call(f32[200,512]{1,0:T(8,128)S(1)} %get-tuple-element.17.mine_ref, f32[200,512]{1,0:T(8,128)S(1)} %collective-permute-done.1.partner_ref, f32[312,128]{1,0:T(8,128)S(1)} %select_maximum_fusion.refs_0_, f32[312,128]{1,0:T(8,128)S(1)} %collective-permute-done.2.refs_1_, ...), custom_call_target="tpu_custom_call" | custom-call | tf_op jit(solution)/shard_map/nearest/pallas_call | solution.py:261
  131.6 1.6 %collective-permute-done.10 = f32[200,128]{1,0:T(8,128)S(1)} collective-permute-done((f32[200,128]{1,0:T(8,128)S(1)}, f32[200,128]{1,0:T(8,128)S(1)}, u32[]{:S(2)}, u32[]{:S(2)}) %collective-permute-start.10) | collective-permute-done | bytes 102432 | tf_op jit(solution)/shard_map/ppermute | solution.py:301
  134.0 2.2 %collective-permute-start.15 = (f32[312,128]{1,0:T(8,128)S(1)}, f32[312,128]{1,0:T(8,128)S(1)}, u32[]{:S(2)}, u32[]{:S(2)}) collective-permute-start(f32[312,128]{1,0:T(8,128)S(1)} %pad_maximum_fusion), channel_id=1, source_target_pairs={{0,96},{16,112},{32,64},{48,80},{64,32},{80,48},{96,0},{112,16},{1... | collective-permute-start | bytes 479240 | tf_op jit(solution)/shard_map/ppermute | solution.py:301
  137.4 4.2 %collective-permute-done.14 = f32[312,128]{1,0:T(8,128)S(1)} collective-permute-done((f32[312,128]{1,0:T(8,128)S(1)}, f32[312,128]{1,0:T(8,128)S(1)}, u32[]{:S(2)}, u32[]{:S(2)}) %collective-permute-start.14) | collective-permute-done | bytes 159776 | tf_op jit(solution)/shard_map/ppermute | solution.py:301
  141.6 1.6 %collective-permute-done.15 = f32[312,128]{1,0:T(8,128)S(1)} collective-permute-done((f32[312,128]{1,0:T(8,128)S(1)}, f32[312,128]{1,0:T(8,128)S(1)}, u32[]{:S(2)}, u32[]{:S(2)}) %collective-permute-start.15) | collective-permute-done | bytes 159776 | tf_op jit(solution)/shard_map/ppermute | solution.py:301
  (76 shorter events, 8.5 us)
Async XLA Ops:
  5.0 11.4 %copy-start.7 = (f32[50,200]{1,0:T(8,128)S(1)}, f32[50,200]{1,0:T(8,128)}, u32[]{:S(2)}) copy-start(f32[50,200]{1,0:T(8,128)} %param.9) | copy-start | bytes 120004
  5.0 11.7 %copy-start.5 = (s32[47,512]{1,0:T(8,128)S(1)}, s32[47,512]{1,0:T(8,128)}, u32[]{:S(2)}) copy-start(s32[47,512]{1,0:T(8,128)} %param.8) | copy-start | bytes 288772
  5.0 47.2 %all-to-all-start = ((bf16[128,80,128]{2,1,0:T(8,128)(2,1)}), bf16[128,80,128]{2,1,0:T(8,128)(2,1)S(1)}, u32[]{:S(2)}, u32[]{:S(2)}) async-start(bf16[128,80,128]{2,1,0:T(8,128)(2,1)} %pack.1), calls=%async_computation | async-start | bytes 5242880 | tf_op jit(solution)/shard_map/all_to_all | solution.py:307
  16.2 36.0 %copy-start.2 = (s32[512]{0:T(512)S(1)}, s32[512]{0:T(512)}, u32[]{:S(2)}) copy-start(s32[512]{0:T(512)} %param.11) | copy-start | bytes 6148
  16.7 53.0 %copy-start.6 = (s32[24064]{0:T(1024)S(1)}, s32[24064]{0:T(1024)}, u32[]{:S(2)}) copy-start(s32[24064]{0:T(1024)} %param.7) | copy-start | bytes 288772
  69.2 13.5 %copy-start.1 = (f32[8,200,128]{2,1,0:T(8,128)S(1)}, f32[8,200,128]{2,1,0:T(8,128)}, u32[]{:S(2)}) copy-start(f32[8,200,128]{2,1,0:T(8,128)} %copy-done) | copy-start | bytes 2457604
  69.3 13.5 %collective-permute-start = (f32[8,200,128]{2,1,0:T(8,128)}, f32[8,200,128]{2,1,0:T(8,128)S(1)}, u32[]{:S(2)}, u32[]{:S(2)}) collective-permute-start(f32[8,200,128]{2,1,0:T(8,128)} %get-tuple-element.18), channel_id=1, source_target_pairs={{0,1},{1,0},{2,3},{3,2},{4,5},{5,4},{6,7},{7,6},{8,9},{9,8},{10,11... | collective-permute-start | bytes 2457608 | tf_op jit(solution)/shard_map/ppermute | solution.py:301
  69.3 13.5 %collective-permute-start.1 = (f32[200,512]{1,0:T(8,128)S(1)}, f32[200,512]{1,0:T(8,128)S(1)}, u32[]{:S(2)}, u32[]{:S(2)}) collective-permute-start(f32[200,512]{1,0:T(8,128)S(1)} %get-tuple-element.17.mine_ref), channel_id=1, source_target_pairs={{0,1},{1,0},{2,3},{3,2},{4,5},{5,4},{6,7},{7,6},{8,9},{9,8},{10,11... | collective-permute-start | bytes 1228808 | tf_op jit(solution)/shard_map/ppermute | solution.py:301
  82.7 4.6 %copy-start.4 = (f32[200,125]{1,0:T(8,128)S(1)}, f32[200,125]{1,0:T(8,128)}, u32[]{:S(2)}) copy-start(f32[200,125]{1,0:T(8,128)} %param.10) | copy-start | bytes 300004
  83.7 43.0 %all-to-all-start.1 = ((f32[8,200,128]{2,1,0:T(8,128)}), f32[8,200,128]{2,1,0:T(8,128)S(1)}, u32[]{:S(2)}, u32[]{:S(2)}) async-start(f32[8,200,128]{2,1,0:T(8,128)} %add.98), calls=%async_computation.1 | async-start | bytes 1638400 | tf_op jit(solution)/shard_map/all_to_all | solution.py:330
  87.3 21.2 %collective-permute-start.8 = (f32[312,128]{1,0:T(8,128)S(1)}, f32[312,128]{1,0:T(8,128)S(1)}, u32[]{:S(2)}, u32[]{:S(2)}) collective-permute-start(f32[312,128]{1,0:T(8,128)S(1)} %select_maximum_fusion.refs_0_), channel_id=1, source_target_pairs={{0,14},{1,15},{2,12},{3,13},{4,10},{5,11},{6,8},{7,9},{8,6},{9,7},... | collective-permute-start | bytes 479240 | tf_op jit(solution)/shard_map/ppermute | solution.py:301
  91.5 22.2 %collective-permute-start.7 = (f32[312,128]{1,0:T(8,128)S(1)}, f32[312,128]{1,0:T(8,128)S(1)}, u32[]{:S(2)}, u32[]{:S(2)}) collective-permute-start(f32[312,128]{1,0:T(8,128)S(1)} %select_maximum_fusion.refs_0_), channel_id=1, source_target_pairs={{0,12},{1,13},{2,14},{3,15},{4,8},{5,9},{6,10},{7,11},{8,4},{9,5},... | collective-permute-start | bytes 479240 | tf_op jit(solution)/shard_map/ppermute | solution.py:301
  92.0 21.8 %collective-permute-start.6 = (f32[312,128]{1,0:T(8,128)S(1)}, f32[312,128]{1,0:T(8,128)S(1)}, u32[]{:S(2)}, u32[]{:S(2)}) collective-permute-start(f32[312,128]{1,0:T(8,128)S(1)} %select_maximum_fusion.refs_0_), channel_id=1, source_target_pairs={{0,10},{1,11},{2,8},{3,9},{4,14},{5,15},{6,12},{7,13},{8,2},{9,3},... | collective-permute-start | bytes 479240 | tf_op jit(solution)/shard_map/ppermute | solution.py:301
  93.8 20.2 %collective-permute-start.5 = (f32[312,128]{1,0:T(8,128)S(1)}, f32[312,128]{1,0:T(8,128)S(1)}, u32[]{:S(2)}, u32[]{:S(2)}) collective-permute-start(f32[312,128]{1,0:T(8,128)S(1)} %select_maximum_fusion.refs_0_), channel_id=1, source_target_pairs={{0,8},{1,9},{2,10},{3,11},{4,12},{5,13},{6,14},{7,15},{8,0},{9,1},... | collective-permute-start | bytes 479240 | tf_op jit(solution)/shard_map/ppermute | solution.py:301
  95.1 18.8 %collective-permute-start.4 = (f32[312,128]{1,0:T(8,128)S(1)}, f32[312,128]{1,0:T(8,128)S(1)}, u32[]{:S(2)}, u32[]{:S(2)}) collective-permute-start(f32[312,128]{1,0:T(8,128)S(1)} %select_maximum_fusion.refs_0_), channel_id=1, source_target_pairs={{0,6},{1,7},{2,4},{3,5},{4,2},{5,3},{6,0},{7,1},{8,14},{9,15},{10,... | collective-permute-start | bytes 479240 | tf_op jit(solution)/shard_map/ppermute | solution.py:301
  108.6 7.1 %collective-permute-start.3 = (f32[312,128]{1,0:T(8,128)S(1)}, f32[312,128]{1,0:T(8,128)S(1)}, u32[]{:S(2)}, u32[]{:S(2)}) collective-permute-start(f32[312,128]{1,0:T(8,128)S(1)} %select_maximum_fusion.refs_0_), channel_id=1, source_target_pairs={{0,4},{1,5},{2,6},{3,7},{4,0},{5,1},{6,2},{7,3},{8,12},{9,13},{10,... | collective-permute-start | bytes 479240 | tf_op jit(solution)/shard_map/ppermute | solution.py:301
  113.7 5.9 %collective-permute-start.2 = (f32[312,128]{1,0:T(8,128)S(1)}, f32[312,128]{1,0:T(8,128)S(1)}, u32[]{:S(2)}, u32[]{:S(2)}) collective-permute-start(f32[312,128]{1,0:T(8,128)S(1)} %select_maximum_fusion.refs_0_), channel_id=1, source_target_pairs={{0,2},{1,3},{2,0},{3,1},{4,6},{5,7},{6,4},{7,5},{8,10},{9,11},{10,... | collective-permute-start | bytes 479240 | tf_op jit(solution)/shard_map/ppermute | solution.py:301
  119.6 1.3 collective-permute-start.11
  121.0 5.8 %collective-permute-start.12 = (f32[112,128]{1,0:T(8,128)S(1)}, f32[112,128]{1,0:T(8,128)S(1)}, u32[]{:S(2)}, u32[]{:S(2)}) collective-permute-start(f32[112,128]{1,0:T(8,128)S(1)} %add.107), channel_id=1, source_target_pairs={{0,16},{16,0},{32,48},{48,32},{64,80},{80,64},{96,112},{112,96},{1... | collective-permute-start | bytes 172040 | tf_op jit(solution)/shard_map/ppermute | solution.py:301
  126.8 6.4 %collective-permute-start.10 = (f32[200,128]{1,0:T(8,128)S(1)}, f32[200,128]{1,0:T(8,128)S(1)}, u32[]{:S(2)}, u32[]{:S(2)}) collective-permute-start(f32[200,128]{1,0:T(8,128)S(1)} %reduce_sum.39), channel_id=1, source_target_pairs={{0,16},{16,0},{32,48},{48,32},{64,80},{80,64},{96,112},{112,96},{1... | collective-permute-start | bytes 307208 | tf_op jit(solution)/shard_map/ppermute | solution.py:301
  131.5 5.3 %collective-permute-start.9 = (f32[1,512]{1,0:T(1,128)S(1)}, f32[1,512]{1,0:T(1,128)S(1)}, u32[]{:S(2)}, u32[]{:S(2)}) collective-permute-start(f32[1,512]{1,0:T(1,128)S(1)} %slice.85), channel_id=1, source_target_pairs={{0,1},{1,0},{2,3},{3,2},{4,5},{5,4},{6,7},{7,6},{8,9},{9,8},{10,11... | collective-permute-start | bytes 6152 | tf_op jit(solution)/shard_map/ppermute | solution.py:301
  133.3 8.3 %collective-permute-start.14 = (f32[312,128]{1,0:T(8,128)S(1)}, f32[312,128]{1,0:T(8,128)S(1)}, u32[]{:S(2)}, u32[]{:S(2)}) collective-permute-start(f32[312,128]{1,0:T(8,128)S(1)} %pad_maximum_fusion), channel_id=1, source_target_pairs={{0,64},{16,80},{32,96},{48,112},{64,0},{80,16},{96,32},{112,48},{1... | collective-permute-start | bytes 479240 | tf_op jit(solution)/shard_map/ppermute | solution.py:301
  134.0 9.2 %collective-permute-start.15 = (f32[312,128]{1,0:T(8,128)S(1)}, f32[312,128]{1,0:T(8,128)S(1)}, u32[]{:S(2)}, u32[]{:S(2)}) collective-permute-start(f32[312,128]{1,0:T(8,128)S(1)} %pad_maximum_fusion), channel_id=1, source_target_pairs={{0,96},{16,112},{32,64},{48,80},{64,32},{80,48},{96,0},{112,16},{1... | collective-permute-start | bytes 479240 | tf_op jit(solution)/shard_map/ppermute | solution.py:301
  136.2 7.0 %collective-permute-start.13 = (f32[312,128]{1,0:T(8,128)S(1)}, f32[312,128]{1,0:T(8,128)S(1)}, u32[]{:S(2)}, u32[]{:S(2)}) collective-permute-start(f32[312,128]{1,0:T(8,128)S(1)} %pad_maximum_fusion), channel_id=1, source_target_pairs={{0,32},{16,48},{32,0},{48,16},{64,96},{80,112},{96,64},{112,80},{1... | collective-permute-start | bytes 479240 | tf_op jit(solution)/shard_map/ppermute | solution.py:301
  (2 other events, 5.5 us)

commit v6 on v5

--- a/solution.py
+++ b/solution.py
@@ -301,6 +301,10 @@
     return lax.ppermute(x, axis, [(i, i ^ mask) for i in range(size)])
 
 
+def add_over_z(x):
+    return (x + swap(x, "board", 2)) + (swap(x, "board", 4) + swap(x, "board", 6))
+
+
 def body(turn_hist, turn_assign, child_rows, turn_centers, flop_centers, flop_assign):
     sent = pack(turn_hist)
     turn_assign, sent = lax.optimization_barrier((turn_assign, sent))
@@ -328,13 +332,13 @@
     received, partner = lax.optimization_barrier((swap(send, "cent", 1), swap(flop_hist, "cent", 1)))
     half = keep + received
     parts = lax.all_to_all(half, "cent", split_axis=0, concat_axis=0, tiled=True, axis_index_groups=CHIPS)
-    flop_part = jnp.sum(parts, axis=0)
+    flop_part, turn_part = lax.optimization_barrier((jnp.sum(parts, axis=0), turn_part))
     flop_part = flop_part + swap(flop_part, "board", 1)
-    total = jnp.concatenate([flop_part, turn_part], axis=0)
-    total = (total + swap(total, "board", 2)) + (swap(total, "board", 4) + swap(total, "board", 6))
-    flop_sums = total[:TURN_CENT, :PANEL].T * (PANEL * 16 / (HANDS * DEVICES))
-    turn_low = total[TURN_CENT:TURN_CENT + BINS]
-    turn_high = total[TURN_CENT + TURN_SPLIT:TURN_CENT + TURN_SPLIT + BINS, :TURN_CENT - LANES]
+    flop_part = add_over_z(flop_part)
+    turn_part = add_over_z(turn_part)
+    flop_sums = flop_part[:, :PANEL].T * (PANEL * 16 / (HANDS * DEVICES))
+    turn_low = turn_part[:BINS]
+    turn_high = turn_part[TURN_SPLIT:TURN_SPLIT + BINS, :TURN_CENT - LANES]
     turn_sums = jnp.concatenate([turn_low, turn_high], axis=1)
     turn_sums = turn_sums * (BINS * TURN_CENT / (turn_hist.shape[1] * DEVICES))
 

time: 145 us -> 147 us (1.014)
  starting transfers between devices: 30.4 us -> 37.1 us
  waiting for transfers between devices: 70.2 us -> 64.9 us
    ppermute x16 -> x19, starting transfers between devices: 15.7 us -> 22.4 us  [swap(): return lax.ppermute(x, axis, [(i, i ^ mask) for i in range(size)])]
    ppermute x16 -> x19, waiting for transfers between devices: 36.3 us -> 31 us  [swap(): return lax.ppermute(x, axis, [(i, i ^ mask) for i in range(size)])]
  transfers between devices with their start and end apart: 18 -> 21, of which waited for: 11 -> 11; matrix products, arithmetic and copies ran while one was open for 2% -> 4% of each run, Pallas kernels for 11% -> 11%
where the time goes in v6:
time: 147 us
  waiting for transfers between devices  64.9 us (44%)
  starting transfers between devices  37.1 us (25%)
  Pallas kernels  36.3 us (25%)
  other arithmetic  4.3 us (3%)
  local copies, waits for them, and re-layouts  2.57 us (2%)
    all_to_all x1, waiting for transfers between devices, body(): lax.all_to_all(sent, ('board', 'cent'), split_axis=0, concat_axis=0, tile...  33.9 us
    ppermute x19, waiting for transfers between devices, swap(): return lax.ppermute(x, axis, [(i, i ^ mask) for i in range(size)])  31 us
    ppermute x19, starting transfers between devices, swap(): return lax.ppermute(x, axis, [(i, i ^ mask) for i in range(size)])  22.4 us
    pallas_call x1, Pallas kernels, member(): pl.pallas_call(member_kernel, in_specs=[SMEM, VMEM, VMEM, VMEM, VMEM], ou...  16.1 us
    pallas_call x1, Pallas kernels, turn_partial(): pl.pallas_call(turn_kernel, grid=(steps,), in_specs=[pl.BlockSpec((BINS,...  12.2 us
    all_to_all x1, starting transfers between devices, body(): lax.all_to_all(sent, ('board', 'cent'), split_axis=0, concat_axis=0, tile...  11.2 us
    pallas_call x1, Pallas kernels, pack(): pl.pallas_call(pack_kernel, grid=(DEVICES // SOURCES_PER_STEP,), in_specs...  4.38 us
    pallas_call x1, Pallas kernels, nearest_of(): pl.pallas_call(nearest_kernel, in_specs=[VMEM] * (2 + len(pieces)), out_s...  3.58 us
  transfers between devices with their start and end apart: 21, of which 11 were waited for; matrix products, arithmetic and copies ran while one was open for 4% of the time, Pallas kernels for 11%

profile of v6, /device:TPU:0, one launch (start us, length us, event | category | flops | bytes accessed | tf_op | source)
XLA Modules:
  0.0 146.8 jit_solution(10608982332126486904)
XLA Ops:
  0.6 4.4 %pack.1 = bf16[128,80,128]{2,1,0:T(8,128)(2,1)} custom-call(bf16[50,24064]{1,0:T(8,128)(2,1)} %hist_ref.3), custom_call_target="tpu_custom_call" | custom-call | tf_op jit(solution)/shard_map/pack/pallas_call | solution.py:65
  5.0 11.2 %all-to-all-start = ((bf16[128,80,128]{2,1,0:T(8,128)(2,1)}), bf16[128,80,128]{2,1,0:T(8,128)(2,1)S(1)}, u32[]{:S(2)}, u32[]{:S(2)}) async-start(bf16[128,80,128]{2,1,0:T(8,128)(2,1)} %pack.1), calls=%async_computation | async-start | bytes 5242880 | tf_op jit(solution)/shard_map/all_to_all | solution.py:311
  18.3 33.9 %all-to-all-done.recv_ref = bf16[128,80,128]{2,1,0:T(8,128)(2,1)S(1)} async-done(((bf16[128,80,128]{2,1,0:T(8,128)(2,1)}), bf16[128,80,128]{2,1,0:T(8,128)(2,1)S(1)}, u32[]{:S(2)}, u32[]{:S(2)}) %all-to-all-start) | async-done | bytes 2621472 | tf_op jit(solution)/shard_map/all_to_all | solution.py:311
  52.2 16.1 %member.1 = (f32[200,512]{1,0:T(8,128)S(1)}, f32[8,200,128]{2,1,0:T(8,128)S(1)}, f32[8,200,128]{2,1,0:T(8,128)}) custom-call(s32[2]{0:T(128)S(1)} %pad_add_fusion.scalar_ref, bf16[128,80,128]{2,1,0:T(8,128)(2,1)S(1)} %all-to-all-done.recv_ref, s32[96,256]{1,0:T(8,128)S(1)} %concatenate.26.place_ref, bf16[264,192]{1,0:T(8,128)(2,1)S(1)} %pad_maximum_fusion.table_ref, ...), custom_call_target="tpu_custom_call" | custom-call | tf_op jit(solution)/shard_map/member/pallas_call | solution.py:224
  70.5 12.2 %turn_sums.1 = f32[112,128]{1,0:T(8,128)} custom-call(bf16[50,24064]{1,0:T(8,128)(2,1)} %hist_ref.3, s32[1,24064]{1,0:T(1,128)} %broadcast_in_dim.28.label_ref), custom_call_target="tpu_custom_call" | custom-call | tf_op jit(solution)/shard_map/turn_sums/pallas_call | solution.py:99
  83.7 3.2 %collective-permute-start.7 = (f32[312,128]{1,0:T(8,128)S(1)}, f32[312,128]{1,0:T(8,128)S(1)}, u32[]{:S(2)}, u32[]{:S(2)}) collective-permute-start(f32[312,128]{1,0:T(8,128)S(1)} %select_maximum_fusion.refs_0_), channel_id=1, source_target_pairs={{0,12},{1,13},{2,14},{3,15},{4,8},{5,9},{6,10},{7,11},{8,4},{9,5},... | collective-permute-start | bytes 479240 | tf_op jit(solution)/shard_map/ppermute | solution.py:301
  87.0 1.0 add.107
  88.0 3.5 %all-to-all-start.1 = ((f32[8,200,128]{2,1,0:T(8,128)}), f32[8,200,128]{2,1,0:T(8,128)S(1)}, u32[]{:S(2)}, u32[]{:S(2)}) async-start(f32[8,200,128]{2,1,0:T(8,128)} %add.107), calls=%async_computation.1 | async-start | bytes 1638400 | tf_op jit(solution)/shard_map/all_to_all | solution.py:334
  91.5 4.4 %collective-permute-start.6 = (f32[312,128]{1,0:T(8,128)S(1)}, f32[312,128]{1,0:T(8,128)S(1)}, u32[]{:S(2)}, u32[]{:S(2)}) collective-permute-start(f32[312,128]{1,0:T(8,128)S(1)} %select_maximum_fusion.refs_0_), channel_id=1, source_target_pairs={{0,10},{1,11},{2,8},{3,9},{4,14},{5,15},{6,12},{7,13},{8,2},{9,3},... | collective-permute-start | bytes 479240 | tf_op jit(solution)/shard_map/ppermute | solution.py:301
  96.4 1.5 %collective-permute-start.4 = (f32[312,128]{1,0:T(8,128)S(1)}, f32[312,128]{1,0:T(8,128)S(1)}, u32[]{:S(2)}, u32[]{:S(2)}) collective-permute-start(f32[312,128]{1,0:T(8,128)S(1)} %select_maximum_fusion.refs_0_), channel_id=1, source_target_pairs={{0,6},{1,7},{2,4},{3,5},{4,2},{5,3},{6,0},{7,1},{8,14},{9,15},{10,... | collective-permute-start | bytes 479240 | tf_op jit(solution)/shard_map/ppermute | solution.py:301
  98.1 1.8 %collective-permute-start.2 = (f32[312,128]{1,0:T(8,128)S(1)}, f32[312,128]{1,0:T(8,128)S(1)}, u32[]{:S(2)}, u32[]{:S(2)}) collective-permute-start(f32[312,128]{1,0:T(8,128)S(1)} %select_maximum_fusion.refs_0_), channel_id=1, source_target_pairs={{0,2},{1,3},{2,0},{3,1},{4,6},{5,7},{6,4},{7,5},{8,10},{9,11},{10,... | collective-permute-start | bytes 479240 | tf_op jit(solution)/shard_map/ppermute | solution.py:301
  99.9 9.9 %collective-permute-done.6.refs_5_ = f32[312,128]{1,0:T(8,128)S(1)} collective-permute-done((f32[312,128]{1,0:T(8,128)S(1)}, f32[312,128]{1,0:T(8,128)S(1)}, u32[]{:S(2)}, u32[]{:S(2)}) %collective-permute-start.6) | collective-permute-done | bytes 159776 | tf_op jit(solution)/shard_map/ppermute | solution.py:301
  109.8 5.9 %collective-permute-done.5.refs_4_ = f32[312,128]{1,0:T(8,128)S(1)} collective-permute-done((f32[312,128]{1,0:T(8,128)S(1)}, f32[312,128]{1,0:T(8,128)S(1)}, u32[]{:S(2)}, u32[]{:S(2)}) %collective-permute-start.5) | collective-permute-done | bytes 159776 | tf_op jit(solution)/shard_map/ppermute | solution.py:301
  116.3 1.2 collective-permute-done.10
  117.5 1.0 collective-permute-start.11
  118.5 5.0 %collective-permute-done.11 = f32[112,128]{1,0:T(8,128)S(1)} collective-permute-done((f32[112,128]{1,0:T(8,128)S(1)}, f32[112,128]{1,0:T(8,128)S(1)}, u32[]{:S(2)}, u32[]{:S(2)}) %collective-permute-start.11) | collective-permute-done | bytes 57376 | tf_op jit(solution)/shard_map/ppermute | solution.py:301
  123.5 3.6 %nearest.1 = f32[1,1024]{1,0:T(1,128)S(1)} custom-call(f32[200,512]{1,0:T(8,128)S(1)} %get-tuple-element.19.mine_ref, f32[200,512]{1,0:T(8,128)S(1)} %collective-permute-done.1.partner_ref, f32[312,128]{1,0:T(8,128)S(1)} %select_maximum_fusion.refs_0_, f32[312,128]{1,0:T(8,128)S(1)} %collective-permute-done.2.refs_1_, ...), custom_call_target="tpu_custom_call" | custom-call | tf_op jit(solution)/shard_map/nearest/pallas_call | solution.py:261
  128.0 1.2 collective-permute-start.13
  129.1 2.3 %collective-permute-start.12 = (f32[112,128]{1,0:T(8,128)S(1)}, f32[112,128]{1,0:T(8,128)S(1)}, u32[]{:S(2)}, u32[]{:S(2)}) collective-permute-start(f32[112,128]{1,0:T(8,128)S(1)} %add.116), channel_id=1, source_target_pairs={{0,32},{16,48},{32,0},{48,16},{64,96},{80,112},{96,64},{112,80},{1... | collective-permute-start | bytes 172040 | tf_op jit(solution)/shard_map/ppermute | solution.py:301
  132.8 1.4 collective-permute-done.14
  134.7 3.5 %collective-permute-done.15 = f32[200,128]{1,0:T(8,128)S(1)} collective-permute-done((f32[200,128]{1,0:T(8,128)S(1)}, f32[200,128]{1,0:T(8,128)S(1)}, u32[]{:S(2)}, u32[]{:S(2)}) %collective-permute-start.15) | collective-permute-done | bytes 102432 | tf_op jit(solution)/shard_map/ppermute | solution.py:301
  138.9 1.5 %collective-permute-start.17 = (f32[200,128]{1,0:T(8,128)S(1)}, f32[200,128]{1,0:T(8,128)S(1)}, u32[]{:S(2)}, u32[]{:S(2)}) collective-permute-start(f32[200,128]{1,0:T(8,128)S(1)} %add.120), channel_id=1, source_target_pairs={{0,64},{16,80},{32,96},{48,112},{64,0},{80,16},{96,32},{112,48},{1... | collective-permute-start | bytes 307208 | tf_op jit(solution)/shard_map/ppermute | solution.py:301
  140.4 2.0 %collective-permute-start.16 = (f32[200,128]{1,0:T(8,128)S(1)}, f32[200,128]{1,0:T(8,128)S(1)}, u32[]{:S(2)}, u32[]{:S(2)}) collective-permute-start(f32[200,128]{1,0:T(8,128)S(1)} %add.120), channel_id=1, source_target_pairs={{0,32},{16,48},{32,0},{48,16},{64,96},{80,112},{96,64},{112,80},{1... | collective-permute-start | bytes 307208 | tf_op jit(solution)/shard_map/ppermute | solution.py:301
  143.0 2.2 %collective-permute-done.18 = f32[200,128]{1,0:T(8,128)S(1)} collective-permute-done((f32[200,128]{1,0:T(8,128)S(1)}, f32[200,128]{1,0:T(8,128)S(1)}, u32[]{:S(2)}, u32[]{:S(2)}) %collective-permute-start.18) | collective-permute-done | bytes 102432 | tf_op jit(solution)/shard_map/ppermute | solution.py:301
  (81 shorter events, 11.9 us)
Async XLA Ops:
  5.0 47.2 %all-to-all-start = ((bf16[128,80,128]{2,1,0:T(8,128)(2,1)}), bf16[128,80,128]{2,1,0:T(8,128)(2,1)S(1)}, u32[]{:S(2)}, u32[]{:S(2)}) async-start(bf16[128,80,128]{2,1,0:T(8,128)(2,1)} %pack.1), calls=%async_computation | async-start | bytes 5242880 | tf_op jit(solution)/shard_map/all_to_all | solution.py:311
  16.2 36.0 %copy-start.2 = (s32[512]{0:T(512)S(1)}, s32[512]{0:T(512)}, u32[]{:S(2)}) copy-start(s32[512]{0:T(512)} %param.11) | copy-start | bytes 6148
  16.7 53.1 %copy-start.6 = (s32[24064]{0:T(1024)S(1)}, s32[24064]{0:T(1024)}, u32[]{:S(2)}) copy-start(s32[24064]{0:T(1024)} %param.7) | copy-start | bytes 288772
  69.3 17.7 %collective-permute-start = (f32[8,200,128]{2,1,0:T(8,128)}, f32[8,200,128]{2,1,0:T(8,128)S(1)}, u32[]{:S(2)}, u32[]{:S(2)}) collective-permute-start(f32[8,200,128]{2,1,0:T(8,128)} %get-tuple-element.20), channel_id=1, source_target_pairs={{0,1},{1,0},{2,3},{3,2},{4,5},{5,4},{6,7},{7,6},{8,9},{9,8},{10,11... | collective-permute-start | bytes 2457608 | tf_op jit(solution)/shard_map/ppermute | solution.py:301
  69.3 17.7 %collective-permute-start.1 = (f32[200,512]{1,0:T(8,128)S(1)}, f32[200,512]{1,0:T(8,128)S(1)}, u32[]{:S(2)}, u32[]{:S(2)}) collective-permute-start(f32[200,512]{1,0:T(8,128)S(1)} %get-tuple-element.19.mine_ref), channel_id=1, source_target_pairs={{0,1},{1,0},{2,3},{3,2},{4,5},{5,4},{6,7},{7,6},{8,9},{9,8},{10,11... | collective-permute-start | bytes 1228808 | tf_op jit(solution)/shard_map/ppermute | solution.py:301
  82.7 33.4 %copy-start.3 = (f32[112,128]{1,0:T(8,128)S(1)}, f32[112,128]{1,0:T(8,128)}, u32[]{:S(2)}) copy-start(f32[112,128]{1,0:T(8,128)} %turn_sums.1) | copy-start | bytes 172036
  83.7 14.2 %collective-permute-start.8 = (f32[312,128]{1,0:T(8,128)S(1)}, f32[312,128]{1,0:T(8,128)S(1)}, u32[]{:S(2)}, u32[]{:S(2)}) collective-permute-start(f32[312,128]{1,0:T(8,128)S(1)} %select_maximum_fusion.refs_0_), channel_id=1, source_target_pairs={{0,14},{1,15},{2,12},{3,13},{4,10},{5,11},{6,8},{7,9},{8,6},{9,7},... | collective-permute-start | bytes 479240 | tf_op jit(solution)/shard_map/ppermute | solution.py:301
  83.7 14.3 %collective-permute-start.7 = (f32[312,128]{1,0:T(8,128)S(1)}, f32[312,128]{1,0:T(8,128)S(1)}, u32[]{:S(2)}, u32[]{:S(2)}) collective-permute-start(f32[312,128]{1,0:T(8,128)S(1)} %select_maximum_fusion.refs_0_), channel_id=1, source_target_pairs={{0,12},{1,13},{2,14},{3,15},{4,8},{5,9},{6,10},{7,11},{8,4},{9,5},... | collective-permute-start | bytes 479240 | tf_op jit(solution)/shard_map/ppermute | solution.py:301
  88.0 39.3 %all-to-all-start.1 = ((f32[8,200,128]{2,1,0:T(8,128)}), f32[8,200,128]{2,1,0:T(8,128)S(1)}, u32[]{:S(2)}, u32[]{:S(2)}) async-start(f32[8,200,128]{2,1,0:T(8,128)} %add.107), calls=%async_computation.1 | async-start | bytes 1638400 | tf_op jit(solution)/shard_map/all_to_all | solution.py:334
  91.5 18.3 %collective-permute-start.6 = (f32[312,128]{1,0:T(8,128)S(1)}, f32[312,128]{1,0:T(8,128)S(1)}, u32[]{:S(2)}, u32[]{:S(2)}) collective-permute-start(f32[312,128]{1,0:T(8,128)S(1)} %select_maximum_fusion.refs_0_), channel_id=1, source_target_pairs={{0,10},{1,11},{2,8},{3,9},{4,14},{5,15},{6,12},{7,13},{8,2},{9,3},... | collective-permute-start | bytes 479240 | tf_op jit(solution)/shard_map/ppermute | solution.py:301
  95.9 19.9 %collective-permute-start.5 = (f32[312,128]{1,0:T(8,128)S(1)}, f32[312,128]{1,0:T(8,128)S(1)}, u32[]{:S(2)}, u32[]{:S(2)}) collective-permute-start(f32[312,128]{1,0:T(8,128)S(1)} %select_maximum_fusion.refs_0_), channel_id=1, source_target_pairs={{0,8},{1,9},{2,10},{3,11},{4,12},{5,13},{6,14},{7,15},{8,0},{9,1},... | collective-permute-start | bytes 479240 | tf_op jit(solution)/shard_map/ppermute | solution.py:301
  96.4 19.4 %collective-permute-start.4 = (f32[312,128]{1,0:T(8,128)S(1)}, f32[312,128]{1,0:T(8,128)S(1)}, u32[]{:S(2)}, u32[]{:S(2)}) collective-permute-start(f32[312,128]{1,0:T(8,128)S(1)} %select_maximum_fusion.refs_0_), channel_id=1, source_target_pairs={{0,6},{1,7},{2,4},{3,5},{4,2},{5,3},{6,0},{7,1},{8,14},{9,15},{10,... | collective-permute-start | bytes 479240 | tf_op jit(solution)/shard_map/ppermute | solution.py:301
  97.9 18.3 %collective-permute-start.3 = (f32[312,128]{1,0:T(8,128)S(1)}, f32[312,128]{1,0:T(8,128)S(1)}, u32[]{:S(2)}, u32[]{:S(2)}) collective-permute-start(f32[312,128]{1,0:T(8,128)S(1)} %select_maximum_fusion.refs_0_), channel_id=1, source_target_pairs={{0,4},{1,5},{2,6},{3,7},{4,0},{5,1},{6,2},{7,3},{8,12},{9,13},{10,... | collective-permute-start | bytes 479240 | tf_op jit(solution)/shard_map/ppermute | solution.py:301
  98.1 18.1 %collective-permute-start.2 = (f32[312,128]{1,0:T(8,128)S(1)}, f32[312,128]{1,0:T(8,128)S(1)}, u32[]{:S(2)}, u32[]{:S(2)}) collective-permute-start(f32[312,128]{1,0:T(8,128)S(1)} %select_maximum_fusion.refs_0_), channel_id=1, source_target_pairs={{0,2},{1,3},{2,0},{3,1},{4,6},{5,7},{6,4},{7,5},{8,10},{9,11},{10,... | collective-permute-start | bytes 479240 | tf_op jit(solution)/shard_map/ppermute | solution.py:301
  116.2 1.3 collective-permute-start.10
  117.5 5.9 %collective-permute-start.11 = (f32[112,128]{1,0:T(8,128)S(1)}, f32[112,128]{1,0:T(8,128)S(1)}, u32[]{:S(2)}, u32[]{:S(2)}) collective-permute-start(f32[112,128]{1,0:T(8,128)S(1)} %add.115), channel_id=1, source_target_pairs={{0,16},{16,0},{32,48},{48,32},{64,80},{80,64},{96,112},{112,96},{1... | collective-permute-start | bytes 172040 | tf_op jit(solution)/shard_map/ppermute | solution.py:301
  127.1 4.4 %collective-permute-start.9 = (f32[1,512]{1,0:T(1,128)S(1)}, f32[1,512]{1,0:T(1,128)S(1)}, u32[]{:S(2)}, u32[]{:S(2)}) collective-permute-start(f32[1,512]{1,0:T(1,128)S(1)} %slice.85), channel_id=1, source_target_pairs={{0,1},{1,0},{2,3},{3,2},{4,5},{5,4},{6,7},{7,6},{8,9},{9,8},{10,11... | collective-permute-start | bytes 6152 | tf_op jit(solution)/shard_map/ppermute | solution.py:301
  127.3 6.8 %collective-permute-start.14 = (f32[112,128]{1,0:T(8,128)S(1)}, f32[112,128]{1,0:T(8,128)S(1)}, u32[]{:S(2)}, u32[]{:S(2)}) collective-permute-start(f32[112,128]{1,0:T(8,128)S(1)} %add.116), channel_id=1, source_target_pairs={{0,96},{16,112},{32,64},{48,80},{64,32},{80,48},{96,0},{112,16},{1... | collective-permute-start | bytes 172040 | tf_op jit(solution)/shard_map/ppermute | solution.py:301
  128.0 6.2 %collective-permute-start.13 = (f32[112,128]{1,0:T(8,128)S(1)}, f32[112,128]{1,0:T(8,128)S(1)}, u32[]{:S(2)}, u32[]{:S(2)}) collective-permute-start(f32[112,128]{1,0:T(8,128)S(1)} %add.116), channel_id=1, source_target_pairs={{0,64},{16,80},{32,96},{48,112},{64,0},{80,16},{96,32},{112,48},{1... | collective-permute-start | bytes 172040 | tf_op jit(solution)/shard_map/ppermute | solution.py:301
  129.1 5.6 %collective-permute-start.12 = (f32[112,128]{1,0:T(8,128)S(1)}, f32[112,128]{1,0:T(8,128)S(1)}, u32[]{:S(2)}, u32[]{:S(2)}) collective-permute-start(f32[112,128]{1,0:T(8,128)S(1)} %add.116), channel_id=1, source_target_pairs={{0,32},{16,48},{32,0},{48,16},{64,96},{80,112},{96,64},{112,80},{1... | collective-permute-start | bytes 172040 | tf_op jit(solution)/shard_map/ppermute | solution.py:301
  132.0 6.2 %collective-permute-start.15 = (f32[200,128]{1,0:T(8,128)S(1)}, f32[200,128]{1,0:T(8,128)S(1)}, u32[]{:S(2)}, u32[]{:S(2)}) collective-permute-start(f32[200,128]{1,0:T(8,128)S(1)} %reduce_sum.39), channel_id=1, source_target_pairs={{0,16},{16,0},{32,48},{48,32},{64,80},{80,64},{96,112},{112,96},{1... | collective-permute-start | bytes 307208 | tf_op jit(solution)/shard_map/ppermute | solution.py:301
  138.2 7.0 %collective-permute-start.18 = (f32[200,128]{1,0:T(8,128)S(1)}, f32[200,128]{1,0:T(8,128)S(1)}, u32[]{:S(2)}, u32[]{:S(2)}) collective-permute-start(f32[200,128]{1,0:T(8,128)S(1)} %add.120), channel_id=1, source_target_pairs={{0,96},{16,112},{32,64},{48,80},{64,32},{80,48},{96,0},{112,16},{1... | collective-permute-start | bytes 307208 | tf_op jit(solution)/shard_map/ppermute | solution.py:301
  138.9 6.4 %collective-permute-start.17 = (f32[200,128]{1,0:T(8,128)S(1)}, f32[200,128]{1,0:T(8,128)S(1)}, u32[]{:S(2)}, u32[]{:S(2)}) collective-permute-start(f32[200,128]{1,0:T(8,128)S(1)} %add.120), channel_id=1, source_target_pairs={{0,64},{16,80},{32,96},{48,112},{64,0},{80,16},{96,32},{112,48},{1... | collective-permute-start | bytes 307208 | tf_op jit(solution)/shard_map/ppermute | solution.py:301
  140.4 5.7 %collective-permute-start.16 = (f32[200,128]{1,0:T(8,128)S(1)}, f32[200,128]{1,0:T(8,128)S(1)}, u32[]{:S(2)}, u32[]{:S(2)}) collective-permute-start(f32[200,128]{1,0:T(8,128)S(1)} %add.120), channel_id=1, source_target_pairs={{0,32},{16,48},{32,0},{48,16},{64,96},{80,112},{96,64},{112,80},{1... | collective-permute-start | bytes 307208 | tf_op jit(solution)/shard_map/ppermute | solution.py:301
  (5 other events, 72.3 us)

commit v7 on v5

--- a/solution.py
+++ b/solution.py
@@ -240,14 +240,13 @@
     )(scalars, recv, place, table, assign)
 
 
-def nearest_kernel(mine_ref, partner_ref, *refs):
-    pieces, out_ref = refs[:-1], refs[-1]
+def nearest_kernel(mine_ref, partner_ref, pieces_ref, out_ref):
     one = jnp.where(lax.broadcasted_iota(i32, (8, 2 * HANDS), 0) == 0, 1.0, 0.0)
     hands = jnp.concatenate([jnp.concatenate([mine_ref[...], partner_ref[...]], axis=1), one], axis=0)
     lane = lax.broadcasted_iota(i32, (8, LANES), 1)
     best = None
-    for ref in pieces:
-        c = ref[0:TURN_CENT, :]
+    for i in range(pieces_ref.shape[0]):
+        c = pieces_ref[i, 0:TURN_CENT, :]
         sq = jnp.broadcast_to(jnp.sum(c * c, axis=0, keepdims=True), (8, LANES))
         sides = jnp.concatenate([-2.0 * c, jnp.where(lane < PANEL, sq, 1e30)], axis=0)
         dist = lax.dot_general(
@@ -260,12 +259,12 @@
 def nearest_of(pieces, flop_hist, partner):
     best = pl.pallas_call(
         nearest_kernel,
-        in_specs=[VMEM] * (2 + len(pieces)),
+        in_specs=[VMEM, VMEM, VMEM],
         out_specs=VMEM,
         out_shape=jax.ShapeDtypeStruct((1, 2 * HANDS), f32),
     compiler_params=pltpu.CompilerParams(vmem_limit_bytes=24 * 1024 * 1024),
         name="nearest",
-    )(flop_hist, partner, *pieces)
+    )(flop_hist, partner, pieces)
     best = jnp.minimum(best[:, :HANDS], swap(best[:, HANDS:], "cent", 1))
     return best[0] + jnp.sum(jnp.square(flop_hist), axis=0)
 
@@ -312,17 +311,16 @@
 
     turn_part = turn_partial(turn_hist, turn_assign[None, :])
     own = jnp.concatenate([jnp.pad(flop_centers, ((0, 0), (0, LANES - PANEL))), turn_part], axis=0)
-    pieces = [own]
-    for mask in range(2, 16, 2):
-        pieces.append(swap(own, "cent", mask))
-
     place = jnp.concatenate([child_rows.reshape(TILES, TILE), jnp.zeros((2, TILE), i32)], axis=0)
     table = center_table(turn_centers)
-    place, table, scalars = lax.optimization_barrier((place, table, scalars))
+
+    own, place, table, scalars = lax.optimization_barrier((own, place, table, scalars))
+    copies = jnp.broadcast_to(own[None], (8,) + own.shape)
+    pieces = lax.all_to_all(copies, "cent", split_axis=0, concat_axis=0, tiled=True, axis_index_groups=CHIPS)
 
     flop_hist, keep, send = member(scalars, arrived, place, table, flop_assign[None, :])
 
-    turn_part = sum((piece[TURN_CENT:] for piece in pieces[1:]), turn_part)
+    turn_part = jnp.sum(pieces[:, TURN_CENT:], axis=0)
     turn_part = turn_part + swap(turn_part, "cent", 1)
     turn_part = turn_part + swap(turn_part, "board", 1)
     received, partner = lax.optimization_barrier((swap(send, "cent", 1), swap(flop_hist, "cent", 1)))

time: 145 us -> 116 us (0.80)
  waiting for transfers between devices: 70.2 us -> 42.2 us
  starting transfers between devices: 30.4 us -> 26.7 us
  other arithmetic: 3.42 us -> 5.27 us
    ppermute x16 -> x9, waiting for transfers between devices: 36.3 us -> 19.5 us  [swap(): return lax.ppermute(x, axis, [(i, i ^ mask) for i in range(size)])]
    all_to_all x1, waiting for transfers between devices: 33.9 us -> 20.1 us  [body(): lax.all_to_all(sent, ('board', 'cent'), split_axis=0, concat_axis=0, tile...]
    ppermute x16 -> x9, starting transfers between devices: 15.7 us -> 5.65 us  [swap(): return lax.ppermute(x, axis, [(i, i ^ mask) for i in range(size)])]
    all_to_all x0 -> x1, starting transfers between devices: none -> 4.25 us  [body(): lax.all_to_all(copies, 'cent', split_axis=0, concat_axis=0, tiled=True, a...]
    all_to_all x1, waiting for transfers between devices: 0.01 us -> 2.6 us  [body(): lax.all_to_all(half, 'cent', split_axis=0, concat_axis=0, tiled=True, axi...]
    all_to_all x1, starting transfers between devices: 3.55 us -> 5.59 us  [body(): lax.all_to_all(half, 'cent', split_axis=0, concat_axis=0, tiled=True, axi...]
  transfers between devices with their start and end apart: 18 -> 12, of which waited for: 11 -> 8; matrix products, arithmetic and copies ran while one was open for 2% -> 5% of each run, Pallas kernels for 11% -> 28%
where the time goes in v7:
time: 116 us; the launch traced here: 115 us
  waiting for transfers between devices  42.2 us (36%)
  Pallas kernels  36.4 us (31%)
  starting transfers between devices  26.7 us (23%)
  other arithmetic  5.27 us (5%)
  local copies, waits for them, and re-layouts  2.76 us (2%)
    all_to_all x1, waiting for transfers between devices, body(): lax.all_to_all(sent, ('board', 'cent'), split_axis=0, concat_axis=0, tile...  20.1 us
    ppermute x9, waiting for transfers between devices, swap(): return lax.ppermute(x, axis, [(i, i ^ mask) for i in range(size)])  19.5 us
    pallas_call x1, Pallas kernels, member(): pl.pallas_call(member_kernel, in_specs=[SMEM, VMEM, VMEM, VMEM, VMEM], ou...  14.9 us
    pallas_call x1, Pallas kernels, turn_partial(): pl.pallas_call(turn_kernel, grid=(steps,), in_specs=[pl.BlockSpec((BINS,...  12.2 us
    all_to_all x1, starting transfers between devices, body(): lax.all_to_all(sent, ('board', 'cent'), split_axis=0, concat_axis=0, tile...  11.2 us
    ppermute x9, starting transfers between devices, swap(): return lax.ppermute(x, axis, [(i, i ^ mask) for i in range(size)])  5.65 us
    all_to_all x1, starting transfers between devices, body(): lax.all_to_all(half, 'cent', split_axis=0, concat_axis=0, tiled=True, axi...  5.59 us
    pallas_call x1, Pallas kernels, nearest_of(): pl.pallas_call(nearest_kernel, in_specs=[VMEM, VMEM, VMEM], out_specs=VME...  4.85 us
  transfers between devices with their start and end apart: 12, of which 8 were waited for; matrix products, arithmetic and copies ran while one was open for 5% of the time, Pallas kernels for 28%

profile of v7, /device:TPU:0, one launch (start us, length us, event | category | flops | bytes accessed | tf_op | source)
XLA Modules:
  0.0 114.9 jit_solution(3314453247914927046)
XLA Ops:
  0.6 4.4 %pack.1 = bf16[128,80,128]{2,1,0:T(8,128)(2,1)} custom-call(bf16[50,24064]{1,0:T(8,128)(2,1)} %hist_ref.3), custom_call_target="tpu_custom_call" | custom-call | tf_op jit(solution)/shard_map/pack/pallas_call | solution.py:65
  5.0 11.2 %all-to-all-start = ((bf16[128,80,128]{2,1,0:T(8,128)(2,1)}), bf16[128,80,128]{2,1,0:T(8,128)(2,1)S(1)}, u32[]{:S(2)}, u32[]{:S(2)}) async-start(bf16[128,80,128]{2,1,0:T(8,128)(2,1)} %pack.1), calls=%async_computation | async-start | bytes 5242880 | tf_op jit(solution)/shard_map/all_to_all | solution.py:306
  17.7 0.7 broadcast_in_dim.14.label_ref
  18.5 12.2 %turn_sums.1 = f32[112,128]{1,0:T(8,128)} custom-call(bf16[50,24064]{1,0:T(8,128)(2,1)} %hist_ref.3, s32[1,24064]{1,0:T(1,128)} %broadcast_in_dim.14.label_ref), custom_call_target="tpu_custom_call" | custom-call | tf_op jit(solution)/shard_map/turn_sums/pallas_call | solution.py:99
  31.2 0.8 select_maximum_fusion
  32.1 20.1 %all-to-all-done.recv_ref = bf16[128,80,128]{2,1,0:T(8,128)(2,1)S(1)} async-done(((bf16[128,80,128]{2,1,0:T(8,128)(2,1)}), bf16[128,80,128]{2,1,0:T(8,128)(2,1)S(1)}, u32[]{:S(2)}, u32[]{:S(2)}) %all-to-all-start) | async-done | bytes 2621472 | tf_op jit(solution)/shard_map/all_to_all | solution.py:306
  52.2 1.1 broadcast_in_dim.35
  53.3 4.3 %all-to-all-start.1 = ((f32[8,312,128]{2,1,0:T(8,128)}), f32[8,312,128]{2,1,0:T(8,128)}, u32[]{:S(2)}, u32[]{:S(2)}) async-start(f32[8,312,128]{2,1,0:T(8,128)} %broadcast_in_dim.35), calls=%async_computation.1 | async-start | bytes 2555904 | tf_op jit(solution)/shard_map/all_to_all | solution.py:319
  57.6 14.9 %member.1 = (f32[200,512]{1,0:T(8,128)S(1)}, f32[8,200,128]{2,1,0:T(8,128)S(1)}, f32[8,200,128]{2,1,0:T(8,128)S(1)}) custom-call(s32[2]{0:T(128)S(1)} %pad_add_fusion.scalar_ref, bf16[128,80,128]{2,1,0:T(8,128)(2,1)S(1)} %all-to-all-done.recv_ref, s32[96,256]{1,0:T(8,128)S(1)} %concatenate.30.place_ref, bf16[264,192]{1,0:T(8,128)(2,1)S(1)} %pad_maximum_fusion.1.table_ref, ...), custom_call_target="tpu_custom_call" | custom-call | tf_op jit(solution)/shard_map/member/pallas_call | solution.py:224
  73.1 2.4 %collective-permute-done.1.partner_ref = f32[200,512]{1,0:T(8,128)S(1)} collective-permute-done((f32[200,512]{1,0:T(8,128)S(1)}, f32[200,512]{1,0:T(8,128)S(1)}, u32[]{:S(2)}, u32[]{:S(2)}) %collective-permute-start.1) | collective-permute-done | bytes 409632 | tf_op jit(solution)/shard_map/ppermute | solution.py:300
  75.5 1.0 add.77
  76.5 5.6 %all-to-all-start.2 = ((f32[8,200,128]{2,1,0:T(8,128)}), f32[8,200,128]{2,1,0:T(8,128)S(1)}, u32[]{:S(2)}, u32[]{:S(2)}) async-start(f32[8,200,128]{2,1,0:T(8,128)} %add.77), calls=%async_computation.2 | async-start | bytes 1638400 | tf_op jit(solution)/shard_map/all_to_all | solution.py:328
  82.1 1.1 slice_reduce_fusion
  83.3 1.2 %collective-permute-done.4 = f32[112,128]{1,0:T(8,128)S(1)} collective-permute-done((f32[112,128]{1,0:T(8,128)S(1)}, f32[112,128]{1,0:T(8,128)S(1)}, u32[]{:S(2)}, u32[]{:S(2)}) %collective-permute-start.4) | collective-permute-done | bytes 57376 | tf_op jit(solution)/shard_map/ppermute | solution.py:300
  84.5 0.7 collective-permute-start.5
  85.2 8.5 %collective-permute-done.5 = f32[112,128]{1,0:T(8,128)S(1)} collective-permute-done((f32[112,128]{1,0:T(8,128)S(1)}, f32[112,128]{1,0:T(8,128)S(1)}, u32[]{:S(2)}, u32[]{:S(2)}) %collective-permute-start.5) | collective-permute-done | bytes 57376 | tf_op jit(solution)/shard_map/ppermute | solution.py:300
  93.7 2.6 %all-to-all-done.2 = f32[8,200,128]{2,1,0:T(8,128)S(1)} async-done(((f32[8,200,128]{2,1,0:T(8,128)}), f32[8,200,128]{2,1,0:T(8,128)S(1)}, u32[]{:S(2)}, u32[]{:S(2)}) %all-to-all-start.2) | async-done | bytes 819232 | tf_op jit(solution)/shard_map/all_to_all | solution.py:328
  96.3 0.7 collective-permute-start.3
  97.0 4.8 %nearest.1 = f32[1,1024]{1,0:T(1,128)S(1)} custom-call(f32[200,512]{1,0:T(8,128)S(1)} %get-tuple-element.19.mine_ref, f32[200,512]{1,0:T(8,128)S(1)} %collective-permute-done.1.partner_ref, f32[8,312,128]{2,1,0:T(8,128)} %all-to-all-done.1.pieces_ref), custom_call_target="tpu_custom_call" | custom-call | tf_op jit(solution)/shard_map/nearest/pallas_call | solution.py:260
  102.6 0.7 collective-permute-start.7
  103.3 2.2 %collective-permute-start.8 = (f32[312,128]{1,0:T(8,128)S(1)}, f32[312,128]{1,0:T(8,128)S(1)}, u32[]{:S(2)}, u32[]{:S(2)}) collective-permute-start(f32[312,128]{1,0:T(8,128)S(1)} %pad_maximum_fusion), channel_id=1, source_target_pairs={{0,96},{16,112},{32,64},{48,80},{64,32},{80,48},{96,0},{112,16},{1... | collective-permute-start | bytes 479240 | tf_op jit(solution)/shard_map/ppermute | solution.py:300
  105.5 0.7 collective-permute-start.6
  106.8 4.4 %collective-permute-done.7 = f32[312,128]{1,0:T(8,128)S(1)} collective-permute-done((f32[312,128]{1,0:T(8,128)S(1)}, f32[312,128]{1,0:T(8,128)S(1)}, u32[]{:S(2)}, u32[]{:S(2)}) %collective-permute-start.7) | collective-permute-done | bytes 159776 | tf_op jit(solution)/shard_map/ppermute | solution.py:300
  111.2 2.4 %collective-permute-done.8 = f32[312,128]{1,0:T(8,128)S(1)} collective-permute-done((f32[312,128]{1,0:T(8,128)S(1)}, f32[312,128]{1,0:T(8,128)S(1)}, u32[]{:S(2)}, u32[]{:S(2)}) %collective-permute-start.8) | collective-permute-done | bytes 159776 | tf_op jit(solution)/shard_map/ppermute | solution.py:300
  (59 shorter events, 5.3 us)
Async XLA Ops:
  5.0 11.4 %copy-start.4 = (f32[50,200]{1,0:T(8,128)S(1)}, f32[50,200]{1,0:T(8,128)}, u32[]{:S(2)}) copy-start(f32[50,200]{1,0:T(8,128)} %param.9) | copy-start | bytes 120004
  5.0 11.7 %copy-start.2 = (s32[47,512]{1,0:T(8,128)S(1)}, s32[47,512]{1,0:T(8,128)}, u32[]{:S(2)}) copy-start(s32[47,512]{1,0:T(8,128)} %param.8) | copy-start | bytes 288772
  5.0 12.7 %copy-start.3 = (s32[24064]{0:T(1024)S(1)}, s32[24064]{0:T(1024)}, u32[]{:S(2)}) copy-start(s32[24064]{0:T(1024)} %param.7) | copy-start | bytes 288772
  5.0 47.2 %all-to-all-start = ((bf16[128,80,128]{2,1,0:T(8,128)(2,1)}), bf16[128,80,128]{2,1,0:T(8,128)(2,1)S(1)}, u32[]{:S(2)}, u32[]{:S(2)}) async-start(bf16[128,80,128]{2,1,0:T(8,128)(2,1)} %pack.1), calls=%async_computation | async-start | bytes 5242880 | tf_op jit(solution)/shard_map/all_to_all | solution.py:306
  17.0 14.2 %copy-start.1 = (f32[200,125]{1,0:T(8,128)S(1)}, f32[200,125]{1,0:T(8,128)}, u32[]{:S(2)}) copy-start(f32[200,125]{1,0:T(8,128)} %param.10) | copy-start | bytes 300004
  30.8 26.7 %copy-start = (s32[512]{0:T(512)S(1)}, s32[512]{0:T(512)}, u32[]{:S(2)}) copy-start(s32[512]{0:T(512)} %param.11) | copy-start | bytes 6148
  53.3 23.2 %all-to-all-start.1 = ((f32[8,312,128]{2,1,0:T(8,128)}), f32[8,312,128]{2,1,0:T(8,128)}, u32[]{:S(2)}, u32[]{:S(2)}) async-start(f32[8,312,128]{2,1,0:T(8,128)} %broadcast_in_dim.35), calls=%async_computation.1 | async-start | bytes 2555904 | tf_op jit(solution)/shard_map/all_to_all | solution.py:319
  72.5 3.0 %collective-permute-start = (f32[8,200,128]{2,1,0:T(8,128)S(1)}, f32[8,200,128]{2,1,0:T(8,128)S(1)}, u32[]{:S(2)}, u32[]{:S(2)}) collective-permute-start(f32[8,200,128]{2,1,0:T(8,128)S(1)} %get-tuple-element.20), channel_id=1, source_target_pairs={{0,1},{1,0},{2,3},{3,2},{4,5},{5,4},{6,7},{7,6},{8,9},{9,8},{10,11... | collective-permute-start | bytes 2457608 | tf_op jit(solution)/shard_map/ppermute | solution.py:300
  72.6 2.9 %collective-permute-start.1 = (f32[200,512]{1,0:T(8,128)S(1)}, f32[200,512]{1,0:T(8,128)S(1)}, u32[]{:S(2)}, u32[]{:S(2)}) collective-permute-start(f32[200,512]{1,0:T(8,128)S(1)} %get-tuple-element.19.mine_ref), channel_id=1, source_target_pairs={{0,1},{1,0},{2,3},{3,2},{4,5},{5,4},{6,7},{7,6},{8,9},{9,8},{10,11... | collective-permute-start | bytes 1228808 | tf_op jit(solution)/shard_map/ppermute | solution.py:300
  76.5 19.7 %all-to-all-start.2 = ((f32[8,200,128]{2,1,0:T(8,128)}), f32[8,200,128]{2,1,0:T(8,128)S(1)}, u32[]{:S(2)}, u32[]{:S(2)}) async-start(f32[8,200,128]{2,1,0:T(8,128)} %add.77), calls=%async_computation.2 | async-start | bytes 1638400 | tf_op jit(solution)/shard_map/all_to_all | solution.py:328
  83.2 1.3 %collective-permute-start.4 = (f32[112,128]{1,0:T(8,128)S(1)}, f32[112,128]{1,0:T(8,128)S(1)}, u32[]{:S(2)}, u32[]{:S(2)}) collective-permute-start(f32[112,128]{1,0:T(8,128)S(1)} %slice_reduce_fusion), channel_id=1, source_target_pairs={{0,1},{1,0},{2,3},{3,2},{4,5},{5,4},{6,7},{7,6},{8,9},{9,8},{10,11... | collective-permute-start | bytes 172040 | tf_op jit(solution)/shard_map/ppermute | solution.py:300
  84.5 9.2 %collective-permute-start.5 = (f32[112,128]{1,0:T(8,128)S(1)}, f32[112,128]{1,0:T(8,128)S(1)}, u32[]{:S(2)}, u32[]{:S(2)}) collective-permute-start(f32[112,128]{1,0:T(8,128)S(1)} %add.79), channel_id=1, source_target_pairs={{0,16},{16,0},{32,48},{48,32},{64,80},{80,64},{96,112},{112,96},{1... | collective-permute-start | bytes 172040 | tf_op jit(solution)/shard_map/ppermute | solution.py:300
  96.3 6.2 %collective-permute-start.3 = (f32[200,128]{1,0:T(8,128)S(1)}, f32[200,128]{1,0:T(8,128)S(1)}, u32[]{:S(2)}, u32[]{:S(2)}) collective-permute-start(f32[200,128]{1,0:T(8,128)S(1)} %reduce_sum.48), channel_id=1, source_target_pairs={{0,16},{16,0},{32,48},{48,32},{64,80},{80,64},{96,112},{112,96},{1... | collective-permute-start | bytes 307208 | tf_op jit(solution)/shard_map/ppermute | solution.py:300
  101.9 4.3 %collective-permute-start.2 = (f32[1,512]{1,0:T(1,128)S(1)}, f32[1,512]{1,0:T(1,128)S(1)}, u32[]{:S(2)}, u32[]{:S(2)}) collective-permute-start(f32[1,512]{1,0:T(1,128)S(1)} %slice.61), channel_id=1, source_target_pairs={{0,1},{1,0},{2,3},{3,2},{4,5},{5,4},{6,7},{7,6},{8,9},{9,8},{10,11... | collective-permute-start | bytes 6152 | tf_op jit(solution)/shard_map/ppermute | solution.py:300
  102.6 8.6 %collective-permute-start.7 = (f32[312,128]{1,0:T(8,128)S(1)}, f32[312,128]{1,0:T(8,128)S(1)}, u32[]{:S(2)}, u32[]{:S(2)}) collective-permute-start(f32[312,128]{1,0:T(8,128)S(1)} %pad_maximum_fusion), channel_id=1, source_target_pairs={{0,64},{16,80},{32,96},{48,112},{64,0},{80,16},{96,32},{112,48},{1... | collective-permute-start | bytes 479240 | tf_op jit(solution)/shard_map/ppermute | solution.py:300
  103.3 10.2 %collective-permute-start.8 = (f32[312,128]{1,0:T(8,128)S(1)}, f32[312,128]{1,0:T(8,128)S(1)}, u32[]{:S(2)}, u32[]{:S(2)}) collective-permute-start(f32[312,128]{1,0:T(8,128)S(1)} %pad_maximum_fusion), channel_id=1, source_target_pairs={{0,96},{16,112},{32,64},{48,80},{64,32},{80,48},{96,0},{112,16},{1... | collective-permute-start | bytes 479240 | tf_op jit(solution)/shard_map/ppermute | solution.py:300
  105.5 8.1 %collective-permute-start.6 = (f32[312,128]{1,0:T(8,128)S(1)}, f32[312,128]{1,0:T(8,128)S(1)}, u32[]{:S(2)}, u32[]{:S(2)}) collective-permute-start(f32[312,128]{1,0:T(8,128)S(1)} %pad_maximum_fusion), channel_id=1, source_target_pairs={{0,32},{16,48},{32,0},{48,16},{64,96},{80,112},{96,64},{112,80},{1... | collective-permute-start | bytes 479240 | tf_op jit(solution)/shard_map/ppermute | solution.py:300

commit v8 on v7

--- a/solution.py
+++ b/solution.py
@@ -323,8 +323,9 @@
     turn_part = jnp.sum(pieces[:, TURN_CENT:], axis=0)
     turn_part = turn_part + swap(turn_part, "cent", 1)
     turn_part = turn_part + swap(turn_part, "board", 1)
-    received, partner = lax.optimization_barrier((swap(send, "cent", 1), swap(flop_hist, "cent", 1)))
-    half = keep + received
+    half = keep + swap(send, "cent", 1)
+    flop_hist, half = lax.optimization_barrier((flop_hist, half))
+    partner = swap(flop_hist, "cent", 1)
     parts = lax.all_to_all(half, "cent", split_axis=0, concat_axis=0, tiled=True, axis_index_groups=CHIPS)
     flop_part = jnp.sum(parts, axis=0)
     flop_part = flop_part + swap(flop_part, "board", 1)

time: 116 us -> 116 us (level)
  no operation moved by 1% of the time
where the time goes in v8:
time: 116 us; the launch traced here: 114 us
  waiting for transfers between devices  41.7 us (36%)
  Pallas kernels  36.4 us (31%)
  starting transfers between devices  26.6 us (23%)
  other arithmetic  5.27 us (5%)
  local copies, waits for them, and re-layouts  2.76 us (2%)
    all_to_all x1, waiting for transfers between devices, body(): lax.all_to_all(sent, ('board', 'cent'), split_axis=0, concat_axis=0, tile...  20.1 us
    ppermute x9, waiting for transfers between devices, swap(): return lax.ppermute(x, axis, [(i, i ^ mask) for i in range(size)])  19 us
    pallas_call x1, Pallas kernels, member(): pl.pallas_call(member_kernel, in_specs=[SMEM, VMEM, VMEM, VMEM, VMEM], ou...  14.9 us
    pallas_call x1, Pallas kernels, turn_partial(): pl.pallas_call(turn_kernel, grid=(steps,), in_specs=[pl.BlockSpec((BINS,...  12.2 us
    all_to_all x1, starting transfers between devices, body(): lax.all_to_all(sent, ('board', 'cent'), split_axis=0, concat_axis=0, tile...  11.2 us
    ppermute x9, starting transfers between devices, swap(): return lax.ppermute(x, axis, [(i, i ^ mask) for i in range(size)])  5.6 us
    all_to_all x1, starting transfers between devices, body(): lax.all_to_all(half, 'cent', split_axis=0, concat_axis=0, tiled=True, axi...  5.59 us
    pallas_call x1, Pallas kernels, nearest_of(): pl.pallas_call(nearest_kernel, in_specs=[VMEM, VMEM, VMEM], out_specs=VME...  4.85 us
  transfers between devices with their start and end apart: 12, of which 8 were waited for; matrix products, arithmetic and copies ran while one was open for 5% of the time, Pallas kernels for 28%

profile of v8, /device:TPU:0, one launch (start us, length us, event | category | flops | bytes accessed | tf_op | source)
XLA Modules:
  0.0 114.3 jit_solution(17522613686947864944)
XLA Ops:
  0.6 4.4 %pack.1 = bf16[128,80,128]{2,1,0:T(8,128)(2,1)} custom-call(bf16[50,24064]{1,0:T(8,128)(2,1)} %hist_ref.3), custom_call_target="tpu_custom_call" | custom-call | tf_op jit(solution)/shard_map/pack/pallas_call | solution.py:65
  5.0 11.2 %all-to-all-start = ((bf16[128,80,128]{2,1,0:T(8,128)(2,1)}), bf16[128,80,128]{2,1,0:T(8,128)(2,1)S(1)}, u32[]{:S(2)}, u32[]{:S(2)}) async-start(bf16[128,80,128]{2,1,0:T(8,128)(2,1)} %pack.1), calls=%async_computation | async-start | bytes 5242880 | tf_op jit(solution)/shard_map/all_to_all | solution.py:306
  17.7 0.7 broadcast_in_dim.14.label_ref
  18.5 12.2 %turn_sums.1 = f32[112,128]{1,0:T(8,128)} custom-call(bf16[50,24064]{1,0:T(8,128)(2,1)} %hist_ref.3, s32[1,24064]{1,0:T(1,128)} %broadcast_in_dim.14.label_ref), custom_call_target="tpu_custom_call" | custom-call | tf_op jit(solution)/shard_map/turn_sums/pallas_call | solution.py:99
  31.2 0.8 select_maximum_fusion
  32.1 20.1 %all-to-all-done.recv_ref = bf16[128,80,128]{2,1,0:T(8,128)(2,1)S(1)} async-done(((bf16[128,80,128]{2,1,0:T(8,128)(2,1)}), bf16[128,80,128]{2,1,0:T(8,128)(2,1)S(1)}, u32[]{:S(2)}, u32[]{:S(2)}) %all-to-all-start) | async-done | bytes 2621472 | tf_op jit(solution)/shard_map/all_to_all | solution.py:306
  52.2 1.1 broadcast_in_dim.35
  53.3 4.3 %all-to-all-start.1 = ((f32[8,312,128]{2,1,0:T(8,128)}), f32[8,312,128]{2,1,0:T(8,128)}, u32[]{:S(2)}, u32[]{:S(2)}) async-start(f32[8,312,128]{2,1,0:T(8,128)} %broadcast_in_dim.35), calls=%async_computation.1 | async-start | bytes 2555904 | tf_op jit(solution)/shard_map/all_to_all | solution.py:319
  57.6 14.9 %member.1 = (f32[200,512]{1,0:T(8,128)S(1)}, f32[8,200,128]{2,1,0:T(8,128)S(1)}, f32[8,200,128]{2,1,0:T(8,128)S(1)}) custom-call(s32[2]{0:T(128)S(1)} %pad_add_fusion.scalar_ref, bf16[128,80,128]{2,1,0:T(8,128)(2,1)S(1)} %all-to-all-done.recv_ref, s32[96,256]{1,0:T(8,128)S(1)} %concatenate.30.place_ref, bf16[264,192]{1,0:T(8,128)(2,1)S(1)} %pad_maximum_fusion.1.table_ref, ...), custom_call_target="tpu_custom_call" | custom-call | tf_op jit(solution)/shard_map/member/pallas_call | solution.py:224
  72.6 2.3 %collective-permute-done = f32[8,200,128]{2,1,0:T(8,128)S(1)} collective-permute-done((f32[8,200,128]{2,1,0:T(8,128)S(1)}, f32[8,200,128]{2,1,0:T(8,128)S(1)}, u32[]{:S(2)}, u32[]{:S(2)}) %collective-permute-start) | collective-permute-done | bytes 819232 | tf_op jit(solution)/shard_map/ppermute | solution.py:300
  74.9 1.0 add.76
  75.9 5.6 %all-to-all-start.2 = ((f32[8,200,128]{2,1,0:T(8,128)}), f32[8,200,128]{2,1,0:T(8,128)S(1)}, u32[]{:S(2)}, u32[]{:S(2)}) async-start(f32[8,200,128]{2,1,0:T(8,128)} %add.76), calls=%async_computation.2 | async-start | bytes 1638400 | tf_op jit(solution)/shard_map/all_to_all | solution.py:329
  81.5 1.1 slice_reduce_fusion
  83.2 0.9 collective-permute-done.4
  84.7 8.4 %collective-permute-done.5 = f32[112,128]{1,0:T(8,128)S(1)} collective-permute-done((f32[112,128]{1,0:T(8,128)S(1)}, f32[112,128]{1,0:T(8,128)S(1)}, u32[]{:S(2)}, u32[]{:S(2)}) %collective-permute-start.5) | collective-permute-done | bytes 57376 | tf_op jit(solution)/shard_map/ppermute | solution.py:300
  93.1 2.6 %all-to-all-done.2 = f32[8,200,128]{2,1,0:T(8,128)S(1)} async-done(((f32[8,200,128]{2,1,0:T(8,128)}), f32[8,200,128]{2,1,0:T(8,128)S(1)}, u32[]{:S(2)}, u32[]{:S(2)}) %all-to-all-start.2) | async-done | bytes 819232 | tf_op jit(solution)/shard_map/all_to_all | solution.py:329
  95.7 0.7 collective-permute-start.3
  96.5 4.8 %nearest.1 = f32[1,1024]{1,0:T(1,128)S(1)} custom-call(f32[200,512]{1,0:T(8,128)S(1)} %get-tuple-element.22.mine_ref, f32[200,512]{1,0:T(8,128)S(1)} %collective-permute-done.1.partner_ref, f32[8,312,128]{2,1,0:T(8,128)} %all-to-all-done.1.pieces_ref), custom_call_target="tpu_custom_call" | custom-call | tf_op jit(solution)/shard_map/nearest/pallas_call | solution.py:260
  102.0 0.7 collective-permute-start.7
  102.7 2.2 %collective-permute-start.8 = (f32[312,128]{1,0:T(8,128)S(1)}, f32[312,128]{1,0:T(8,128)S(1)}, u32[]{:S(2)}, u32[]{:S(2)}) collective-permute-start(f32[312,128]{1,0:T(8,128)S(1)} %pad_maximum_fusion), channel_id=1, source_target_pairs={{0,96},{16,112},{32,64},{48,80},{64,32},{80,48},{96,0},{112,16},{1... | collective-permute-start | bytes 479240 | tf_op jit(solution)/shard_map/ppermute | solution.py:300
  104.9 0.7 collective-permute-start.6
  106.2 4.4 %collective-permute-done.7 = f32[312,128]{1,0:T(8,128)S(1)} collective-permute-done((f32[312,128]{1,0:T(8,128)S(1)}, f32[312,128]{1,0:T(8,128)S(1)}, u32[]{:S(2)}, u32[]{:S(2)}) %collective-permute-start.7) | collective-permute-done | bytes 159776 | tf_op jit(solution)/shard_map/ppermute | solution.py:300
  110.6 2.4 %collective-permute-done.8 = f32[312,128]{1,0:T(8,128)S(1)} collective-permute-done((f32[312,128]{1,0:T(8,128)S(1)}, f32[312,128]{1,0:T(8,128)S(1)}, u32[]{:S(2)}, u32[]{:S(2)}) %collective-permute-start.8) | collective-permute-done | bytes 159776 | tf_op jit(solution)/shard_map/ppermute | solution.py:300
  113.0 0.7 fusion.1
  (59 shorter events, 5.3 us)
Async XLA Ops:
  5.0 11.4 %copy-start.4 = (f32[50,200]{1,0:T(8,128)S(1)}, f32[50,200]{1,0:T(8,128)}, u32[]{:S(2)}) copy-start(f32[50,200]{1,0:T(8,128)} %param.9) | copy-start | bytes 120004
  5.0 11.7 %copy-start.2 = (s32[47,512]{1,0:T(8,128)S(1)}, s32[47,512]{1,0:T(8,128)}, u32[]{:S(2)}) copy-start(s32[47,512]{1,0:T(8,128)} %param.8) | copy-start | bytes 288772
  5.0 12.7 %copy-start.3 = (s32[24064]{0:T(1024)S(1)}, s32[24064]{0:T(1024)}, u32[]{:S(2)}) copy-start(s32[24064]{0:T(1024)} %param.7) | copy-start | bytes 288772
  5.0 47.2 %all-to-all-start = ((bf16[128,80,128]{2,1,0:T(8,128)(2,1)}), bf16[128,80,128]{2,1,0:T(8,128)(2,1)S(1)}, u32[]{:S(2)}, u32[]{:S(2)}) async-start(bf16[128,80,128]{2,1,0:T(8,128)(2,1)} %pack.1), calls=%async_computation | async-start | bytes 5242880 | tf_op jit(solution)/shard_map/all_to_all | solution.py:306
  17.0 14.2 %copy-start.1 = (f32[200,125]{1,0:T(8,128)S(1)}, f32[200,125]{1,0:T(8,128)}, u32[]{:S(2)}) copy-start(f32[200,125]{1,0:T(8,128)} %param.10) | copy-start | bytes 300004
  30.8 26.7 %copy-start = (s32[512]{0:T(512)S(1)}, s32[512]{0:T(512)}, u32[]{:S(2)}) copy-start(s32[512]{0:T(512)} %param.11) | copy-start | bytes 6148
  53.3 22.6 %all-to-all-start.1 = ((f32[8,312,128]{2,1,0:T(8,128)}), f32[8,312,128]{2,1,0:T(8,128)}, u32[]{:S(2)}, u32[]{:S(2)}) async-start(f32[8,312,128]{2,1,0:T(8,128)} %broadcast_in_dim.35), calls=%async_computation.1 | async-start | bytes 2555904 | tf_op jit(solution)/shard_map/all_to_all | solution.py:319
  72.5 2.4 %collective-permute-start = (f32[8,200,128]{2,1,0:T(8,128)S(1)}, f32[8,200,128]{2,1,0:T(8,128)S(1)}, u32[]{:S(2)}, u32[]{:S(2)}) collective-permute-start(f32[8,200,128]{2,1,0:T(8,128)S(1)} %get-tuple-element.21), channel_id=1, source_target_pairs={{0,1},{1,0},{2,3},{3,2},{4,5},{5,4},{6,7},{7,6},{8,9},{9,8},{10,11... | collective-permute-start | bytes 2457608 | tf_op jit(solution)/shard_map/ppermute | solution.py:300
  75.9 19.7 %all-to-all-start.2 = ((f32[8,200,128]{2,1,0:T(8,128)}), f32[8,200,128]{2,1,0:T(8,128)S(1)}, u32[]{:S(2)}, u32[]{:S(2)}) async-start(f32[8,200,128]{2,1,0:T(8,128)} %add.76), calls=%async_computation.2 | async-start | bytes 1638400 | tf_op jit(solution)/shard_map/all_to_all | solution.py:329
  81.5 14.9 %collective-permute-start.1 = (f32[200,512]{1,0:T(8,128)S(1)}, f32[200,512]{1,0:T(8,128)S(1)}, u32[]{:S(2)}, u32[]{:S(2)}) collective-permute-start(f32[200,512]{1,0:T(8,128)S(1)} %get-tuple-element.22.mine_ref), channel_id=1, source_target_pairs={{0,1},{1,0},{2,3},{3,2},{4,5},{5,4},{6,7},{7,6},{8,9},{9,8},{10,11... | collective-permute-start | bytes 1228808 | tf_op jit(solution)/shard_map/ppermute | solution.py:300
  82.6 1.5 %collective-permute-start.4 = (f32[112,128]{1,0:T(8,128)S(1)}, f32[112,128]{1,0:T(8,128)S(1)}, u32[]{:S(2)}, u32[]{:S(2)}) collective-permute-start(f32[112,128]{1,0:T(8,128)S(1)} %slice_reduce_fusion), channel_id=1, source_target_pairs={{0,1},{1,0},{2,3},{3,2},{4,5},{5,4},{6,7},{7,6},{8,9},{9,8},{10,11... | collective-permute-start | bytes 172040 | tf_op jit(solution)/shard_map/ppermute | solution.py:300
  84.1 9.0 %collective-permute-start.5 = (f32[112,128]{1,0:T(8,128)S(1)}, f32[112,128]{1,0:T(8,128)S(1)}, u32[]{:S(2)}, u32[]{:S(2)}) collective-permute-start(f32[112,128]{1,0:T(8,128)S(1)} %add.79), channel_id=1, source_target_pairs={{0,16},{16,0},{32,48},{48,32},{64,80},{80,64},{96,112},{112,96},{1... | collective-permute-start | bytes 172040 | tf_op jit(solution)/shard_map/ppermute | solution.py:300
  95.7 6.2 %collective-permute-start.3 = (f32[200,128]{1,0:T(8,128)S(1)}, f32[200,128]{1,0:T(8,128)S(1)}, u32[]{:S(2)}, u32[]{:S(2)}) collective-permute-start(f32[200,128]{1,0:T(8,128)S(1)} %reduce_sum.48), channel_id=1, source_target_pairs={{0,16},{16,0},{32,48},{48,32},{64,80},{80,64},{96,112},{112,96},{1... | collective-permute-start | bytes 307208 | tf_op jit(solution)/shard_map/ppermute | solution.py:300
  101.3 4.3 %collective-permute-start.2 = (f32[1,512]{1,0:T(1,128)S(1)}, f32[1,512]{1,0:T(1,128)S(1)}, u32[]{:S(2)}, u32[]{:S(2)}) collective-permute-start(f32[1,512]{1,0:T(1,128)S(1)} %slice.61), channel_id=1, source_target_pairs={{0,1},{1,0},{2,3},{3,2},{4,5},{5,4},{6,7},{7,6},{8,9},{9,8},{10,11... | collective-permute-start | bytes 6152 | tf_op jit(solution)/shard_map/ppermute | solution.py:300
  102.0 8.6 %collective-permute-start.7 = (f32[312,128]{1,0:T(8,128)S(1)}, f32[312,128]{1,0:T(8,128)S(1)}, u32[]{:S(2)}, u32[]{:S(2)}) collective-permute-start(f32[312,128]{1,0:T(8,128)S(1)} %pad_maximum_fusion), channel_id=1, source_target_pairs={{0,64},{16,80},{32,96},{48,112},{64,0},{80,16},{96,32},{112,48},{1... | collective-permute-start | bytes 479240 | tf_op jit(solution)/shard_map/ppermute | solution.py:300
  102.7 10.2 %collective-permute-start.8 = (f32[312,128]{1,0:T(8,128)S(1)}, f32[312,128]{1,0:T(8,128)S(1)}, u32[]{:S(2)}, u32[]{:S(2)}) collective-permute-start(f32[312,128]{1,0:T(8,128)S(1)} %pad_maximum_fusion), channel_id=1, source_target_pairs={{0,96},{16,112},{32,64},{48,80},{64,32},{80,48},{96,0},{112,16},{1... | collective-permute-start | bytes 479240 | tf_op jit(solution)/shard_map/ppermute | solution.py:300
  104.9 8.1 %collective-permute-start.6 = (f32[312,128]{1,0:T(8,128)S(1)}, f32[312,128]{1,0:T(8,128)S(1)}, u32[]{:S(2)}, u32[]{:S(2)}) collective-permute-start(f32[312,128]{1,0:T(8,128)S(1)} %pad_maximum_fusion), channel_id=1, source_target_pairs={{0,32},{16,48},{32,0},{48,16},{64,96},{80,112},{96,64},{112,80},{1... | collective-permute-start | bytes 479240 | tf_op jit(solution)/shard_map/ppermute | solution.py:300

commit v9 on v8

--- a/solution.py
+++ b/solution.py
@@ -32,14 +32,15 @@
     return table
 
 
-def pack_kernel(hist_ref, out_ref):
+def pack_kernel(ref0, ref1, ref2, ref3, out_ref):
+    groups = (ref0, ref1, ref2, ref3)
     lane = lax.broadcasted_iota(i32, (16, LANES), 1)
     for d in range(SOURCES_PER_STEP):
         t0, o = divmod(BLOCK * d, LANES)
         three = o + BLOCK > 2 * LANES
 
         def parts(lo, hi):
-            tiles = [hist_ref[lo:hi, (t0 + t) * LANES:(t0 + t + 1) * LANES].astype(f32)
+            tiles = [groups[lo // 16][0:hi - lo, (t0 + t) * LANES:(t0 + t + 1) * LANES].astype(f32)
                      for t in range(3 if three else 2)]
             upper = lane[:hi - lo] >= o
             a = jnp.where(upper, tiles[0], tiles[1]) if o else tiles[0]
@@ -65,11 +66,11 @@
     return pl.pallas_call(
         pack_kernel,
         grid=(DEVICES // SOURCES_PER_STEP,),
-        in_specs=[pl.BlockSpec((BINS, width), lambda i: (0, i))],
+        in_specs=[pl.BlockSpec((16, width), lambda i, g=g: (g, i)) for g in range(4)],
         out_specs=pl.BlockSpec((SOURCES_PER_STEP, PACK_ROWS, LANES), lambda i: (i, 0, 0)),
         out_shape=jax.ShapeDtypeStruct((DEVICES, PACK_ROWS, LANES), bf16),
         name="pack",
-    )(turn_hist)
+    )(turn_hist, turn_hist, turn_hist, turn_hist)
 
 
 def turn_kernel(hist_ref, label_ref, out_ref):
@@ -300,6 +301,27 @@
     return lax.ppermute(x, axis, [(i, i ^ mask) for i in range(size)])
 
 
+def finish(first, second, third, fourth, flop_scale, turn_scale):
+    def kernel(a_ref, b_ref, c_ref, d_ref, flop_ref, turn_ref):
+        total = (a_ref[...] + b_ref[...]) + (c_ref[...] + d_ref[...])
+        flop_ref[...] = total[:TURN_CENT, :PANEL] * flop_scale
+        turn = total[TURN_CENT:] * turn_scale
+        turn_ref[:, :LANES] = turn[:BINS]
+        turn_ref[:, LANES:] = turn[TURN_SPLIT:TURN_SPLIT + BINS, :TURN_CENT - LANES]
+
+    return pl.pallas_call(
+        kernel,
+        in_specs=[VMEM] * 4,
+        out_specs=[VMEM] * 2,
+        out_shape=[
+            jax.ShapeDtypeStruct((TURN_CENT, PANEL), f32),
+            jax.ShapeDtypeStruct((BINS, TURN_CENT), f32),
+        ],
+        compiler_params=pltpu.CompilerParams(vmem_limit_bytes=8 * 1024 * 1024),
+        name="finish",
+    )(first, second, third, fourth)
+
+
 def body(turn_hist, turn_assign, child_rows, turn_centers, flop_centers, flop_assign):
     sent = pack(turn_hist)
     turn_assign, sent = lax.optimization_barrier((turn_assign, sent))
@@ -330,12 +352,10 @@
     flop_part = jnp.sum(parts, axis=0)
     flop_part = flop_part + swap(flop_part, "board", 1)
     total = jnp.concatenate([flop_part, turn_part], axis=0)
-    total = (total + swap(total, "board", 2)) + (swap(total, "board", 4) + swap(total, "board", 6))
-    flop_sums = total[:TURN_CENT, :PANEL].T * (PANEL * 16 / (HANDS * DEVICES))
-    turn_low = total[TURN_CENT:TURN_CENT + BINS]
-    turn_high = total[TURN_CENT + TURN_SPLIT:TURN_CENT + TURN_SPLIT + BINS, :TURN_CENT - LANES]
-    turn_sums = jnp.concatenate([turn_low, turn_high], axis=1)
-    turn_sums = turn_sums * (BINS * TURN_CENT / (turn_hist.shape[1] * DEVICES))
+    flop_sums, turn_sums = finish(
+        total, swap(total, "board", 2), swap(total, "board", 4), swap(total, "board", 6),
+        PANEL * 16 / (HANDS * DEVICES), BINS * TURN_CENT / (turn_hist.shape[1] * DEVICES))
+    flop_sums = flop_sums.T
 
     nearest = nearest_of(pieces, flop_hist, partner)
     return nearest, turn_sums, flop_sums

time: 116 us -> 115 us (level)
  other arithmetic: 5.27 us -> 3.95 us
    mul x2 -> x0, other arithmetic: 1.28 us -> none  [the longest x1 0.65 us: body(): flop_sums = total[:TURN_CENT, :PANEL].T * (PANEL * 16 / (HANDS * DEVICES))]
where the time goes in v9:
time: 115 us; the launch traced here: 114 us
  waiting for transfers between devices  41.4 us (36%)
  Pallas kernels  37.2 us (32%)
  starting transfers between devices  27.2 us (24%)
  other arithmetic  3.95 us (3%)
  local copies, waits for them, and re-layouts  2.75 us (2%)
    all_to_all x1, waiting for transfers between devices, body(): lax.all_to_all(sent, ('board', 'cent'), split_axis=0, concat_axis=0, tile...  20.1 us
    ppermute x9, waiting for transfers between devices, swap(): return lax.ppermute(x, axis, [(i, i ^ mask) for i in range(size)])  18.7 us
    pallas_call x1, Pallas kernels, member(): pl.pallas_call(member_kernel, in_specs=[SMEM, VMEM, VMEM, VMEM, VMEM], ou...  14.9 us
    pallas_call x1, Pallas kernels, turn_partial(): pl.pallas_call(turn_kernel, grid=(steps,), in_specs=[pl.BlockSpec((BINS,...  12.2 us
    all_to_all x1, starting transfers between devices, body(): lax.all_to_all(sent, ('board', 'cent'), split_axis=0, concat_axis=0, tile...  11.2 us
    ppermute x9, starting transfers between devices, swap(): return lax.ppermute(x, axis, [(i, i ^ mask) for i in range(size)])  6.19 us
    all_to_all x1, starting transfers between devices, body(): lax.all_to_all(half, 'cent', split_axis=0, concat_axis=0, tiled=True, axi...  5.59 us
    pallas_call x1, Pallas kernels, nearest_of(): pl.pallas_call(nearest_kernel, in_specs=[VMEM, VMEM, VMEM], out_specs=VME...  4.85 us
  transfers between devices with their start and end apart: 12, of which 8 were waited for; matrix products, arithmetic and copies ran while one was open for 5% of the time, Pallas kernels for 28%

profile of v9, /device:TPU:0, one launch (start us, length us, event | category | flops | bytes accessed | tf_op | source)
XLA Modules:
  0.0 114.1 jit_solution(11821085765637155466)
XLA Ops:
  0.6 4.5 %pack.1 = bf16[128,80,128]{2,1,0:T(8,128)(2,1)} custom-call(bf16[50,24064]{1,0:T(8,128)(2,1)} %hist_ref.1, bf16[50,24064]{1,0:T(8,128)(2,1)} %hist_ref.1, bf16[50,24064]{1,0:T(8,128)(2,1)} %hist_ref.1, bf16[50,24064]{1,0:T(8,128)(2,1)} %hist_ref.1), custom_call_target="tpu_custom_call" | custom-call | tf_op jit(solution)/shard_map/pack/pallas_call | solution.py:66
  5.1 11.2 %all-to-all-start = ((bf16[128,80,128]{2,1,0:T(8,128)(2,1)}), bf16[128,80,128]{2,1,0:T(8,128)(2,1)S(1)}, u32[]{:S(2)}, u32[]{:S(2)}) async-start(bf16[128,80,128]{2,1,0:T(8,128)(2,1)} %pack.1), calls=%async_computation | async-start | bytes 5242880 | tf_op jit(solution)/shard_map/all_to_all | solution.py:328
  17.8 0.7 broadcast_in_dim.14.label_ref
  18.5 12.2 %turn_sums.1 = f32[112,128]{1,0:T(8,128)} custom-call(bf16[50,24064]{1,0:T(8,128)(2,1)} %hist_ref.1, s32[1,24064]{1,0:T(1,128)} %broadcast_in_dim.14.label_ref), custom_call_target="tpu_custom_call" | custom-call | tf_op jit(solution)/shard_map/turn_sums/pallas_call | solution.py:100
  31.3 0.8 select_maximum_fusion
  32.1 20.1 %all-to-all-done.recv_ref = bf16[128,80,128]{2,1,0:T(8,128)(2,1)S(1)} async-done(((bf16[128,80,128]{2,1,0:T(8,128)(2,1)}), bf16[128,80,128]{2,1,0:T(8,128)(2,1)S(1)}, u32[]{:S(2)}, u32[]{:S(2)}) %all-to-all-start) | async-done | bytes 2621472 | tf_op jit(solution)/shard_map/all_to_all | solution.py:328
  52.3 1.1 broadcast_in_dim.35
  53.4 4.3 %all-to-all-start.1 = ((f32[8,312,128]{2,1,0:T(8,128)}), f32[8,312,128]{2,1,0:T(8,128)}, u32[]{:S(2)}, u32[]{:S(2)}) async-start(f32[8,312,128]{2,1,0:T(8,128)} %broadcast_in_dim.35), calls=%async_computation.1 | async-start | bytes 2555904 | tf_op jit(solution)/shard_map/all_to_all | solution.py:341
  57.7 14.9 %member.1 = (f32[200,512]{1,0:T(8,128)S(1)}, f32[8,200,128]{2,1,0:T(8,128)S(1)}, f32[8,200,128]{2,1,0:T(8,128)S(1)}) custom-call(s32[2]{0:T(128)S(1)} %pad_add_fusion.scalar_ref, bf16[128,80,128]{2,1,0:T(8,128)(2,1)S(1)} %all-to-all-done.recv_ref, s32[96,256]{1,0:T(8,128)S(1)} %concatenate.27.place_ref, bf16[264,192]{1,0:T(8,128)(2,1)S(1)} %pad_maximum_fusion.1.table_ref, ...), custom_call_target="tpu_custom_call" | custom-call | tf_op jit(solution)/shard_map/member/pallas_call | solution.py:225
  72.7 2.3 %collective-permute-done = f32[8,200,128]{2,1,0:T(8,128)S(1)} collective-permute-done((f32[8,200,128]{2,1,0:T(8,128)S(1)}, f32[8,200,128]{2,1,0:T(8,128)S(1)}, u32[]{:S(2)}, u32[]{:S(2)}) %collective-permute-start) | collective-permute-done | bytes 819232 | tf_op jit(solution)/shard_map/ppermute | solution.py:301
  75.0 1.0 add.67
  76.0 5.6 %all-to-all-start.2 = ((f32[8,200,128]{2,1,0:T(8,128)}), f32[8,200,128]{2,1,0:T(8,128)S(1)}, u32[]{:S(2)}, u32[]{:S(2)}) async-start(f32[8,200,128]{2,1,0:T(8,128)} %add.67), calls=%async_computation.2 | async-start | bytes 1638400 | tf_op jit(solution)/shard_map/all_to_all | solution.py:351
  81.6 1.1 slice_reduce_fusion
  83.3 0.9 collective-permute-done.4
  84.8 8.4 %collective-permute-done.5 = f32[112,128]{1,0:T(8,128)S(1)} collective-permute-done((f32[112,128]{1,0:T(8,128)S(1)}, f32[112,128]{1,0:T(8,128)S(1)}, u32[]{:S(2)}, u32[]{:S(2)}) %collective-permute-start.5) | collective-permute-done | bytes 57376 | tf_op jit(solution)/shard_map/ppermute | solution.py:301
  93.2 2.6 %all-to-all-done.2 = f32[8,200,128]{2,1,0:T(8,128)S(1)} async-done(((f32[8,200,128]{2,1,0:T(8,128)}), f32[8,200,128]{2,1,0:T(8,128)S(1)}, u32[]{:S(2)}, u32[]{:S(2)}) %all-to-all-start.2) | async-done | bytes 819232 | tf_op jit(solution)/shard_map/all_to_all | solution.py:351
  95.8 0.7 collective-permute-start.3
  96.5 4.8 %nearest.1 = f32[1,1024]{1,0:T(1,128)S(1)} custom-call(f32[200,512]{1,0:T(8,128)S(1)} %get-tuple-element.24.mine_ref, f32[200,512]{1,0:T(8,128)S(1)} %collective-permute-done.1.partner_ref, f32[8,312,128]{2,1,0:T(8,128)} %all-to-all-done.1.pieces_ref), custom_call_target="tpu_custom_call" | custom-call | tf_op jit(solution)/shard_map/nearest/pallas_call | solution.py:261
  102.1 0.7 collective-permute-start.8
  102.8 1.6 %collective-permute-start.7 = (f32[312,128]{1,0:T(8,128)S(1)}, f32[312,128]{1,0:T(8,128)S(1)}, u32[]{:S(2)}, u32[]{:S(2)}) collective-permute-start(f32[312,128]{1,0:T(8,128)S(1)} %pad_maximum_fusion.a_ref), channel_id=1, source_target_pairs={{0,64},{16,80},{32,96},{48,112},{64,0},{80,16},{96,32},{112,48},{1... | collective-permute-start | bytes 479240 | tf_op jit(solution)/shard_map/ppermute | solution.py:301
  104.4 1.9 %collective-permute-start.6 = (f32[312,128]{1,0:T(8,128)S(1)}, f32[312,128]{1,0:T(8,128)S(1)}, u32[]{:S(2)}, u32[]{:S(2)}) collective-permute-start(f32[312,128]{1,0:T(8,128)S(1)} %pad_maximum_fusion.a_ref), channel_id=1, source_target_pairs={{0,32},{16,48},{32,0},{48,16},{64,96},{80,112},{96,64},{112,80},{1... | collective-permute-start | bytes 479240 | tf_op jit(solution)/shard_map/ppermute | solution.py:301
  106.9 5.9 %collective-permute-done.8.d_ref = f32[312,128]{1,0:T(8,128)S(1)} collective-permute-done((f32[312,128]{1,0:T(8,128)S(1)}, f32[312,128]{1,0:T(8,128)S(1)}, u32[]{:S(2)}, u32[]{:S(2)}) %collective-permute-start.8) | collective-permute-done | bytes 159776 | tf_op jit(solution)/shard_map/ppermute | solution.py:301
  112.8 0.6 collective-permute-done.6.b_ref
  113.4 0.7 finish.1
  (55 shorter events, 4.6 us)
Async XLA Ops:
  5.1 11.4 %copy-start.4 = (f32[50,200]{1,0:T(8,128)S(1)}, f32[50,200]{1,0:T(8,128)}, u32[]{:S(2)}) copy-start(f32[50,200]{1,0:T(8,128)} %param.9) | copy-start | bytes 120004
  5.1 11.7 %copy-start.2 = (s32[47,512]{1,0:T(8,128)S(1)}, s32[47,512]{1,0:T(8,128)}, u32[]{:S(2)}) copy-start(s32[47,512]{1,0:T(8,128)} %param.8) | copy-start | bytes 288772
  5.1 12.7 %copy-start.3 = (s32[24064]{0:T(1024)S(1)}, s32[24064]{0:T(1024)}, u32[]{:S(2)}) copy-start(s32[24064]{0:T(1024)} %param.7) | copy-start | bytes 288772
  5.1 47.2 %all-to-all-start = ((bf16[128,80,128]{2,1,0:T(8,128)(2,1)}), bf16[128,80,128]{2,1,0:T(8,128)(2,1)S(1)}, u32[]{:S(2)}, u32[]{:S(2)}) async-start(bf16[128,80,128]{2,1,0:T(8,128)(2,1)} %pack.1), calls=%async_computation | async-start | bytes 5242880 | tf_op jit(solution)/shard_map/all_to_all | solution.py:328
  17.1 14.2 %copy-start.1 = (f32[200,125]{1,0:T(8,128)S(1)}, f32[200,125]{1,0:T(8,128)}, u32[]{:S(2)}) copy-start(f32[200,125]{1,0:T(8,128)} %param.10) | copy-start | bytes 300004
  30.9 26.8 %copy-start = (s32[512]{0:T(512)S(1)}, s32[512]{0:T(512)}, u32[]{:S(2)}) copy-start(s32[512]{0:T(512)} %param.11) | copy-start | bytes 6148
  53.4 22.6 %all-to-all-start.1 = ((f32[8,312,128]{2,1,0:T(8,128)}), f32[8,312,128]{2,1,0:T(8,128)}, u32[]{:S(2)}, u32[]{:S(2)}) async-start(f32[8,312,128]{2,1,0:T(8,128)} %broadcast_in_dim.35), calls=%async_computation.1 | async-start | bytes 2555904 | tf_op jit(solution)/shard_map/all_to_all | solution.py:341
  72.6 2.4 %collective-permute-start = (f32[8,200,128]{2,1,0:T(8,128)S(1)}, f32[8,200,128]{2,1,0:T(8,128)S(1)}, u32[]{:S(2)}, u32[]{:S(2)}) collective-permute-start(f32[8,200,128]{2,1,0:T(8,128)S(1)} %get-tuple-element.23), channel_id=1, source_target_pairs={{0,1},{1,0},{2,3},{3,2},{4,5},{5,4},{6,7},{7,6},{8,9},{9,8},{10,11... | collective-permute-start | bytes 2457608 | tf_op jit(solution)/shard_map/ppermute | solution.py:301
  76.0 19.7 %all-to-all-start.2 = ((f32[8,200,128]{2,1,0:T(8,128)}), f32[8,200,128]{2,1,0:T(8,128)S(1)}, u32[]{:S(2)}, u32[]{:S(2)}) async-start(f32[8,200,128]{2,1,0:T(8,128)} %add.67), calls=%async_computation.2 | async-start | bytes 1638400 | tf_op jit(solution)/shard_map/all_to_all | solution.py:351
  81.6 14.9 %collective-permute-start.1 = (f32[200,512]{1,0:T(8,128)S(1)}, f32[200,512]{1,0:T(8,128)S(1)}, u32[]{:S(2)}, u32[]{:S(2)}) collective-permute-start(f32[200,512]{1,0:T(8,128)S(1)} %get-tuple-element.24.mine_ref), channel_id=1, source_target_pairs={{0,1},{1,0},{2,3},{3,2},{4,5},{5,4},{6,7},{7,6},{8,9},{9,8},{10,11... | collective-permute-start | bytes 1228808 | tf_op jit(solution)/shard_map/ppermute | solution.py:301
  82.7 1.5 %collective-permute-start.4 = (f32[112,128]{1,0:T(8,128)S(1)}, f32[112,128]{1,0:T(8,128)S(1)}, u32[]{:S(2)}, u32[]{:S(2)}) collective-permute-start(f32[112,128]{1,0:T(8,128)S(1)} %slice_reduce_fusion), channel_id=1, source_target_pairs={{0,1},{1,0},{2,3},{3,2},{4,5},{5,4},{6,7},{7,6},{8,9},{9,8},{10,11... | collective-permute-start | bytes 172040 | tf_op jit(solution)/shard_map/ppermute | solution.py:301
  84.2 9.0 %collective-permute-start.5 = (f32[112,128]{1,0:T(8,128)S(1)}, f32[112,128]{1,0:T(8,128)S(1)}, u32[]{:S(2)}, u32[]{:S(2)}) collective-permute-start(f32[112,128]{1,0:T(8,128)S(1)} %add.70), channel_id=1, source_target_pairs={{0,16},{16,0},{32,48},{48,32},{64,80},{80,64},{96,112},{112,96},{1... | collective-permute-start | bytes 172040 | tf_op jit(solution)/shard_map/ppermute | solution.py:301
  95.8 6.2 %collective-permute-start.3 = (f32[200,128]{1,0:T(8,128)S(1)}, f32[200,128]{1,0:T(8,128)S(1)}, u32[]{:S(2)}, u32[]{:S(2)}) collective-permute-start(f32[200,128]{1,0:T(8,128)S(1)} %reduce_sum.48), channel_id=1, source_target_pairs={{0,16},{16,0},{32,48},{48,32},{64,80},{80,64},{96,112},{112,96},{1... | collective-permute-start | bytes 307208 | tf_op jit(solution)/shard_map/ppermute | solution.py:301
  101.4 4.9 %collective-permute-start.2 = (f32[1,512]{1,0:T(1,128)S(1)}, f32[1,512]{1,0:T(1,128)S(1)}, u32[]{:S(2)}, u32[]{:S(2)}) collective-permute-start(f32[1,512]{1,0:T(1,128)S(1)} %slice.49), channel_id=1, source_target_pairs={{0,1},{1,0},{2,3},{3,2},{4,5},{5,4},{6,7},{7,6},{8,9},{9,8},{10,11... | collective-permute-start | bytes 6152 | tf_op jit(solution)/shard_map/ppermute | solution.py:301
  102.1 10.7 %collective-permute-start.8 = (f32[312,128]{1,0:T(8,128)S(1)}, f32[312,128]{1,0:T(8,128)S(1)}, u32[]{:S(2)}, u32[]{:S(2)}) collective-permute-start(f32[312,128]{1,0:T(8,128)S(1)} %pad_maximum_fusion.a_ref), channel_id=1, source_target_pairs={{0,96},{16,112},{32,64},{48,80},{64,32},{80,48},{96,0},{112,16},{1... | collective-permute-start | bytes 479240 | tf_op jit(solution)/shard_map/ppermute | solution.py:301
  102.8 10.0 %collective-permute-start.7 = (f32[312,128]{1,0:T(8,128)S(1)}, f32[312,128]{1,0:T(8,128)S(1)}, u32[]{:S(2)}, u32[]{:S(2)}) collective-permute-start(f32[312,128]{1,0:T(8,128)S(1)} %pad_maximum_fusion.a_ref), channel_id=1, source_target_pairs={{0,64},{16,80},{32,96},{48,112},{64,0},{80,16},{96,32},{112,48},{1... | collective-permute-start | bytes 479240 | tf_op jit(solution)/shard_map/ppermute | solution.py:301
  104.4 9.0 %collective-permute-start.6 = (f32[312,128]{1,0:T(8,128)S(1)}, f32[312,128]{1,0:T(8,128)S(1)}, u32[]{:S(2)}, u32[]{:S(2)}) collective-permute-start(f32[312,128]{1,0:T(8,128)S(1)} %pad_maximum_fusion.a_ref), channel_id=1, source_target_pairs={{0,32},{16,48},{32,0},{48,16},{64,96},{80,112},{96,64},{112,80},{1... | collective-permute-start | bytes 479240 | tf_op jit(solution)/shard_map/ppermute | solution.py:301

commit v10 on v9

--- a/solution.py
+++ b/solution.py
@@ -19,8 +19,8 @@
 DEVICES = 128
 SOURCES_PER_STEP = 32
 PACK_ROWS = 80
-TURN_SPLIT = 56
-TURN_ROWS = 112
+TURN_SPLIT = 50
+TURN_ROWS = 104
 
 
 def fold_table(bins):
@@ -32,15 +32,14 @@
     return table
 
 
-def pack_kernel(ref0, ref1, ref2, ref3, out_ref):
-    groups = (ref0, ref1, ref2, ref3)
+def pack_kernel(hist_ref, out_ref):
     lane = lax.broadcasted_iota(i32, (16, LANES), 1)
     for d in range(SOURCES_PER_STEP):
         t0, o = divmod(BLOCK * d, LANES)
         three = o + BLOCK > 2 * LANES
 
         def parts(lo, hi):
-            tiles = [groups[lo // 16][0:hi - lo, (t0 + t) * LANES:(t0 + t + 1) * LANES].astype(f32)
+            tiles = [hist_ref[lo:hi, (t0 + t) * LANES:(t0 + t + 1) * LANES].astype(f32)
                      for t in range(3 if three else 2)]
             upper = lane[:hi - lo] >= o
             a = jnp.where(upper, tiles[0], tiles[1]) if o else tiles[0]
@@ -66,11 +65,11 @@
     return pl.pallas_call(
         pack_kernel,
         grid=(DEVICES // SOURCES_PER_STEP,),
-        in_specs=[pl.BlockSpec((16, width), lambda i, g=g: (g, i)) for g in range(4)],
+        in_specs=[pl.BlockSpec((BINS, width), lambda i: (0, i))],
         out_specs=pl.BlockSpec((SOURCES_PER_STEP, PACK_ROWS, LANES), lambda i: (i, 0, 0)),
         out_shape=jax.ShapeDtypeStruct((DEVICES, PACK_ROWS, LANES), bf16),
         name="pack",
-    )(turn_hist, turn_hist, turn_hist, turn_hist)
+    )(turn_hist)
 
 
 def turn_kernel(hist_ref, label_ref, out_ref):

time: 115 us -> 114 us (level)
  no operation moved by 1% of the time
where the time goes in v10:
time: 114 us
  waiting for transfers between devices  41.2 us (36%)
  Pallas kernels  37.1 us (33%)
  starting transfers between devices  27.2 us (24%)
  other arithmetic  3.91 us (3%)
  local copies, waits for them, and re-layouts  2.72 us (2%)
    all_to_all x1, waiting for transfers between devices, body(): lax.all_to_all(sent, ('board', 'cent'), split_axis=0, concat_axis=0, tile...  20.1 us
    ppermute x9, waiting for transfers between devices, swap(): return lax.ppermute(x, axis, [(i, i ^ mask) for i in range(size)])  18.4 us
    pallas_call x1, Pallas kernels, member(): pl.pallas_call(member_kernel, in_specs=[SMEM, VMEM, VMEM, VMEM, VMEM], ou...  14.9 us
    pallas_call x1, Pallas kernels, turn_partial(): pl.pallas_call(turn_kernel, grid=(steps,), in_specs=[pl.BlockSpec((BINS,...  12.2 us
    all_to_all x1, starting transfers between devices, body(): lax.all_to_all(sent, ('board', 'cent'), split_axis=0, concat_axis=0, tile...  11.2 us
    ppermute x9, starting transfers between devices, swap(): return lax.ppermute(x, axis, [(i, i ^ mask) for i in range(size)])  6.19 us
    all_to_all x1, starting transfers between devices, body(): lax.all_to_all(half, 'cent', split_axis=0, concat_axis=0, tiled=True, axi...  5.59 us
    pallas_call x1, Pallas kernels, nearest_of(): pl.pallas_call(nearest_kernel, in_specs=[VMEM, VMEM, VMEM], out_specs=VME...  4.83 us
  transfers between devices with their start and end apart: 12, of which 8 were waited for; matrix products, arithmetic and copies ran while one was open for 5% of the time, Pallas kernels for 28%

profile of v10, /device:TPU:0, one launch (start us, length us, event | category | flops | bytes accessed | tf_op | source)
XLA Modules:
  0.0 113.7 jit_solution(2711802412080755627)
XLA Ops:
  0.6 4.4 %pack.1 = bf16[128,80,128]{2,1,0:T(8,128)(2,1)} custom-call(bf16[50,24064]{1,0:T(8,128)(2,1)} %hist_ref.3), custom_call_target="tpu_custom_call" | custom-call | tf_op jit(solution)/shard_map/pack/pallas_call | solution.py:65
  5.0 11.2 %all-to-all-start = ((bf16[128,80,128]{2,1,0:T(8,128)(2,1)}), bf16[128,80,128]{2,1,0:T(8,128)(2,1)S(1)}, u32[]{:S(2)}, u32[]{:S(2)}) async-start(bf16[128,80,128]{2,1,0:T(8,128)(2,1)} %pack.1), calls=%async_computation | async-start | bytes 5242880 | tf_op jit(solution)/shard_map/all_to_all | solution.py:327
  17.7 0.7 broadcast_in_dim.14.label_ref
  18.4 12.2 %turn_sums.1 = f32[104,128]{1,0:T(8,128)} custom-call(bf16[50,24064]{1,0:T(8,128)(2,1)} %hist_ref.3, s32[1,24064]{1,0:T(1,128)} %broadcast_in_dim.14.label_ref), custom_call_target="tpu_custom_call" | custom-call | tf_op jit(solution)/shard_map/turn_sums/pallas_call | solution.py:99
  31.2 0.8 select_maximum_fusion
  32.0 20.1 %all-to-all-done.recv_ref = bf16[128,80,128]{2,1,0:T(8,128)(2,1)S(1)} async-done(((bf16[128,80,128]{2,1,0:T(8,128)(2,1)}), bf16[128,80,128]{2,1,0:T(8,128)(2,1)S(1)}, u32[]{:S(2)}, u32[]{:S(2)}) %all-to-all-start) | async-done | bytes 2621472 | tf_op jit(solution)/shard_map/all_to_all | solution.py:327
  52.2 1.1 broadcast_in_dim.35
  53.3 4.3 %all-to-all-start.1 = ((f32[8,304,128]{2,1,0:T(8,128)}), f32[8,304,128]{2,1,0:T(8,128)}, u32[]{:S(2)}, u32[]{:S(2)}) async-start(f32[8,304,128]{2,1,0:T(8,128)} %broadcast_in_dim.35), calls=%async_computation.1 | async-start | bytes 2490368 | tf_op jit(solution)/shard_map/all_to_all | solution.py:340
  57.6 14.9 %member.1 = (f32[200,512]{1,0:T(8,128)S(1)}, f32[8,200,128]{2,1,0:T(8,128)S(1)}, f32[8,200,128]{2,1,0:T(8,128)S(1)}) custom-call(s32[2]{0:T(128)S(1)} %pad_add_fusion.scalar_ref, bf16[128,80,128]{2,1,0:T(8,128)(2,1)S(1)} %all-to-all-done.recv_ref, s32[96,256]{1,0:T(8,128)S(1)} %concatenate.27.place_ref, bf16[264,192]{1,0:T(8,128)(2,1)S(1)} %pad_maximum_fusion.1.table_ref, ...), custom_call_target="tpu_custom_call" | custom-call | tf_op jit(solution)/shard_map/member/pallas_call | solution.py:224
  72.6 2.3 %collective-permute-done = f32[8,200,128]{2,1,0:T(8,128)S(1)} collective-permute-done((f32[8,200,128]{2,1,0:T(8,128)S(1)}, f32[8,200,128]{2,1,0:T(8,128)S(1)}, u32[]{:S(2)}, u32[]{:S(2)}) %collective-permute-start) | collective-permute-done | bytes 819232 | tf_op jit(solution)/shard_map/ppermute | solution.py:300
  74.9 1.0 add.67
  75.9 5.6 %all-to-all-start.2 = ((f32[8,200,128]{2,1,0:T(8,128)}), f32[8,200,128]{2,1,0:T(8,128)S(1)}, u32[]{:S(2)}, u32[]{:S(2)}) async-start(f32[8,200,128]{2,1,0:T(8,128)} %add.67), calls=%async_computation.2 | async-start | bytes 1638400 | tf_op jit(solution)/shard_map/all_to_all | solution.py:350
  81.5 1.0 slice_reduce_fusion
  83.1 0.9 collective-permute-done.4
  84.6 8.3 %collective-permute-done.5 = f32[104,128]{1,0:T(8,128)S(1)} collective-permute-done((f32[104,128]{1,0:T(8,128)S(1)}, f32[104,128]{1,0:T(8,128)S(1)}, u32[]{:S(2)}, u32[]{:S(2)}) %collective-permute-start.5) | collective-permute-done | bytes 53280 | tf_op jit(solution)/shard_map/ppermute | solution.py:300
  92.9 2.7 %all-to-all-done.2 = f32[8,200,128]{2,1,0:T(8,128)S(1)} async-done(((f32[8,200,128]{2,1,0:T(8,128)}), f32[8,200,128]{2,1,0:T(8,128)S(1)}, u32[]{:S(2)}, u32[]{:S(2)}) %all-to-all-start.2) | async-done | bytes 819232 | tf_op jit(solution)/shard_map/all_to_all | solution.py:350
  95.6 0.7 collective-permute-start.3
  96.4 4.8 %nearest.1 = f32[1,1024]{1,0:T(1,128)S(1)} custom-call(f32[200,512]{1,0:T(8,128)S(1)} %get-tuple-element.24.mine_ref, f32[200,512]{1,0:T(8,128)S(1)} %collective-permute-done.1.partner_ref, f32[8,304,128]{2,1,0:T(8,128)} %all-to-all-done.1.pieces_ref), custom_call_target="tpu_custom_call" | custom-call | tf_op jit(solution)/shard_map/nearest/pallas_call | solution.py:260
  101.9 0.7 collective-permute-start.8
  102.6 1.6 %collective-permute-start.7 = (f32[304,128]{1,0:T(8,128)S(1)}, f32[304,128]{1,0:T(8,128)S(1)}, u32[]{:S(2)}, u32[]{:S(2)}) collective-permute-start(f32[304,128]{1,0:T(8,128)S(1)} %pad_maximum_fusion.a_ref), channel_id=1, source_target_pairs={{0,64},{16,80},{32,96},{48,112},{64,0},{80,16},{96,32},{112,48},{1... | collective-permute-start | bytes 466952 | tf_op jit(solution)/shard_map/ppermute | solution.py:300
  104.2 1.9 %collective-permute-start.6 = (f32[304,128]{1,0:T(8,128)S(1)}, f32[304,128]{1,0:T(8,128)S(1)}, u32[]{:S(2)}, u32[]{:S(2)}) collective-permute-start(f32[304,128]{1,0:T(8,128)S(1)} %pad_maximum_fusion.a_ref), channel_id=1, source_target_pairs={{0,32},{16,48},{32,0},{48,16},{64,96},{80,112},{96,64},{112,80},{1... | collective-permute-start | bytes 466952 | tf_op jit(solution)/shard_map/ppermute | solution.py:300
  106.7 5.7 %collective-permute-done.8.d_ref = f32[304,128]{1,0:T(8,128)S(1)} collective-permute-done((f32[304,128]{1,0:T(8,128)S(1)}, f32[304,128]{1,0:T(8,128)S(1)}, u32[]{:S(2)}, u32[]{:S(2)}) %collective-permute-start.8) | collective-permute-done | bytes 155680 | tf_op jit(solution)/shard_map/ppermute | solution.py:300
  112.4 0.6 collective-permute-done.6.b_ref
  113.0 0.7 finish.1
  (55 shorter events, 4.6 us)
Async XLA Ops:
  5.0 11.4 %copy-start.4 = (f32[50,200]{1,0:T(8,128)S(1)}, f32[50,200]{1,0:T(8,128)}, u32[]{:S(2)}) copy-start(f32[50,200]{1,0:T(8,128)} %param.9) | copy-start | bytes 120004
  5.0 11.7 %copy-start.2 = (s32[47,512]{1,0:T(8,128)S(1)}, s32[47,512]{1,0:T(8,128)}, u32[]{:S(2)}) copy-start(s32[47,512]{1,0:T(8,128)} %param.8) | copy-start | bytes 288772
  5.0 12.7 %copy-start.3 = (s32[24064]{0:T(1024)S(1)}, s32[24064]{0:T(1024)}, u32[]{:S(2)}) copy-start(s32[24064]{0:T(1024)} %param.7) | copy-start | bytes 288772
  5.0 47.2 %all-to-all-start = ((bf16[128,80,128]{2,1,0:T(8,128)(2,1)}), bf16[128,80,128]{2,1,0:T(8,128)(2,1)S(1)}, u32[]{:S(2)}, u32[]{:S(2)}) async-start(bf16[128,80,128]{2,1,0:T(8,128)(2,1)} %pack.1), calls=%async_computation | async-start | bytes 5242880 | tf_op jit(solution)/shard_map/all_to_all | solution.py:327
  17.0 14.2 %copy-start.1 = (f32[200,125]{1,0:T(8,128)S(1)}, f32[200,125]{1,0:T(8,128)}, u32[]{:S(2)}) copy-start(f32[200,125]{1,0:T(8,128)} %param.10) | copy-start | bytes 300004
  30.8 26.7 %copy-start = (s32[512]{0:T(512)S(1)}, s32[512]{0:T(512)}, u32[]{:S(2)}) copy-start(s32[512]{0:T(512)} %param.11) | copy-start | bytes 6148
  53.3 22.6 %all-to-all-start.1 = ((f32[8,304,128]{2,1,0:T(8,128)}), f32[8,304,128]{2,1,0:T(8,128)}, u32[]{:S(2)}, u32[]{:S(2)}) async-start(f32[8,304,128]{2,1,0:T(8,128)} %broadcast_in_dim.35), calls=%async_computation.1 | async-start | bytes 2490368 | tf_op jit(solution)/shard_map/all_to_all | solution.py:340
  72.5 2.4 %collective-permute-start = (f32[8,200,128]{2,1,0:T(8,128)S(1)}, f32[8,200,128]{2,1,0:T(8,128)S(1)}, u32[]{:S(2)}, u32[]{:S(2)}) collective-permute-start(f32[8,200,128]{2,1,0:T(8,128)S(1)} %get-tuple-element.23), channel_id=1, source_target_pairs={{0,1},{1,0},{2,3},{3,2},{4,5},{5,4},{6,7},{7,6},{8,9},{9,8},{10,11... | collective-permute-start | bytes 2457608 | tf_op jit(solution)/shard_map/ppermute | solution.py:300
  75.9 19.7 %all-to-all-start.2 = ((f32[8,200,128]{2,1,0:T(8,128)}), f32[8,200,128]{2,1,0:T(8,128)S(1)}, u32[]{:S(2)}, u32[]{:S(2)}) async-start(f32[8,200,128]{2,1,0:T(8,128)} %add.67), calls=%async_computation.2 | async-start | bytes 1638400 | tf_op jit(solution)/shard_map/all_to_all | solution.py:350
  81.5 14.9 %collective-permute-start.1 = (f32[200,512]{1,0:T(8,128)S(1)}, f32[200,512]{1,0:T(8,128)S(1)}, u32[]{:S(2)}, u32[]{:S(2)}) collective-permute-start(f32[200,512]{1,0:T(8,128)S(1)} %get-tuple-element.24.mine_ref), channel_id=1, source_target_pairs={{0,1},{1,0},{2,3},{3,2},{4,5},{5,4},{6,7},{7,6},{8,9},{9,8},{10,11... | collective-permute-start | bytes 1228808 | tf_op jit(solution)/shard_map/ppermute | solution.py:300
  82.5 1.5 %collective-permute-start.4 = (f32[104,128]{1,0:T(8,128)S(1)}, f32[104,128]{1,0:T(8,128)S(1)}, u32[]{:S(2)}, u32[]{:S(2)}) collective-permute-start(f32[104,128]{1,0:T(8,128)S(1)} %slice_reduce_fusion), channel_id=1, source_target_pairs={{0,1},{1,0},{2,3},{3,2},{4,5},{5,4},{6,7},{7,6},{8,9},{9,8},{10,11... | collective-permute-start | bytes 159752 | tf_op jit(solution)/shard_map/ppermute | solution.py:300
  84.0 8.9 %collective-permute-start.5 = (f32[104,128]{1,0:T(8,128)S(1)}, f32[104,128]{1,0:T(8,128)S(1)}, u32[]{:S(2)}, u32[]{:S(2)}) collective-permute-start(f32[104,128]{1,0:T(8,128)S(1)} %add.70), channel_id=1, source_target_pairs={{0,16},{16,0},{32,48},{48,32},{64,80},{80,64},{96,112},{112,96},{1... | collective-permute-start | bytes 159752 | tf_op jit(solution)/shard_map/ppermute | solution.py:300
  95.6 6.2 %collective-permute-start.3 = (f32[200,128]{1,0:T(8,128)S(1)}, f32[200,128]{1,0:T(8,128)S(1)}, u32[]{:S(2)}, u32[]{:S(2)}) collective-permute-start(f32[200,128]{1,0:T(8,128)S(1)} %reduce_sum.48), channel_id=1, source_target_pairs={{0,16},{16,0},{32,48},{48,32},{64,80},{80,64},{96,112},{112,96},{1... | collective-permute-start | bytes 307208 | tf_op jit(solution)/shard_map/ppermute | solution.py:300
  101.2 4.9 %collective-permute-start.2 = (f32[1,512]{1,0:T(1,128)S(1)}, f32[1,512]{1,0:T(1,128)S(1)}, u32[]{:S(2)}, u32[]{:S(2)}) collective-permute-start(f32[1,512]{1,0:T(1,128)S(1)} %slice.49), channel_id=1, source_target_pairs={{0,1},{1,0},{2,3},{3,2},{4,5},{5,4},{6,7},{7,6},{8,9},{9,8},{10,11... | collective-permute-start | bytes 6152 | tf_op jit(solution)/shard_map/ppermute | solution.py:300
  101.9 10.5 %collective-permute-start.8 = (f32[304,128]{1,0:T(8,128)S(1)}, f32[304,128]{1,0:T(8,128)S(1)}, u32[]{:S(2)}, u32[]{:S(2)}) collective-permute-start(f32[304,128]{1,0:T(8,128)S(1)} %pad_maximum_fusion.a_ref), channel_id=1, source_target_pairs={{0,96},{16,112},{32,64},{48,80},{64,32},{80,48},{96,0},{112,16},{1... | collective-permute-start | bytes 466952 | tf_op jit(solution)/shard_map/ppermute | solution.py:300
  102.6 9.8 %collective-permute-start.7 = (f32[304,128]{1,0:T(8,128)S(1)}, f32[304,128]{1,0:T(8,128)S(1)}, u32[]{:S(2)}, u32[]{:S(2)}) collective-permute-start(f32[304,128]{1,0:T(8,128)S(1)} %pad_maximum_fusion.a_ref), channel_id=1, source_target_pairs={{0,64},{16,80},{32,96},{48,112},{64,0},{80,16},{96,32},{112,48},{1... | collective-permute-start | bytes 466952 | tf_op jit(solution)/shard_map/ppermute | solution.py:300
  104.2 8.8 %collective-permute-start.6 = (f32[304,128]{1,0:T(8,128)S(1)}, f32[304,128]{1,0:T(8,128)S(1)}, u32[]{:S(2)}, u32[]{:S(2)}) collective-permute-start(f32[304,128]{1,0:T(8,128)S(1)} %pad_maximum_fusion.a_ref), channel_id=1, source_target_pairs={{0,32},{16,48},{32,0},{48,16},{64,96},{80,112},{96,64},{112,80},{1... | collective-permute-start | bytes 466952 | tf_op jit(solution)/shard_map/ppermute | solution.py:300

commit v11 on v10

--- a/solution.py
+++ b/solution.py
@@ -240,13 +240,14 @@
     )(scalars, recv, place, table, assign)
 
 
-def nearest_kernel(mine_ref, partner_ref, pieces_ref, out_ref):
+def nearest_kernel(mine_ref, partner_ref, *refs):
+    pieces, out_ref = refs[:-1], refs[-1]
     one = jnp.where(lax.broadcasted_iota(i32, (8, 2 * HANDS), 0) == 0, 1.0, 0.0)
     hands = jnp.concatenate([jnp.concatenate([mine_ref[...], partner_ref[...]], axis=1), one], axis=0)
     lane = lax.broadcasted_iota(i32, (8, LANES), 1)
     best = None
-    for i in range(pieces_ref.shape[0]):
-        c = pieces_ref[i, 0:TURN_CENT, :]
+    for ref in pieces:
+        c = ref[0:TURN_CENT, :]
         sq = jnp.broadcast_to(jnp.sum(c * c, axis=0, keepdims=True), (8, LANES))
         sides = jnp.concatenate([-2.0 * c, jnp.where(lane < PANEL, sq, 1e30)], axis=0)
         dist = lax.dot_general(
@@ -259,12 +260,12 @@
 def nearest_of(pieces, flop_hist, partner):
     best = pl.pallas_call(
         nearest_kernel,
-        in_specs=[VMEM, VMEM, VMEM],
+        in_specs=[VMEM] * (2 + len(pieces)),
         out_specs=VMEM,
         out_shape=jax.ShapeDtypeStruct((1, 2 * HANDS), f32),
     compiler_params=pltpu.CompilerParams(vmem_limit_bytes=24 * 1024 * 1024),
         name="nearest",
-    )(flop_hist, partner, pieces)
+    )(flop_hist, partner, *pieces)
     best = jnp.minimum(best[:, :HANDS], swap(best[:, HANDS:], "cent", 1))
     return best[0] + jnp.sum(jnp.square(flop_hist), axis=0)
 
@@ -332,16 +333,16 @@
 
     turn_part = turn_partial(turn_hist, turn_assign[None, :])
     own = jnp.concatenate([jnp.pad(flop_centers, ((0, 0), (0, LANES - PANEL))), turn_part], axis=0)
+    pieces = [own]
+    for mask in range(2, 16, 2):
+        pieces.append(swap(own, "cent", mask))
     place = jnp.concatenate([child_rows.reshape(TILES, TILE), jnp.zeros((2, TILE), i32)], axis=0)
     table = center_table(turn_centers)
 
-    own, place, table, scalars = lax.optimization_barrier((own, place, table, scalars))
-    copies = jnp.broadcast_to(own[None], (8,) + own.shape)
-    pieces = lax.all_to_all(copies, "cent", split_axis=0, concat_axis=0, tiled=True, axis_index_groups=CHIPS)
-
+    place, table, scalars = lax.optimization_barrier((place, table, scalars))
     flop_hist, keep, send = member(scalars, arrived, place, table, flop_assign[None, :])
 
-    turn_part = jnp.sum(pieces[:, TURN_CENT:], axis=0)
+    turn_part = sum((piece[TURN_CENT:] for piece in pieces[1:]), turn_part)
     turn_part = turn_part + swap(turn_part, "cent", 1)
     turn_part = turn_part + swap(turn_part, "board", 1)
     half = keep + swap(send, "cent", 1)

time: 114 us -> 144 us (1.26)
  waiting for transfers between devices: 41.2 us -> 69.3 us
  starting transfers between devices: 27.2 us -> 31.5 us
  other arithmetic: 3.91 us -> 2.09 us
    ppermute x9 -> x16, waiting for transfers between devices: 18.4 us -> 35.4 us  [swap(): return lax.ppermute(x, axis, [(i, i ^ mask) for i in range(size)])]
    all_to_all x1, waiting for transfers between devices: 20.1 us -> 33.9 us  [body(): lax.all_to_all(sent, ('board', 'cent'), split_axis=0, concat_axis=0, tile...]
    ppermute x9 -> x16, starting transfers between devices: 6.19 us -> 16.7 us  [swap(): return lax.ppermute(x, axis, [(i, i ^ mask) for i in range(size)])]
    all_to_all x1 -> x0, starting transfers between devices: 4.26 us -> none  [body(): lax.all_to_all(copies, 'cent', split_axis=0, concat_axis=0, tiled=True, a...]
    all_to_all x1, waiting for transfers between devices: 2.65 us -> 0.01 us  [body(): lax.all_to_all(half, 'cent', split_axis=0, concat_axis=0, tiled=True, axi...]
    all_to_all x1, starting transfers between devices: 5.59 us -> 3.55 us  [body(): lax.all_to_all(half, 'cent', split_axis=0, concat_axis=0, tiled=True, axi...]
  transfers between devices with their start and end apart: 12 -> 18, of which waited for: 8 -> 10; matrix products, arithmetic and copies ran while one was open for 5% -> 2% of each run, Pallas kernels for 28% -> 11%
where the time goes in v11:
time: 144 us
  waiting for transfers between devices  69.3 us (48%)
  Pallas kernels  37 us (26%)
  starting transfers between devices  31.5 us (22%)
  local copies, waits for them, and re-layouts  2.57 us (2%)
  other arithmetic  2.09 us (1%)
    ppermute x16, waiting for transfers between devices, swap(): return lax.ppermute(x, axis, [(i, i ^ mask) for i in range(size)])  35.4 us
    all_to_all x1, waiting for transfers between devices, body(): lax.all_to_all(sent, ('board', 'cent'), split_axis=0, concat_axis=0, tile...  33.9 us
    ppermute x16, starting transfers between devices, swap(): return lax.ppermute(x, axis, [(i, i ^ mask) for i in range(size)])  16.7 us
    pallas_call x1, Pallas kernels, member(): pl.pallas_call(member_kernel, in_specs=[SMEM, VMEM, VMEM, VMEM, VMEM], ou...  16.1 us
    pallas_call x1, Pallas kernels, turn_partial(): pl.pallas_call(turn_kernel, grid=(steps,), in_specs=[pl.BlockSpec((BINS,...  12.2 us
    all_to_all x1, starting transfers between devices, body(): lax.all_to_all(sent, ('board', 'cent'), split_axis=0, concat_axis=0, tile...  11.2 us
    pallas_call x1, Pallas kernels, pack(): pl.pallas_call(pack_kernel, grid=(DEVICES // SOURCES_PER_STEP,), in_specs...  4.39 us
    pallas_call x1, Pallas kernels, nearest_of(): pl.pallas_call(nearest_kernel, in_specs=[VMEM] * (2 + len(pieces)), out_s...  3.57 us
  transfers between devices with their start and end apart: 18, of which 10 were waited for; matrix products, arithmetic and copies ran while one was open for 2% of the time, Pallas kernels for 11%

profile of v11, /device:TPU:0, one launch (start us, length us, event | category | flops | bytes accessed | tf_op | source)
XLA Modules:
  0.0 144.0 jit_solution(8536682056484851912)
XLA Ops:
  0.6 4.4 %pack.1 = bf16[128,80,128]{2,1,0:T(8,128)(2,1)} custom-call(bf16[50,24064]{1,0:T(8,128)(2,1)} %hist_ref.3), custom_call_target="tpu_custom_call" | custom-call | tf_op jit(solution)/shard_map/pack/pallas_call | solution.py:65
  5.0 11.2 %all-to-all-start = ((bf16[128,80,128]{2,1,0:T(8,128)(2,1)}), bf16[128,80,128]{2,1,0:T(8,128)(2,1)S(1)}, u32[]{:S(2)}, u32[]{:S(2)}) async-start(bf16[128,80,128]{2,1,0:T(8,128)(2,1)} %pack.1), calls=%async_computation | async-start | bytes 5242880 | tf_op jit(solution)/shard_map/all_to_all | solution.py:328
  18.3 33.9 %all-to-all-done.recv_ref = bf16[128,80,128]{2,1,0:T(8,128)(2,1)S(1)} async-done(((bf16[128,80,128]{2,1,0:T(8,128)(2,1)}), bf16[128,80,128]{2,1,0:T(8,128)(2,1)S(1)}, u32[]{:S(2)}, u32[]{:S(2)}) %all-to-all-start) | async-done | bytes 2621472 | tf_op jit(solution)/shard_map/all_to_all | solution.py:328
  52.2 16.1 %member.1 = (f32[200,512]{1,0:T(8,128)S(1)}, f32[8,200,128]{2,1,0:T(8,128)S(1)}, f32[8,200,128]{2,1,0:T(8,128)}) custom-call(s32[2]{0:T(128)S(1)} %pad_add_fusion.scalar_ref, bf16[128,80,128]{2,1,0:T(8,128)(2,1)S(1)} %all-to-all-done.recv_ref, s32[96,256]{1,0:T(8,128)S(1)} %concatenate.26.place_ref, bf16[264,192]{1,0:T(8,128)(2,1)S(1)} %pad_maximum_fusion.1.table_ref, ...), custom_call_target="tpu_custom_call" | custom-call | tf_op jit(solution)/shard_map/member/pallas_call | solution.py:224
  68.3 1.0 copy-done
  70.0 12.2 %turn_sums.1 = f32[104,128]{1,0:T(8,128)} custom-call(bf16[50,24064]{1,0:T(8,128)(2,1)} %hist_ref.3, s32[1,24064]{1,0:T(1,128)} %broadcast_in_dim.28.label_ref), custom_call_target="tpu_custom_call" | custom-call | tf_op jit(solution)/shard_map/turn_sums/pallas_call | solution.py:99
  82.2 1.0 add.88
  83.2 3.5 %all-to-all-start.1 = ((f32[8,200,128]{2,1,0:T(8,128)}), f32[8,200,128]{2,1,0:T(8,128)S(1)}, u32[]{:S(2)}, u32[]{:S(2)}) async-start(f32[8,200,128]{2,1,0:T(8,128)} %add.88), calls=%async_computation.1 | async-start | bytes 1638400 | tf_op jit(solution)/shard_map/all_to_all | solution.py:351
  86.8 4.1 %collective-permute-start.8 = (f32[304,128]{1,0:T(8,128)S(1)}, f32[304,128]{1,0:T(8,128)S(1)}, u32[]{:S(2)}, u32[]{:S(2)}) collective-permute-start(f32[304,128]{1,0:T(8,128)S(1)} %select_maximum_fusion.refs_0_), channel_id=1, source_target_pairs={{0,14},{1,15},{2,12},{3,13},{4,10},{5,11},{6,8},{7,9},{8,6},{9,7},... | collective-permute-start | bytes 466952 | tf_op jit(solution)/shard_map/ppermute | solution.py:301
  91.5 1.8 %collective-permute-start.6 = (f32[304,128]{1,0:T(8,128)S(1)}, f32[304,128]{1,0:T(8,128)S(1)}, u32[]{:S(2)}, u32[]{:S(2)}) collective-permute-start(f32[304,128]{1,0:T(8,128)S(1)} %select_maximum_fusion.refs_0_), channel_id=1, source_target_pairs={{0,10},{1,11},{2,8},{3,9},{4,14},{5,15},{6,12},{7,13},{8,2},{9,3},... | collective-permute-start | bytes 466952 | tf_op jit(solution)/shard_map/ppermute | solution.py:301
  93.3 1.3 collective-permute-start.5
  94.6 1.6 %collective-permute-start.4 = (f32[304,128]{1,0:T(8,128)S(1)}, f32[304,128]{1,0:T(8,128)S(1)}, u32[]{:S(2)}, u32[]{:S(2)}) collective-permute-start(f32[304,128]{1,0:T(8,128)S(1)} %select_maximum_fusion.refs_0_), channel_id=1, source_target_pairs={{0,6},{1,7},{2,4},{3,5},{4,2},{5,3},{6,0},{7,1},{8,14},{9,15},{10,... | collective-permute-start | bytes 466952 | tf_op jit(solution)/shard_map/ppermute | solution.py:301
  96.2 11.3 %collective-permute-done.8.refs_7_ = f32[304,128]{1,0:T(8,128)S(1)} collective-permute-done((f32[304,128]{1,0:T(8,128)S(1)}, f32[304,128]{1,0:T(8,128)S(1)}, u32[]{:S(2)}, u32[]{:S(2)}) %collective-permute-start.8) | collective-permute-done | bytes 155680 | tf_op jit(solution)/shard_map/ppermute | solution.py:301
  107.7 6.0 %collective-permute-done.7.refs_6_ = f32[304,128]{1,0:T(8,128)S(1)} collective-permute-done((f32[304,128]{1,0:T(8,128)S(1)}, f32[304,128]{1,0:T(8,128)S(1)}, u32[]{:S(2)}, u32[]{:S(2)}) %collective-permute-start.7) | collective-permute-done | bytes 155680 | tf_op jit(solution)/shard_map/ppermute | solution.py:301
  114.4 1.1 collective-permute-done.3.refs_2_
  115.5 4.1 %collective-permute-done.2.refs_1_ = f32[304,128]{1,0:T(8,128)S(1)} collective-permute-done((f32[304,128]{1,0:T(8,128)S(1)}, f32[304,128]{1,0:T(8,128)S(1)}, u32[]{:S(2)}, u32[]{:S(2)}) %collective-permute-start.2) | collective-permute-done | bytes 155680 | tf_op jit(solution)/shard_map/ppermute | solution.py:301
  119.7 1.2 collective-permute-done.11
  120.9 1.0 collective-permute-start.12
  121.9 4.7 %collective-permute-done.12 = f32[104,128]{1,0:T(8,128)S(1)} collective-permute-done((f32[104,128]{1,0:T(8,128)S(1)}, f32[104,128]{1,0:T(8,128)S(1)}, u32[]{:S(2)}, u32[]{:S(2)}) %collective-permute-start.12) | collective-permute-done | bytes 53280 | tf_op jit(solution)/shard_map/ppermute | solution.py:301
  126.7 1.2 collective-permute-start.10
  128.0 3.6 %nearest.1 = f32[1,1024]{1,0:T(1,128)S(1)} custom-call(f32[200,512]{1,0:T(8,128)S(1)} %get-tuple-element.22.mine_ref, f32[200,512]{1,0:T(8,128)S(1)} %collective-permute-done.1.partner_ref, f32[304,128]{1,0:T(8,128)S(1)} %select_maximum_fusion.refs_0_, f32[304,128]{1,0:T(8,128)S(1)} %collective-permute-done.2.refs_1_, ...), custom_call_target="tpu_custom_call" | custom-call | tf_op jit(solution)/shard_map/nearest/pallas_call | solution.py:261
  131.6 1.5 %collective-permute-done.10 = f32[200,128]{1,0:T(8,128)S(1)} collective-permute-done((f32[200,128]{1,0:T(8,128)S(1)}, f32[200,128]{1,0:T(8,128)S(1)}, u32[]{:S(2)}, u32[]{:S(2)}) %collective-permute-start.10) | collective-permute-done | bytes 102432 | tf_op jit(solution)/shard_map/ppermute | solution.py:301
  134.5 2.8 %collective-permute-start.13 = (f32[304,128]{1,0:T(8,128)S(1)}, f32[304,128]{1,0:T(8,128)S(1)}, u32[]{:S(2)}, u32[]{:S(2)}) collective-permute-start(f32[304,128]{1,0:T(8,128)S(1)} %pad_maximum_fusion.a_ref), channel_id=1, source_target_pairs={{0,32},{16,48},{32,0},{48,16},{64,96},{80,112},{96,64},{112,80},{1... | collective-permute-start | bytes 466952 | tf_op jit(solution)/shard_map/ppermute | solution.py:301
  138.0 4.8 %collective-permute-done.15.d_ref = f32[304,128]{1,0:T(8,128)S(1)} collective-permute-done((f32[304,128]{1,0:T(8,128)S(1)}, f32[304,128]{1,0:T(8,128)S(1)}, u32[]{:S(2)}, u32[]{:S(2)}) %collective-permute-start.15) | collective-permute-done | bytes 155680 | tf_op jit(solution)/shard_map/ppermute | solution.py:301
  (72 shorter events, 7.7 us)
Async XLA Ops:
  5.0 11.4 %copy-start.7 = (f32[50,200]{1,0:T(8,128)S(1)}, f32[50,200]{1,0:T(8,128)}, u32[]{:S(2)}) copy-start(f32[50,200]{1,0:T(8,128)} %param.9) | copy-start | bytes 120004
  5.0 11.7 %copy-start.5 = (s32[47,512]{1,0:T(8,128)S(1)}, s32[47,512]{1,0:T(8,128)}, u32[]{:S(2)}) copy-start(s32[47,512]{1,0:T(8,128)} %param.8) | copy-start | bytes 288772
  5.0 47.2 %all-to-all-start = ((bf16[128,80,128]{2,1,0:T(8,128)(2,1)}), bf16[128,80,128]{2,1,0:T(8,128)(2,1)S(1)}, u32[]{:S(2)}, u32[]{:S(2)}) async-start(bf16[128,80,128]{2,1,0:T(8,128)(2,1)} %pack.1), calls=%async_computation | async-start | bytes 5242880 | tf_op jit(solution)/shard_map/all_to_all | solution.py:328
  16.2 36.0 %copy-start.2 = (s32[512]{0:T(512)S(1)}, s32[512]{0:T(512)}, u32[]{:S(2)}) copy-start(s32[512]{0:T(512)} %param.11) | copy-start | bytes 6148
  16.7 52.5 %copy-start.6 = (s32[24064]{0:T(1024)S(1)}, s32[24064]{0:T(1024)}, u32[]{:S(2)}) copy-start(s32[24064]{0:T(1024)} %param.7) | copy-start | bytes 288772
  69.3 13.0 %copy-start.1 = (f32[8,200,128]{2,1,0:T(8,128)S(1)}, f32[8,200,128]{2,1,0:T(8,128)}, u32[]{:S(2)}) copy-start(f32[8,200,128]{2,1,0:T(8,128)} %copy-done) | copy-start | bytes 2457604
  69.3 13.0 %collective-permute-start = (f32[8,200,128]{2,1,0:T(8,128)}, f32[8,200,128]{2,1,0:T(8,128)S(1)}, u32[]{:S(2)}, u32[]{:S(2)}) collective-permute-start(f32[8,200,128]{2,1,0:T(8,128)} %get-tuple-element.21), channel_id=1, source_target_pairs={{0,1},{1,0},{2,3},{3,2},{4,5},{5,4},{6,7},{7,6},{8,9},{9,8},{10,11... | collective-permute-start | bytes 2457608 | tf_op jit(solution)/shard_map/ppermute | solution.py:301
  82.2 4.6 %copy-start.4 = (f32[200,125]{1,0:T(8,128)S(1)}, f32[200,125]{1,0:T(8,128)}, u32[]{:S(2)}) copy-start(f32[200,125]{1,0:T(8,128)} %param.10) | copy-start | bytes 300004
  83.2 43.4 %all-to-all-start.1 = ((f32[8,200,128]{2,1,0:T(8,128)}), f32[8,200,128]{2,1,0:T(8,128)S(1)}, u32[]{:S(2)}, u32[]{:S(2)}) async-start(f32[8,200,128]{2,1,0:T(8,128)} %add.88), calls=%async_computation.1 | async-start | bytes 1638400 | tf_op jit(solution)/shard_map/all_to_all | solution.py:351
  86.8 20.7 %collective-permute-start.8 = (f32[304,128]{1,0:T(8,128)S(1)}, f32[304,128]{1,0:T(8,128)S(1)}, u32[]{:S(2)}, u32[]{:S(2)}) collective-permute-start(f32[304,128]{1,0:T(8,128)S(1)} %select_maximum_fusion.refs_0_), channel_id=1, source_target_pairs={{0,14},{1,15},{2,12},{3,13},{4,10},{5,11},{6,8},{7,9},{8,6},{9,7},... | collective-permute-start | bytes 466952 | tf_op jit(solution)/shard_map/ppermute | solution.py:301
  91.0 22.7 %collective-permute-start.7 = (f32[304,128]{1,0:T(8,128)S(1)}, f32[304,128]{1,0:T(8,128)S(1)}, u32[]{:S(2)}, u32[]{:S(2)}) collective-permute-start(f32[304,128]{1,0:T(8,128)S(1)} %select_maximum_fusion.refs_0_), channel_id=1, source_target_pairs={{0,12},{1,13},{2,14},{3,15},{4,8},{5,9},{6,10},{7,11},{8,4},{9,5},... | collective-permute-start | bytes 466952 | tf_op jit(solution)/shard_map/ppermute | solution.py:301
  91.5 22.9 %collective-permute-start.6 = (f32[304,128]{1,0:T(8,128)S(1)}, f32[304,128]{1,0:T(8,128)S(1)}, u32[]{:S(2)}, u32[]{:S(2)}) collective-permute-start(f32[304,128]{1,0:T(8,128)S(1)} %select_maximum_fusion.refs_0_), channel_id=1, source_target_pairs={{0,10},{1,11},{2,8},{3,9},{4,14},{5,15},{6,12},{7,13},{8,2},{9,3},... | collective-permute-start | bytes 466952 | tf_op jit(solution)/shard_map/ppermute | solution.py:301
  93.3 21.1 %collective-permute-start.5 = (f32[304,128]{1,0:T(8,128)S(1)}, f32[304,128]{1,0:T(8,128)S(1)}, u32[]{:S(2)}, u32[]{:S(2)}) collective-permute-start(f32[304,128]{1,0:T(8,128)S(1)} %select_maximum_fusion.refs_0_), channel_id=1, source_target_pairs={{0,8},{1,9},{2,10},{3,11},{4,12},{5,13},{6,14},{7,15},{8,0},{9,1},... | collective-permute-start | bytes 466952 | tf_op jit(solution)/shard_map/ppermute | solution.py:301
  94.6 19.8 %collective-permute-start.4 = (f32[304,128]{1,0:T(8,128)S(1)}, f32[304,128]{1,0:T(8,128)S(1)}, u32[]{:S(2)}, u32[]{:S(2)}) collective-permute-start(f32[304,128]{1,0:T(8,128)S(1)} %select_maximum_fusion.refs_0_), channel_id=1, source_target_pairs={{0,6},{1,7},{2,4},{3,5},{4,2},{5,3},{6,0},{7,1},{8,14},{9,15},{10,... | collective-permute-start | bytes 466952 | tf_op jit(solution)/shard_map/ppermute | solution.py:301
  107.5 8.0 %collective-permute-start.3 = (f32[304,128]{1,0:T(8,128)S(1)}, f32[304,128]{1,0:T(8,128)S(1)}, u32[]{:S(2)}, u32[]{:S(2)}) collective-permute-start(f32[304,128]{1,0:T(8,128)S(1)} %select_maximum_fusion.refs_0_), channel_id=1, source_target_pairs={{0,4},{1,5},{2,6},{3,7},{4,0},{5,1},{6,2},{7,3},{8,12},{9,13},{10,... | collective-permute-start | bytes 466952 | tf_op jit(solution)/shard_map/ppermute | solution.py:301
  113.6 5.9 %collective-permute-start.2 = (f32[304,128]{1,0:T(8,128)S(1)}, f32[304,128]{1,0:T(8,128)S(1)}, u32[]{:S(2)}, u32[]{:S(2)}) collective-permute-start(f32[304,128]{1,0:T(8,128)S(1)} %select_maximum_fusion.refs_0_), channel_id=1, source_target_pairs={{0,2},{1,3},{2,0},{3,1},{4,6},{5,7},{6,4},{7,5},{8,10},{9,11},{10,... | collective-permute-start | bytes 466952 | tf_op jit(solution)/shard_map/ppermute | solution.py:301
  114.3 13.6 %collective-permute-start.1 = (f32[200,512]{1,0:T(8,128)S(1)}, f32[200,512]{1,0:T(8,128)S(1)}, u32[]{:S(2)}, u32[]{:S(2)}) collective-permute-start(f32[200,512]{1,0:T(8,128)S(1)} %get-tuple-element.22.mine_ref), channel_id=1, source_target_pairs={{0,1},{1,0},{2,3},{3,2},{4,5},{5,4},{6,7},{7,6},{8,9},{9,8},{10,11... | collective-permute-start | bytes 1228808 | tf_op jit(solution)/shard_map/ppermute | solution.py:301
  119.6 1.3 collective-permute-start.11
  120.9 5.7 %collective-permute-start.12 = (f32[104,128]{1,0:T(8,128)S(1)}, f32[104,128]{1,0:T(8,128)S(1)}, u32[]{:S(2)}, u32[]{:S(2)}) collective-permute-start(f32[104,128]{1,0:T(8,128)S(1)} %add.98), channel_id=1, source_target_pairs={{0,16},{16,0},{32,48},{48,32},{64,80},{80,64},{96,112},{112,96},{1... | collective-permute-start | bytes 159752 | tf_op jit(solution)/shard_map/ppermute | solution.py:301
  126.7 6.4 %collective-permute-start.10 = (f32[200,128]{1,0:T(8,128)S(1)}, f32[200,128]{1,0:T(8,128)S(1)}, u32[]{:S(2)}, u32[]{:S(2)}) collective-permute-start(f32[200,128]{1,0:T(8,128)S(1)} %reduce_sum.39), channel_id=1, source_target_pairs={{0,16},{16,0},{32,48},{48,32},{64,80},{80,64},{96,112},{112,96},{1... | collective-permute-start | bytes 307208 | tf_op jit(solution)/shard_map/ppermute | solution.py:301
  131.5 5.8 %collective-permute-start.9 = (f32[1,512]{1,0:T(1,128)S(1)}, f32[1,512]{1,0:T(1,128)S(1)}, u32[]{:S(2)}, u32[]{:S(2)}) collective-permute-start(f32[1,512]{1,0:T(1,128)S(1)} %slice.73), channel_id=1, source_target_pairs={{0,1},{1,0},{2,3},{3,2},{4,5},{5,4},{6,7},{7,6},{8,9},{9,8},{10,11... | collective-permute-start | bytes 6152 | tf_op jit(solution)/shard_map/ppermute | solution.py:301
  133.2 9.5 %collective-permute-start.15 = (f32[304,128]{1,0:T(8,128)S(1)}, f32[304,128]{1,0:T(8,128)S(1)}, u32[]{:S(2)}, u32[]{:S(2)}) collective-permute-start(f32[304,128]{1,0:T(8,128)S(1)} %pad_maximum_fusion.a_ref), channel_id=1, source_target_pairs={{0,96},{16,112},{32,64},{48,80},{64,32},{80,48},{96,0},{112,16},{1... | collective-permute-start | bytes 466952 | tf_op jit(solution)/shard_map/ppermute | solution.py:301
  133.9 8.9 %collective-permute-start.14 = (f32[304,128]{1,0:T(8,128)S(1)}, f32[304,128]{1,0:T(8,128)S(1)}, u32[]{:S(2)}, u32[]{:S(2)}) collective-permute-start(f32[304,128]{1,0:T(8,128)S(1)} %pad_maximum_fusion.a_ref), channel_id=1, source_target_pairs={{0,64},{16,80},{32,96},{48,112},{64,0},{80,16},{96,32},{112,48},{1... | collective-permute-start | bytes 466952 | tf_op jit(solution)/shard_map/ppermute | solution.py:301
  134.5 8.8 %collective-permute-start.13 = (f32[304,128]{1,0:T(8,128)S(1)}, f32[304,128]{1,0:T(8,128)S(1)}, u32[]{:S(2)}, u32[]{:S(2)}) collective-permute-start(f32[304,128]{1,0:T(8,128)S(1)} %pad_maximum_fusion.a_ref), channel_id=1, source_target_pairs={{0,32},{16,48},{32,0},{48,16},{64,96},{80,112},{96,64},{112,80},{1... | collective-permute-start | bytes 466952 | tf_op jit(solution)/shard_map/ppermute | solution.py:301
  (2 other events, 5.5 us)
